TPU v7x, 32 devices: a whole 2x2x4 slice. The times are simulated.
32 devices in a mesh: rows: 8 (over z, x), chan: 4 (over y, core).
Axes of the slice: x: 2, y: 2, z: 4, core: 2. Of those that a mesh axis runs over, the one named last changes fastest.
Arguments:
- tokens: bfloat16 [8192, 1024], P(('rows', 'chan')), may hold values from -6 to 6
- cotangent: bfloat16 [8192, 1024], P(('rows', 'chan')), may hold values from -6 to 6
- segments: int32 [8, 1024], P('rows'), may hold values from 0 to 3, never falling along the last dimension, each value on 1 to 512 neighbouring positions
- w_query: bfloat16 [1024, 1024], P(None, 'chan'), may hold values from -0.25 to 0.25
- w_key: bfloat16 [1024, 1024], P(None, 'chan'), may hold values from -0.1875 to 0.1875
- w_value: bfloat16 [1024, 1024], P(None, 'chan'), may hold values from -0.1875 to 0.1875
- w_out: bfloat16 [1024, 1024], P(None, 'chan'), may hold values from -0.75 to 0.75
- w_up: bfloat16 [1024, 4096], P(None, 'chan'), may hold values from -0.1875 to 0.1875
- up_bias: float32 [4096], P('chan'), may hold values from -3 to 3
- w_down: bfloat16 [1024, 4096], P(None, 'chan'), may hold values from -0.09375 to 0.09375
- down_bias: float32 [1024], replicated, may hold values from -3 to 3
- norm1_gain: float32 [1024], replicated, may hold values from 0.5 to 1.5
- norm1_bias: float32 [1024], replicated, may hold values from -2 to 2
- norm2_gain: float32 [1024], replicated, may hold values from 0.5 to 1.5
- norm2_bias: float32 [1024], replicated, may hold values from -2 to 2
- decay_rates: float32 [1024, 16], P('chan'), may hold values from 0.00048828125 to 0.03125
- input_mix: float32 [1024, 16], P('chan'), may hold values from -4 to 4
- key_mix: float32 [1024, 16], P('chan'), may hold values from -1.5 to 1.5
- value_mix: float32 [1024, 16], P('chan'), may hold values from -1.5 to 1.5
- key_skip: float32 [1024], P('chan'), may hold values from -3 to 3
- value_skip: float32 [1024], P('chan'), may hold values from -3 to 3
Outputs:
- output: bfloat16 [8192, 1024], P(('rows', 'chan'))
- grad_tokens: bfloat16 [8192, 1024], P(('rows', 'chan'))
- grad_w_query: float32 [1024, 1024], P('rows', 'chan')
- grad_w_key: float32 [1024, 1024], P('rows', 'chan')
- grad_w_value: float32 [1024, 1024], P('rows', 'chan')
- grad_w_out: float32 [1024, 1024], P('rows', 'chan')
- grad_w_up: float32 [1024, 4096], P('rows', 'chan')
- grad_up_bias: float32 [4096], replicated
- grad_w_down: float32 [1024, 4096], P('rows', 'chan')
- grad_down_bias: float32 [1024], replicated
- grad_norm1_gain: float32 [1024], replicated
- grad_norm1_bias: float32 [1024], replicated
- grad_norm2_gain: float32 [1024], replicated
- grad_norm2_bias: float32 [1024], replicated
- grad_decay_rates: float32 [1024, 16], replicated
- grad_input_mix: float32 [1024, 16], replicated
- grad_key_mix: float32 [1024, 16], replicated
- grad_value_mix: float32 [1024, 16], replicated
- grad_key_skip: float32 [1024], replicated
- grad_value_skip: float32 [1024], replicated
Inputs may be any that keep to these rules, and one draw needn't show every extreme that they name: `segments`: along a row segment ids never fall; each segment spans 1 to 512 tokens, one exactly that many.
All inputs are finite; a program needn't handle non-finite values.
Results may differ from a plain program's by a relative error of at most 0.014.
The roundings to bfloat16 on the way count: a program that leaves them out, or rounds other values in their place, can miss the bound.
Values may be sent and summed in bfloat16 or wider, within the bound.
A program may use at most 128 MiB of HBM per device.

v0:
```python
import jax
import jax.numpy as jnp
from jax import lax
from jax.sharding import PartitionSpec as P

D = 1024
HEADS = 8
FF = 4096
CTX = 128
BLK = 512
SQ = 256
LEN = 1024


def layer_norm(values, gain, bias):
    centered = values - jnp.mean(values, axis=-1, keepdims=True)
    variance = jnp.mean(centered * centered, axis=-1, keepdims=True)
    return centered * lax.rsqrt(variance + 1e-05) * gain + bias


def segment_starts(segment_rows):
    row_count, length_all = segment_rows.shape
    previous = jnp.concatenate([segment_rows[:, :1], segment_rows[:, :-1]], axis=1)
    row_first = (jnp.arange(length_all, dtype=jnp.int32) == 0)[None, :]
    return (
        jnp.where(row_first | (segment_rows != previous), 1, 0)
        .astype(jnp.int32)
        .reshape(row_count * length_all)
    )


def ssm_block(previous, block_in, mixers):
    decay_rates, input_mix, key_mix, value_mix, key_skip, value_skip = mixers
    inputs, starts = block_in
    positions = jnp.arange(inputs.shape[0], dtype=jnp.int32)
    last_start = lax.cummax(jnp.where(starts > 0, positions, -1), axis=0)
    offsets = positions.astype(jnp.float32)[:, None, None]
    growth = jnp.exp(offsets * decay_rates)
    input_scale = jnp.sqrt(-jnp.expm1(-2.0 * decay_rates)) * input_mix
    summands = growth * input_scale * inputs[:, :, None]
    running = jnp.cumsum(summands, axis=0)
    before = jnp.take(running, jnp.maximum(last_start - 1, 0), axis=0)
    before = jnp.where((last_start >= 1)[:, None, None], before, 0.0)
    carried = jnp.where(
        (last_start < 0)[:, None, None],
        jnp.exp(-(offsets + 1.0) * decay_rates) * previous[None],
        0.0,
    )
    states = jnp.exp(-offsets * decay_rates) * (running - before) + carried
    ctx_keys = jnp.sum(states * key_mix, axis=2) + key_skip * inputs
    ctx_values = jnp.sum(states * value_mix, axis=2) + value_skip * inputs
    return (states[-1], (ctx_keys, ctx_values))


def ssm_scan(inputs, starts, mixers):
    token_count, channels = inputs.shape
    state_count = mixers[0].shape[1]
    block_count = token_count // SQ

    def step_fn(previous, block_in):
        return ssm_block(previous, block_in, mixers)

    initial = jnp.zeros((channels, state_count), jnp.float32)
    final_state, (ctx_keys, ctx_values) = lax.scan(
        jax.checkpoint(step_fn),
        initial,
        (inputs.reshape(block_count, SQ, channels), starts.reshape(block_count, SQ)),
    )
    return (ctx_keys.reshape(token_count, channels), ctx_values.reshape(token_count, channels))


def block_mask(query_segment, context_segment):
    positions = jnp.arange(query_segment.shape[0], dtype=jnp.int32)
    own_part = (positions[None, :] <= positions[:, None]) & (
        query_segment[None, :] == query_segment[:, None]
    )
    ctx_part = context_segment[None, :] == query_segment[:, None]
    return jnp.concatenate([own_part, ctx_part], axis=1)


def split_blocks(values, head_count):
    token_count, columns = values.shape
    return values.reshape(token_count // BLK, BLK, head_count, columns // head_count)


def context_of(blocked):
    padding = jnp.zeros((1, CTX) + blocked.shape[2:], blocked.dtype)
    return jnp.concatenate([padding, blocked[:-1, BLK - CTX :]], axis=0)


def context_back(grad_ctx):
    block_count = grad_ctx.shape[0]
    leading = jnp.zeros((block_count - 1, BLK - CTX) + grad_ctx.shape[2:], jnp.float32)
    inner = jnp.concatenate([leading, grad_ctx[1:]], axis=1)
    trailing = jnp.zeros((1, BLK) + grad_ctx.shape[2:], jnp.float32)
    return jnp.concatenate([inner, trailing], axis=0)


def context_segments(flat_segments):
    seg_blocks = flat_segments.reshape(-1, BLK)
    block_count = seg_blocks.shape[0]
    earlier = jnp.concatenate(
        [jnp.full((1, CTX), -1, jnp.int32), seg_blocks[:-1, BLK - CTX :]], axis=0
    )
    row_first = (jnp.arange(block_count, dtype=jnp.int32) % (LEN // BLK) == 0)[:, None]
    return (seg_blocks, jnp.where(row_first, -1, earlier))


def block_scores(queries, key_all, query_segment, context_segment):
    scores = jnp.einsum(
        "qhd,khd->hqk", queries, key_all, preferred_element_type=jnp.float32
    ) * queries.shape[2] ** (-0.5)
    return jnp.where(block_mask(query_segment, context_segment)[None], scores, -1e30)


def block_forward(block_items):
    queries, key_own, key_ctx, value_own, value_ctx, query_segment, context_segment = block_items
    key_all = jnp.concatenate([key_own, key_ctx], axis=0)
    value_all = jnp.concatenate([value_own, value_ctx], axis=0)
    masked = block_scores(queries, key_all, query_segment, context_segment)
    row_max = jnp.max(masked, axis=2, keepdims=True)
    log_total = row_max + jnp.log(jnp.sum(jnp.exp(masked - row_max), axis=2, keepdims=True))
    attn_probs = jnp.exp(masked - log_total).astype(jnp.bfloat16)
    block_out = jnp.einsum(
        "hqk,khd->qhd", attn_probs, value_all, preferred_element_type=jnp.float32
    )
    return (block_out.astype(jnp.bfloat16), log_total[:, :, 0])


def block_backward(block_items):
    (
        queries,
        key_own,
        key_ctx,
        value_own,
        value_ctx,
        query_segment,
        context_segment,
        log_total,
        grad_out,
    ) = block_items
    key_all = jnp.concatenate([key_own, key_ctx], axis=0)
    value_all = jnp.concatenate([value_own, value_ctx], axis=0)
    scale = queries.shape[2] ** (-0.5)
    attn_probs = jnp.exp(
        block_scores(queries, key_all, query_segment, context_segment) - log_total[:, :, None]
    )
    grad_probs = jnp.einsum("qhd,khd->hqk", grad_out, value_all, preferred_element_type=jnp.float32)
    grad_value_all = jnp.einsum(
        "hqk,qhd->khd",
        attn_probs.astype(jnp.bfloat16),
        grad_out,
        preferred_element_type=jnp.float32,
    )
    weighted = jnp.sum(attn_probs * grad_probs, axis=2, keepdims=True)
    grad_scores = (attn_probs * (grad_probs - weighted)).astype(jnp.bfloat16)
    grad_queries = (
        jnp.einsum("hqk,khd->qhd", grad_scores, key_all, preferred_element_type=jnp.float32) * scale
    )
    grad_key_all = (
        jnp.einsum("hqk,qhd->khd", grad_scores, queries, preferred_element_type=jnp.float32) * scale
    )
    own_count = queries.shape[0]
    return (
        grad_queries,
        grad_key_all[:own_count],
        grad_key_all[own_count:],
        grad_value_all[:own_count],
        grad_value_all[own_count:],
    )


def attend(queries, keys_own, values_own, ctx_key, ctx_value, flat_segments):
    head_count = queries.shape[1] // (D // HEADS)
    query_segment, context_segment = context_segments(flat_segments)
    block_out, log_total = lax.map(
        block_forward,
        (
            split_blocks(queries, head_count),
            split_blocks(keys_own, head_count),
            context_of(split_blocks(ctx_key, head_count)),
            split_blocks(values_own, head_count),
            context_of(split_blocks(ctx_value, head_count)),
            query_segment,
            context_segment,
        ),
    )
    return (block_out.reshape(queries.shape), log_total)


def attend_back(
    queries, keys_own, values_own, ctx_key, ctx_value, flat_segments, log_total, grad_out
):
    head_count = queries.shape[1] // (D // HEADS)
    query_segment, context_segment = context_segments(flat_segments)
    grad_q, grad_k, grad_kc, grad_v, grad_vc = lax.map(
        block_backward,
        (
            split_blocks(queries, head_count),
            split_blocks(keys_own, head_count),
            context_of(split_blocks(ctx_key, head_count)),
            split_blocks(values_own, head_count),
            context_of(split_blocks(ctx_value, head_count)),
            query_segment,
            context_segment,
            log_total,
            split_blocks(grad_out, head_count),
        ),
    )
    shape_all = queries.shape
    return (
        grad_q.reshape(shape_all).astype(jnp.bfloat16),
        grad_k.reshape(shape_all).astype(jnp.bfloat16),
        grad_v.reshape(shape_all).astype(jnp.bfloat16),
        context_back(grad_kc).reshape(shape_all),
        context_back(grad_vc).reshape(shape_all),
    )


def matmul_t(left_side, right_side):
    return lax.dot_general(
        left_side, right_side, (((1,), (1,)), ((), ())), preferred_element_type=jnp.float32
    )


def blocked_grad(left_side, right_side, row_parts, chan_parts):
    left_split = left_side.reshape(left_side.shape[0], row_parts, left_side.shape[1] // row_parts)
    right_split = right_side.reshape(
        right_side.shape[0], chan_parts, right_side.shape[1] // chan_parts
    )
    product = jnp.einsum(
        "tab,tcd->acbd", left_split, right_split, preferred_element_type=jnp.float32
    )
    return product.reshape(row_parts * chan_parts * left_split.shape[2], right_split.shape[2])


def widen_part(shard_part, length_all, offset_index):
    zero_fill = jnp.zeros((length_all,) + shard_part.shape[1:], jnp.float32)
    return lax.dynamic_update_slice_in_dim(
        zero_fill, shard_part, offset_index * shard_part.shape[0], 0
    )


def shards(
    tokens,
    cotangent,
    segments,
    w_query,
    w_key,
    w_value,
    w_out,
    w_up,
    up_bias,
    w_down,
    down_bias,
    norm1_gain,
    norm1_bias,
    norm2_gain,
    norm2_bias,
    decay_rates,
    input_mix,
    key_mix,
    value_mix,
    key_skip,
    value_skip,
):
    row_parts = lax.axis_size("rows")
    chan_parts = lax.axis_size("chan")
    chan_index = lax.axis_index("chan")
    residual = tokens.astype(jnp.float32)
    first_normed, norm1_back = jax.vjp(layer_norm, residual, norm1_gain, norm1_bias)
    first_hidden = first_normed.astype(jnp.bfloat16)
    full_query, full_key, full_value, full_out = (
        lax.all_gather(w_query, "chan", axis=1, tiled=True),
        lax.all_gather(w_key, "chan", axis=1, tiled=True),
        lax.all_gather(w_value, "chan", axis=1, tiled=True),
        lax.all_gather(w_out, "chan", axis=1, tiled=True),
    )
    queries = jnp.dot(first_hidden, full_query, preferred_element_type=jnp.float32).astype(
        jnp.bfloat16
    )
    keyed = jnp.dot(first_hidden, full_key, preferred_element_type=jnp.float32).astype(jnp.bfloat16)
    valued = jnp.dot(first_hidden, full_value, preferred_element_type=jnp.float32).astype(
        jnp.bfloat16
    )
    head_query, head_key, head_value, head_input = (
        lax.all_to_all(queries, "chan", split_axis=1, concat_axis=0, tiled=True),
        lax.all_to_all(keyed, "chan", split_axis=1, concat_axis=0, tiled=True),
        lax.all_to_all(valued, "chan", split_axis=1, concat_axis=0, tiled=True),
        lax.all_to_all(first_hidden, "chan", split_axis=1, concat_axis=0, tiled=True),
    )
    starts = segment_starts(segments)
    flat_segments = segments.reshape(-1)
    mixers = (decay_rates, input_mix, key_mix, value_mix, key_skip, value_skip)

    def run_ssm(inputs, weights):
        return ssm_scan(inputs, starts, weights)

    (ctx_key, ctx_value), ssm_back = jax.vjp(run_ssm, head_input.astype(jnp.float32), mixers)
    ctx_key = ctx_key.astype(jnp.bfloat16)
    ctx_value = ctx_value.astype(jnp.bfloat16)
    head_out, log_total = attend(
        head_query, head_key, head_value, ctx_key, ctx_value, flat_segments
    )
    attn_out = lax.all_to_all(head_out, "chan", split_axis=0, concat_axis=1, tiled=True)
    second_residual = residual + jnp.dot(attn_out, full_out, preferred_element_type=jnp.float32)
    second_normed, norm2_back = jax.vjp(layer_norm, second_residual, norm2_gain, norm2_bias)
    second_hidden = second_normed.astype(jnp.bfloat16)
    group_hidden = lax.all_gather(second_hidden, "chan", axis=0, tiled=True)
    preact = jnp.dot(group_hidden, w_up, preferred_element_type=jnp.float32) + up_bias
    activated, gelu_back = jax.vjp(jax.nn.gelu, preact)
    act_low = activated.astype(jnp.bfloat16)
    picked = act_low
    ffn_out = lax.psum_scatter(
        matmul_t(picked, w_down).astype(jnp.bfloat16), "chan", scatter_dimension=0, tiled=True
    ).astype(jnp.float32)
    output = (second_residual + ffn_out + down_bias).astype(jnp.bfloat16)
    group_cot = lax.all_gather(cotangent, "chan", axis=0, tiled=True)
    grad_act = jnp.dot(group_cot, w_down, preferred_element_type=jnp.float32)
    grad_preact = gelu_back(grad_act)[0].astype(jnp.bfloat16)
    picked = grad_preact
    grad_second_hidden = lax.psum_scatter(
        matmul_t(picked, w_up).astype(jnp.bfloat16), "chan", scatter_dimension=0, tiled=True
    ).astype(jnp.float32)
    contract_rows = (((0,), (0,)), ((), ()))
    grad_up_w, grad_down_w = (
        lax.psum_scatter(
            lax.dot_general(
                group_hidden, grad_preact, contract_rows, preferred_element_type=jnp.float32
            ).astype(jnp.bfloat16),
            "rows",
            scatter_dimension=0,
            tiled=True,
        ).astype(jnp.float32),
        lax.psum_scatter(
            lax.dot_general(
                group_cot, act_low, contract_rows, preferred_element_type=jnp.float32
            ).astype(jnp.bfloat16),
            "rows",
            scatter_dimension=0,
            tiled=True,
        ).astype(jnp.float32),
    )
    up_bias_grad = widen_part(jnp.sum(grad_preact.astype(jnp.float32), axis=0), FF, chan_index)
    down_bias_grad = jnp.sum(cotangent.astype(jnp.float32), axis=0)
    grad_resid_part, grad_gain2, grad_bias2 = norm2_back(grad_second_hidden)
    grad_second_residual = cotangent.astype(jnp.float32) + grad_resid_part
    grad_branch = grad_second_residual.astype(jnp.bfloat16)
    grad_attention = matmul_t(grad_branch, full_out).astype(jnp.bfloat16)
    head_grad = lax.all_to_all(grad_attention, "chan", split_axis=1, concat_axis=0, tiled=True)
    grad_q, grad_k, grad_v, grad_ck, grad_cv = attend_back(
        head_query, head_key, head_value, ctx_key, ctx_value, flat_segments, log_total, head_grad
    )
    grad_input, grad_mixers = ssm_back((grad_ck, grad_cv))
    back_query, back_key, back_value, back_input = (
        lax.all_to_all(grad_q, "chan", split_axis=0, concat_axis=1, tiled=True),
        lax.all_to_all(grad_k, "chan", split_axis=0, concat_axis=1, tiled=True),
        lax.all_to_all(grad_v, "chan", split_axis=0, concat_axis=1, tiled=True),
        lax.all_to_all(
            grad_input.astype(jnp.bfloat16), "chan", split_axis=0, concat_axis=1, tiled=True
        ),
    )
    grad_first_hidden = (
        matmul_t(back_query, full_query)
        + matmul_t(back_key, full_key)
        + matmul_t(back_value, full_value)
        + back_input.astype(jnp.float32)
    )
    grad_first_part, grad_gain1, grad_bias1 = norm1_back(grad_first_hidden)
    grad_tokens = (grad_second_residual + grad_first_part).astype(jnp.bfloat16)
    grad_query_w, grad_key_w, grad_value_w, grad_out_w = (
        lax.psum_scatter(
            blocked_grad(first_hidden, back_query, row_parts, chan_parts),
            ("rows", "chan"),
            scatter_dimension=0,
            tiled=True,
        ),
        lax.psum_scatter(
            blocked_grad(first_hidden, back_key, row_parts, chan_parts),
            ("rows", "chan"),
            scatter_dimension=0,
            tiled=True,
        ),
        lax.psum_scatter(
            blocked_grad(first_hidden, back_value, row_parts, chan_parts),
            ("rows", "chan"),
            scatter_dimension=0,
            tiled=True,
        ),
        lax.psum_scatter(
            blocked_grad(attn_out, grad_branch, row_parts, chan_parts),
            ("rows", "chan"),
            scatter_dimension=0,
            tiled=True,
        ),
    )
    summed = lax.psum(
        (
            grad_gain1,
            grad_bias1,
            grad_gain2,
            grad_bias2,
            down_bias_grad,
            up_bias_grad,
            widen_part(grad_mixers[0], D, chan_index),
            widen_part(grad_mixers[1], D, chan_index),
            widen_part(grad_mixers[2], D, chan_index),
            widen_part(grad_mixers[3], D, chan_index),
            widen_part(grad_mixers[4], D, chan_index),
            widen_part(grad_mixers[5], D, chan_index),
        ),
        ("rows", "chan"),
    )
    return (
        output,
        grad_tokens,
        grad_query_w,
        grad_key_w,
        grad_value_w,
        grad_out_w,
        grad_up_w,
        summed[5],
        grad_down_w,
        summed[4],
        summed[0],
        summed[1],
        summed[2],
        summed[3],
        summed[6],
        summed[7],
        summed[8],
        summed[9],
        summed[10],
        summed[11],
    )


def solution(mesh):
    in_specs = (
        P(("rows", "chan"), None),
        P(("rows", "chan"), None),
        P("rows", None),
        P(None, "chan"),
        P(None, "chan"),
        P(None, "chan"),
        P(None, "chan"),
        P(None, "chan"),
        P("chan"),
        P(None, "chan"),
        P(),
        P(),
        P(),
        P(),
        P(),
        P("chan", None),
        P("chan", None),
        P("chan", None),
        P("chan", None),
        P("chan"),
        P("chan"),
    )
    out_specs = (
        P(("rows", "chan"), None),
        P(("rows", "chan"), None),
        P("rows", "chan"),
        P("rows", "chan"),
        P("rows", "chan"),
        P("rows", "chan"),
        P("rows", "chan"),
        P(),
        P("rows", "chan"),
        P(),
        P(),
        P(),
        P(),
        P(),
        P(),
        P(),
        P(),
        P(),
        P(),
        P(),
    )
    return jax.shard_map(shards, mesh=mesh, in_specs=in_specs, out_specs=out_specs, check_vma=False)
```

profile of v0, /device:TPU:0, one launch (start us, length us, event | category | flops | bytes accessed | tf_op | source)
XLA Modules:
  0.0 1819.1 jit_solution(18391646115877101129)
XLA Ops:
  23.5 16.9 all-gather.11.cloned.1.call-done
  47.7 21.8 %all-gather.9.cloned.1.call-done = bf16[1024,1024]{1,0:T(8,128)(2,1)} async-done(((bf16[1024,256]{1,0:T(8,128)(2,1)}), bf16[1024,1024]{1,0:T(8,128)(2,1)}) %all-gather.9.cloned.1.call-update) | async-done | bytes 2097168 | tf_op jit(solution)/shard_map/all_gather | solution.py:274
  78.1 20.6 %all-gather.7.cloned.1.call-done = bf16[1024,1024]{1,0:T(8,128)(2,1)} async-done(((bf16[1024,256]{1,0:T(8,128)(2,1)}), bf16[1024,1024]{1,0:T(8,128)(2,1)}) %all-gather.7.cloned.1.call-update) | async-done | bytes 2097168 | tf_op jit(solution)/shard_map/all_gather | solution.py:276
  107.9 460.0 %while.85 = (s32[]{:T(128)}, f32[256,16]{0,1:T(8,128)S(1)}, bf16[4,256,256]{2,1,0:T(8,128)(2,1)}, bf16[4,256,256]{2,1,0:T(8,128)(2,1)}, f32[4,256,16]{1,2,0:T(8,...) while((s32[]{:T(128)}, f32[256,16]{0,1:T(8,128)S(1)}, ...), condition=%wide.region_9.10_spmd.clone.clone, body=%wide.region_2.9_spmd.clone.clone.sunk | while | flops 151174912 | bytes 53320048 | solution.py:64
  110.0 97.2 %fusion.221 = f32[16,256,2,128]{1,0,3,2:T(8,128)S(1)} fusion(f32[16,256,2,128]{1,0,3,2:T(8,128)S(1)} %bitcast.409), kind=kOutput, calls=%fused_computation.282.clone.1 | output fusion | flops 133169152 | bytes 8388608 | tf_op jit(solution)/shard_map/reduce-window.46
  214.8 7.0 multiply_reduce_fusion.20
  225.0 97.2 %fusion.221 = f32[16,256,2,128]{1,0,3,2:T(8,128)S(1)} fusion(f32[16,256,2,128]{1,0,3,2:T(8,128)S(1)} %bitcast.409), kind=kOutput, calls=%fused_computation.282.clone.1 | output fusion | flops 133169152 | bytes 8388608 | tf_op jit(solution)/shard_map/reduce-window.46
  329.8 7.0 multiply_reduce_fusion.20
  339.9 97.2 %fusion.221 = f32[16,256,2,128]{1,0,3,2:T(8,128)S(1)} fusion(f32[16,256,2,128]{1,0,3,2:T(8,128)S(1)} %bitcast.409), kind=kOutput, calls=%fused_computation.282.clone.1 | output fusion | flops 133169152 | bytes 8388608 | tf_op jit(solution)/shard_map/reduce-window.46
  444.7 7.0 multiply_reduce_fusion.20
  454.9 97.2 %fusion.221 = f32[16,256,2,128]{1,0,3,2:T(8,128)S(1)} fusion(f32[16,256,2,128]{1,0,3,2:T(8,128)S(1)} %bitcast.409), kind=kOutput, calls=%fused_computation.282.clone.1 | output fusion | flops 133169152 | bytes 8388608 | tf_op jit(solution)/shard_map/reduce-window.46
  559.7 7.0 multiply_reduce_fusion.20
  584.4 19.6 %while.82 = (s32[]{:T(128)}, bf16[2,512,2,128]{3,2,1,0:T(2,128)(2,1)}, f32[2,2,512]{2,1,0:T(2,128)}, bf16[2,512,2,128]{3,2,1,0:T(2,128)(2,1)}, bf16[2,128,2,128]...) while((s32[]{:T(128)}, ...), condition=%wide.region_13.14_spmd, body=%wide.region_10.13_spmd.sunk | while | flops 345373696 | bytes 14132945 | solution.py:176
  605.4 12.3 all_to_all.154
  623.4 22.5 %all-gather.15.cloned.1.call-done = bf16[1024,1024]{1,0:T(8,128)(2,1)} async-done(((bf16[256,1024]{1,0:T(8,128)(2,1)}), bf16[1024,1024]{1,0:T(8,128)(2,1)}) %all-gather.15.cloned.1.call-update) | async-done | bytes 2097168 | tf_op jit(solution)/shard_map/all_gather | solution.py:309
  645.9 6.6 fusion.125
  652.6 17.4 all-gather.17.cloned.1.call-done
  670.0 8.0 convert_reduce_fusion
  689.8 6.5 convert_bitcast_fusion
  699.0 15.6 reduce-scatter.13.cloned.1.call-done
  716.7 32.1 %reduce-scatter.11.cloned.1.call-done = bf16[256,1024]{1,0:T(8,128)(2,1)} async-done(((bf16[1024,1024]{1,0:T(8,128)(2,1)}), bf16[256,1024]{1,0:T(8,128)(2,1)}) %reduce-scatter.11.cloned.1.call-update) | async-done | bytes 524304 | tf_op jit(solution)/shard_map/reduce_scatter | solution.py:314
  766.5 19.8 %while.83 = (s32[]{:T(128)}, bf16[2,512,2,128]{1,3,2,0:T(8,128)(2,1)}, bf16[2,512,2,128]{1,3,2,0:T(8,128)(2,1)}, f32[2,128,2,128]{1,3,2,0:T(8,128)}, bf16[2,512,...) while((s32[]{:T(128)}, ...), condition=%wide.region_22.23_spmd, body=%wide.region_20.22_spmd.sunk | while | flops 848198656 | bytes 45578216 | solution.py:196
  791.5 324.4 %while.84 = (s32[]{:T(128)}, f32[256,16]{0,1:T(8,128)S(1)}, f32[256,16]{0,1:T(8,128)S(1)}, f32[256,16]{0,1:T(8,128)S(1)}, f32[256]{0:T(256)S(1)}, /*index=5*/f32...) while((s32[]{:T(128)}, f32[256,16]{0,1:T(8,128)S(1)}, ...), condition=%wide.region_41.42_spmd.clone, body=%wide.region_23.41_spmd.clone.sunk | while | flops 322500352 | bytes 102800232 | solution.py:64
  803.8 9.6 negate_select_fusion.2
  813.4 37.2 %scatter_fusion = f32[256,256,16]{1,2,0:T(8,128)} fusion(f32[256,256,16]{1,2,0:T(8,128)} %get-tuple-element.1927, s32[256]{0:T(256)S(1)} %fusion.217, f32[256,256,16]{1,2,0:T(8,128)} %get-tuple-element.1928), kind=kCustom, calls=%fused_computation.2.clone.clone.1 | custom fusion | flops 1048576 | bytes 12583936 | tf_op jit(solution)/shard_map/transpose(jvp())/while/body/eval_jaxpr/checkpoint/jit(_take)/scatter-add | solution.py:42
  850.5 10.8 fusion.218
  863.7 8.5 multiply_reduce_fusion.18
  884.8 9.7 negate_select_fusion.2
  894.5 37.1 %scatter_fusion = f32[256,256,16]{1,2,0:T(8,128)} fusion(f32[256,256,16]{1,2,0:T(8,128)} %get-tuple-element.1927, s32[256]{0:T(256)S(1)} %fusion.217, f32[256,256,16]{1,2,0:T(8,128)} %get-tuple-element.1928), kind=kCustom, calls=%fused_computation.2.clone.clone.1 | custom fusion | flops 1048576 | bytes 12583936 | tf_op jit(solution)/shard_map/transpose(jvp())/while/body/eval_jaxpr/checkpoint/jit(_take)/scatter-add | solution.py:42
  931.6 10.8 fusion.218
  944.6 8.5 multiply_reduce_fusion.18
  965.7 9.6 negate_select_fusion.2
  975.3 37.2 %scatter_fusion = f32[256,256,16]{1,2,0:T(8,128)} fusion(f32[256,256,16]{1,2,0:T(8,128)} %get-tuple-element.1927, s32[256]{0:T(256)S(1)} %fusion.217, f32[256,256,16]{1,2,0:T(8,128)} %get-tuple-element.1928), kind=kCustom, calls=%fused_computation.2.clone.clone.1 | custom fusion | flops 1048576 | bytes 12583936 | tf_op jit(solution)/shard_map/transpose(jvp())/while/body/eval_jaxpr/checkpoint/jit(_take)/scatter-add | solution.py:42
  1012.6 10.8 fusion.218
  1025.6 8.5 multiply_reduce_fusion.18
  1046.7 9.6 negate_select_fusion.2
  1056.3 37.1 %scatter_fusion = f32[256,256,16]{1,2,0:T(8,128)} fusion(f32[256,256,16]{1,2,0:T(8,128)} %get-tuple-element.1927, s32[256]{0:T(256)S(1)} %fusion.217, f32[256,256,16]{1,2,0:T(8,128)} %get-tuple-element.1928), kind=kCustom, calls=%fused_computation.2.clone.clone.1 | custom fusion | flops 1048576 | bytes 12583936 | tf_op jit(solution)/shard_map/transpose(jvp())/while/body/eval_jaxpr/checkpoint/jit(_take)/scatter-add | solution.py:42
  1093.4 10.8 fusion.218
  1106.5 8.5 multiply_reduce_fusion.18
  1127.8 8.7 all-to-all-done.8
  1141.4 11.4 all_to_all.155
  1157.7 11.3 all_to_all.156
  1191.4 40.4 %all-reduce.8 = (f32[4096]{0:T(1024)}, f32[1024]{0:T(1024)}, f32[1024]{0:T(1024)}, f32[1024]{0:T(1024)}, f32[1024]{0:T(1024)}, /*index=5*/f32[1024]{0:T(1024)}, f32[1024]{0:T(1024)}, f32[1024]{0:T(1024)}) all-reduce(f32[4096]{0:T(1024)S(1)} %dynamic_update_slice.85, ...), channel_id=1, replica_groups=mesh['rows'=8,'chan'=4] {'rows','chan'}, use_global_device_ids=true, to_apply=%region_50.51 | all-reduce | flops 11264 | bytes 90112 | tf_op jit(solution)/shard_map/psum | solution.py:397
  1231.8 11.3 all-reduce.12.cloned.1.call-done
  1243.1 143.3 %reduce-scatter.21.cloned.1.call-done = f32[128,256]{1,0:T(8,128)} async-done(((f32[4096,256]{1,0:T(8,128)}), f32[128,256]{1,0:T(8,128)}) %reduce-scatter.21.cloned.1.call-update) | async-done | bytes 131088 | tf_op jit(solution)/shard_map/reduce_scatter | solution.py:390
  1386.5 140.4 %reduce-scatter.19.cloned.1.call-done = f32[128,256]{1,0:T(8,128)} async-done(((f32[4096,256]{1,0:T(8,128)}), f32[128,256]{1,0:T(8,128)}) %reduce-scatter.19.cloned.1.call-update) | async-done | bytes 131088 | tf_op jit(solution)/shard_map/reduce_scatter | solution.py:384
  1526.9 139.9 %reduce-scatter.17.cloned.1.call-done = f32[128,256]{1,0:T(8,128)} async-done(((f32[4096,256]{1,0:T(8,128)}), f32[128,256]{1,0:T(8,128)}) %reduce-scatter.17.cloned.1.call-update) | async-done | bytes 131088 | tf_op jit(solution)/shard_map/reduce_scatter | solution.py:378
  1666.8 139.7 %reduce-scatter.15.cloned.1.call-done = f32[128,256]{1,0:T(8,128)} async-done(((f32[4096,256]{1,0:T(8,128)}), f32[128,256]{1,0:T(8,128)}) %reduce-scatter.15.cloned.1.call-update) | async-done | bytes 131088 | tf_op jit(solution)/shard_map/reduce_scatter | solution.py:372
  (668 shorter events, 293.6 us)
Async XLA Ops:
  7.2 662.8 %copy-start = (bf16[1024,1024]{1,0:T(8,128)(2,1)S(1)}, bf16[1024,1024]{1,0:T(8,128)(2,1)}, u32[]{:S(2)}) copy-start(bf16[1024,1024]{1,0:T(8,128)(2,1)} %param.38) | copy-start | bytes 6291460
  7.2 11.9 copy-start.64
  7.2 16.2 copy-start.5
  7.2 16.2 copy-start.27
  7.2 33.1 %all-gather.11.cloned.1.call-start = ((), (), s32[]{:S(2)}) async-start(), calls=%async_computation.20 | async-start | bytes 2621440 | tf_op jit(solution)/shard_map/all_gather | solution.py:275
  8.0 61.5 %all-gather.9.cloned.1.call-start = ((), (), s32[]{:S(2)}) async-start(), calls=%async_computation.19 | async-start | bytes 2621440 | tf_op jit(solution)/shard_map/all_gather | solution.py:274
  8.7 89.9 %all-gather.7.cloned.1.call-start = ((), (), s32[]{:S(2)}) async-start(), calls=%async_computation.18 | async-start | bytes 2621440 | tf_op jit(solution)/shard_map/all_gather | solution.py:276
  13.4 58.5 %copy-start.12 = (bf16[256,1024]{1,0:T(8,128)(2,1)}, bf16[256,1024]{1,0:T(8,128)(2,1)S(1)}, u32[]{:S(2)}) copy-start(bf16[256,1024]{1,0:T(8,128)(2,1)S(1)} %fusion.100) | copy-start | bytes 1572868
  14.3 29.3 %all-to-all-start.1 = ((bf16[256,4,256]{2,0,1:T(8,128)(2,1)}), bf16[256,4,256]{2,0,1:T(8,128)(2,1)S(1)}, u32[]{:S(2)}, u32[]{:S(2)}) async-start(bf16[256,4,256]{2,0,1:T(8,128)(2,1)} %bitcast.438), calls=%async_computation.1 | async-start | bytes 1048576 | tf_op jit(solution)/shard_map/all_to_all | solution.py:290
  18.5 600.2 %all-gather.13.cloned.1.call-start = ((), (), s32[]{:S(2)}) async-start(), calls=%async_computation.21 | async-start | bytes 2621440 | tf_op jit(solution)/shard_map/all_gather | solution.py:277
  43.5 29.1 %copy-start.20 = (bf16[256,4,256]{2,0,1:T(8,128)(2,1)}, bf16[256,4,256]{2,0,1:T(8,128)(2,1)S(1)}, u32[]{:S(2)}) copy-start(bf16[256,4,256]{2,0,1:T(8,128)(2,1)S(1)} %all-to-all-done.1) | copy-start | bytes 1572868
  43.5 29.1 %all-to-all-start.3 = ((bf16[256,4,256]{2,0,1:T(8,128)(2,1)}), bf16[256,4,256]{2,0,1:T(8,128)(2,1)}, u32[]{:S(2)}, u32[]{:S(2)}) async-start(bf16[256,4,256]{2,0,1:T(8,128)(2,1)} %bitcast.440), calls=%async_computation.3 | async-start | bytes 1048576 | tf_op jit(solution)/shard_map/all_to_all | solution.py:288
  72.7 29.3 %all-to-all-start.2 = ((bf16[256,4,256]{2,0,1:T(8,128)(2,1)}), bf16[256,4,256]{2,0,1:T(8,128)(2,1)}, u32[]{:S(2)}, u32[]{:S(2)}) async-start(bf16[256,4,256]{2,0,1:T(8,128)(2,1)} %bitcast.278), calls=%async_computation.2 | async-start | bytes 1048576 | tf_op jit(solution)/shard_map/all_to_all | solution.py:287
  76.8 31.1 %copy-start.14 = (f32[256,16]{0,1:T(8,128)S(1)}, f32[256,16]{0,1:T(8,128)}, u32[]{:S(2)}) copy-start(f32[256,16]{0,1:T(8,128)} %param.46) | copy-start | bytes 49156
  76.8 31.0 %copy-start.16 = (f32[256,16]{0,1:T(8,128)S(1)}, f32[256,16]{0,1:T(8,128)}, u32[]{:S(2)}) copy-start(f32[256,16]{0,1:T(8,128)} %param.47) | copy-start | bytes 49156
  76.8 31.0 %copy-start.42 = (f32[256]{0:T(256)S(1)}, f32[256]{0:T(256)}, u32[]{:S(2)}) copy-start(f32[256]{0:T(256)} %param.48) | copy-start | bytes 3076
  76.9 31.0 %copy-start.44 = (f32[256]{0:T(256)S(1)}, f32[256]{0:T(256)}, u32[]{:S(2)}) copy-start(f32[256]{0:T(256)} %param.49) | copy-start | bytes 3076
  102.0 480.5 %all-to-all-start = ((bf16[256,4,256]{2,0,1:T(8,128)(2,1)}), bf16[256,4,256]{2,0,1:T(8,128)(2,1)}, u32[]{:S(2)}, u32[]{:S(2)}) async-start(bf16[256,4,256]{2,0,1:T(8,128)(2,1)} %bitcast.437), calls=%async_computation | async-start | bytes 1048576 | tf_op jit(solution)/shard_map/all_to_all | solution.py:289
  106.1 539.8 %all-gather.15.cloned.1.call-start = ((), (), s32[]{:S(2)}) async-start(), calls=%async_computation.22 | async-start | bytes 2621440 | tf_op jit(solution)/shard_map/all_gather | solution.py:309
  214.8 7.1 copy-start.25
  329.8 7.1 copy-start.25
  444.7 7.1 copy-start.25
  559.7 7.1 copy-start.25
  567.8 16.6 copy-start.4
  604.0 17.6 copy-start.61
  604.0 17.6 copy-start.71
  622.7 47.2 %all-gather.17.cloned.1.call-start = ((), (), s32[]{:S(2)}) async-start(), calls=%async_computation.24 | async-start | bytes 2621440 | tf_op jit(solution)/shard_map/all_gather | solution.py:318
  623.3 46.6 %copy-start.75 = (f32[1024]{0:T(1024)S(1)}, f32[1024]{0:T(1024)}, u32[]{:S(2)}) copy-start(f32[1024]{0:T(1024)} %param.37) | copy-start | bytes 12292
  623.3 91.3 %reduce-scatter.13.cloned.1.call-start = ((), (), s32[]{:S(2)}) async-start(), calls=%async_computation.25 | async-start | bytes 2621440 | tf_op jit(solution)/shard_map/reduce_scatter | solution.py:322
  670.0 9.3 copy-start.74
  683.1 65.7 %reduce-scatter.11.cloned.1.call-start = ((), (), s32[]{:S(2)}) async-start(), calls=%async_computation.23 | async-start | bytes 2621440 | tf_op jit(solution)/shard_map/reduce_scatter | solution.py:314
  689.6 486.6 %reduce-scatter.25.cloned.1.call-start = ((), (), s32[]{:S(2)}) async-start(), calls=%async_computation.31 | async-start | bytes 2359296
  696.3 52.6 %copy-start.73 = (f32[1024]{0:T(1024)S(1)}, f32[1024]{0:T(1024)}, u32[]{:S(2)}) copy-start(f32[1024]{0:T(1024)} %param.39) | copy-start | bytes 12292
  698.9 52.5 %copy-start.10 = (bf16[256,1024]{1,0:T(8,128)(2,1)S(1)}, bf16[256,1024]{1,0:T(8,128)(2,1)}, u32[]{:S(2)}) copy-start(bf16[256,1024]{1,0:T(8,128)(2,1)} %param.30) | copy-start | bytes 1572868
  751.4 11.4 copy-start.8
  751.4 11.4 copy-start.67
  753.3 12.3 all-to-all-start.5
  756.7 421.5 %reduce-scatter.23.cloned.1.call-start = ((), (), s32[]{:S(2)}) async-start(), calls=%async_computation.30 | async-start | bytes 2359296 | tf_op jit(solution)/shard_map/reduce_scatter | solution.py:327
  762.8 480.3 %all-reduce.12.cloned.1.call-start = ((), (), s32[]{:S(2)}) async-start(), calls=%async_computation.32 | async-start | bytes 524288 | tf_op jit(solution)/shard_map/psum | solution.py:397
  1117.2 269.2 %reduce-scatter.21.cloned.1.call-start = ((), (), s32[]{:S(2)}) async-start(), calls=%async_computation.29 | async-start | bytes 4325376 | tf_op jit(solution)/shard_map/reduce_scatter | solution.py:390
  1124.1 12.4 all-to-all-start.8
  1127.6 399.3 %reduce-scatter.19.cloned.1.call-start = ((), (), s32[]{:S(2)}) async-start(), calls=%async_computation.28 | async-start | bytes 4325376 | tf_op jit(solution)/shard_map/reduce_scatter | solution.py:384
  1139.7 527.1 %reduce-scatter.17.cloned.1.call-start = ((), (), s32[]{:S(2)}) async-start(), calls=%async_computation.27 | async-start | bytes 4325376 | tf_op jit(solution)/shard_map/reduce_scatter | solution.py:378
  1155.9 650.5 %reduce-scatter.15.cloned.1.call-start = ((), (), s32[]{:S(2)}) async-start(), calls=%async_computation.26 | async-start | bytes 4325376 | tf_op jit(solution)/shard_map/reduce_scatter | solution.py:372
  1172.2 7.9 copy-start.56
  1172.2 8.0 copy-start.58
  1172.2 12.4 all-to-all-start.9
  1188.3 624.0 %copy-start.1 = (bf16[1024,1024]{1,0:T(8,128)(2,1)S(1)}, bf16[1024,1024]{1,0:T(8,128)(2,1)}, u32[]{:S(2)}) copy-start(bf16[1024,1024]{1,0:T(8,128)(2,1)} %param.38) | copy-start | bytes 6291460
  (78 other events, 185.7 us)
Sparse Core Ops, SparseCore 0:
  9.6 30.7 all-gather.10
  41.9 27.5 all-gather.8
  71.1 27.5 all-gather.6
  100.0 27.8 all-gather.12
  622.8 23.0 all-gather.14
  647.3 22.5 all-gather.16
  683.2 31.4 reduce-scatter.12
  717.3 31.4 reduce-scatter.10
  752.3 67.8 reduce-scatter.24
  823.6 66.7 reduce-scatter.22
  1117.4 125.7 all-reduce.11
  1245.8 140.5 reduce-scatter.20
  1389.3 137.5 reduce-scatter.18
  1529.6 137.1 reduce-scatter.16
  1669.5 136.9 reduce-scatter.14
where the time goes:
time: 1830 us; the launch traced here: 1820 us
  other arithmetic  739 us (40%)
  waiting for transfers between devices  738 us (40%)
  local copies, waits for them, and re-layouts  154 us (8%)
  blocking collectives  75.4 us (4%)
  matrix products  67.8 us (4%)
  starting transfers between devices  28 us (2%)
    another operation x61, other arithmetic  461 us
    scatter-add x4, other arithmetic, ssm_block(): before = jnp.take(running, jnp.maximum(last_start - 1, 0), axis=0)  149 us
    reduce_scatter x1, waiting for transfers between devices, shards(): lax.psum_scatter(blocked_grad(attn_out, grad_branch, row_parts, chan_part...  143 us
    reduce_scatter x1, waiting for transfers between devices, shards(): lax.psum_scatter(blocked_grad(first_hidden, back_value, row_parts, chan_p...  140 us
    reduce_scatter x1, waiting for transfers between devices, shards(): lax.psum_scatter(blocked_grad(first_hidden, back_key, row_parts, chan_par...  140 us
    reduce_scatter x1, waiting for transfers between devices, shards(): lax.psum_scatter(blocked_grad(first_hidden, back_query, row_parts, chan_p...  140 us
    reduce_sum x12, other arithmetic, ssm_block(): ctx_values = jnp.sum(states * value_mix, axis=2) + value_skip * inputs  62.3 us
    psum x1, blocking collectives, shards(): lax.psum((grad_gain1, grad_bias1, grad_gain2, grad_bias2, down_bias_grad,...  40.4 us
  transfers between devices with their start and end apart: 22, of which 15 were waited for; matrix products, arithmetic and copies ran while one was open for 50% of the time, Pallas kernels for 0%

commit v1 on v0

v1 whole, which is shorter than its diff:
```python
import functools

import jax
import jax.numpy as jnp
from jax import lax
from jax.experimental import pallas as pl
from jax.experimental.pallas import tpu as pltpu
from jax.sharding import PartitionSpec as P

HEAD = 128
CTX = 128
BLK = 512
EPS = 1e-05
NEG = -1e30
F32 = jnp.float32
BF16 = jnp.bfloat16
NN = (((1,), (0,)), ((), ()))
NT = (((1,), (1,)), ((), ()))
TN = (((0,), (0,)), ((), ()))


def dot(left, right, dims=NN):
    return lax.dot_general(left, right, dims, preferred_element_type=F32)


def ssm_local(x_ref, mask_col, par_ref, first, count, g, e, keep_ref=None):
    a = par_ref[0]
    row = lax.broadcasted_iota(jnp.int32, (8, 1), 0)

    def step(i, carry):
        g, e = carry
        base = pl.multiple_of(first + i * 8, 8)
        x8 = x_ref[pl.ds(base, 8), :].astype(F32)
        x8 = jnp.where(mask_col(row + base), x8, 0.0)
        for t in range(8):
            e = a * e + g
            g = a * g + x8[t : t + 1, :]
            if keep_ref is not None:
                keep_ref[i * 8 + t] = g
        return (g, e)

    return lax.fori_loop(0, count // 8, step, (g, e))


def ssm_prefix(x_ref, mask_col, par_ref):
    a128, d128 = par_ref[6], par_ref[7]
    zero = jnp.zeros(par_ref.shape[1:], F32)
    parts = (BLK - CTX) // 128
    a = par_ref[0]
    row = lax.broadcasted_iota(jnp.int32, (8, 1), 0)

    def step(i, carry):
        out = []
        for j in range(parts):
            g, e = carry[j]
            base = pl.multiple_of(j * 128 + i * 8, 8)
            x8 = x_ref[pl.ds(base, 8), :].astype(F32)
            x8 = jnp.where(mask_col(row + base), x8, 0.0)
            for t in range(8):
                e = a * e + g
                g = a * g + x8[t : t + 1, :]
            out.append((g, e))
        return tuple(out)

    ends = lax.fori_loop(0, 16, step, tuple((zero, zero) for _ in range(parts)))
    g, e = ends[0]
    for j in range(1, parts):
        e = ends[j][1] + a128 * e + d128 * g
        g = ends[j][0] + a128 * g
    return g, e


def segment_mask(seg_ref):
    segs = seg_ref[...]
    here = segs[:, BLK : BLK + 1]
    first = jnp.sum(jnp.where(segs < here, 1, 0), axis=1, keepdims=True)
    return lambda index: index >= first


def ssm_fwd_kernel(x_ref, seg_ref, par_ref, skip_ref, ck_ref, cv_ref, g_ref):
    mask_col = segment_mask(seg_ref)
    g, e = ssm_prefix(x_ref, mask_col, par_ref)
    a, kb, vb = par_ref[0], par_ref[4], par_ref[5]
    first = BLK - CTX
    row = lax.broadcasted_iota(jnp.int32, (8, 1), 0)

    def step(i, g):
        base = pl.multiple_of(first + i * 8, 8)
        raw = x_ref[pl.ds(base, 8), :].astype(F32)
        x8 = jnp.where(mask_col(row + base), raw, 0.0)
        ks, vs = [], []
        for t in range(8):
            g = a * g + x8[t : t + 1, :]
            ks.append(jnp.sum(g * kb, axis=0, keepdims=True))
            vs.append(jnp.sum(g * vb, axis=0, keepdims=True))
        at = pl.ds(pl.multiple_of(i * 8, 8), 8)
        g_ref[at, :] = jnp.concatenate(ks, axis=0) + skip_ref[0:1, :] * raw
        ck_ref[at, :] = jnp.concatenate(vs, axis=0) + skip_ref[1:2, :] * raw
        return g

    lax.fori_loop(0, CTX // 8, step, g)
    cv_ref[...] = ck_ref[...]
    ck_ref[...] = g_ref[...]


def ssm_bwd_kernel(x_ref, seg_ref, par_ref, skip_ref, gk_ref, gv_ref, gx_ref, gp_ref, gs_ref, keep_ref):
    mask_col = segment_mask(seg_ref)
    g0, e0 = ssm_prefix(x_ref, mask_col, par_ref)
    a, b, km, vm = par_ref[0], par_ref[1], par_ref[2], par_ref[3]
    first = BLK - CTX
    zero = jnp.zeros(par_ref.shape[1:], F32)
    keep_ref[0] = g0
    row = lax.broadcasted_iota(jnp.int32, (8, 1), 0)

    def ahead(i, g):
        base = pl.multiple_of(first + i * 8, 8)
        x8 = jnp.where(mask_col(row + base), x_ref[pl.ds(base, 8), :].astype(F32), 0.0)
        for t in range(8):
            g = a * g + x8[t : t + 1, :]
            keep_ref[i * 8 + t + 1] = g
        return g

    lax.fori_loop(0, CTX // 8, ahead, g0)

    def back(j, carry):
        lam, sk, sv, sx, sg = carry
        i = CTX // 8 - 1 - j
        base = pl.multiple_of(first + i * 8, 8)
        at = pl.ds(pl.multiple_of(i * 8, 8), 8)
        raw = x_ref[pl.ds(base, 8), :].astype(F32)
        inside = mask_col(row + base)
        x8 = jnp.where(inside, raw, 0.0)
        k8 = gk_ref[at, :]
        v8 = gv_ref[at, :]
        outs = [None] * 8
        for t in reversed(range(8)):
            kt, vt, xt = k8[t : t + 1, :], v8[t : t + 1, :], x8[t : t + 1, :]
            lam = a * lam + km * kt + vm * vt
            now = keep_ref[i * 8 + t + 1]
            sk = sk + now * kt
            sv = sv + now * vt
            sx = sx + lam * xt
            sg = sg + lam * keep_ref[i * 8 + t]
            outs[t] = jnp.sum(lam * b, axis=0, keepdims=True)
        gx = jnp.where(inside, jnp.concatenate(outs, axis=0), 0.0)
        gx_ref[pl.ds(base, 8), :] = gx + skip_ref[0:1, :] * k8 + skip_ref[1:2, :] * v8
        return (lam, sk, sv, sx, sg)

    lam, sk, sv, sx, sg = lax.fori_loop(0, CTX // 8, back, (zero,) * 5)
    sx = sx + lam * (a * g0)
    sg = sg + lam * (a * e0)
    gp_ref[0] = sk * b
    gp_ref[1] = sv * b
    gp_ref[2] = sx
    gp_ref[3] = sg

    def tail(j, w):
        i = first // 8 - 1 - j
        base = pl.multiple_of(i * 8, 8)
        outs = [None] * 8
        for t in reversed(range(8)):
            w = a * w
            outs[t] = jnp.sum(w, axis=0, keepdims=True)
        gx_ref[pl.ds(base, 8), :] = jnp.where(
            mask_col(row + base), jnp.concatenate(outs, axis=0), 0.0
        )
        return w

    lax.fori_loop(0, first // 8, tail, lam * b)
    raw = x_ref[first:BLK, :].astype(F32)
    gs_ref[0:1, :] = jnp.sum(gk_ref[...] * raw, axis=0, keepdims=True)
    gs_ref[1:2, :] = jnp.sum(gv_ref[...] * raw, axis=0, keepdims=True)
    gx_ref[BLK:, :] = jnp.zeros((gx_ref.shape[0] - BLK, gx_ref.shape[1]), F32)


def call(kernel, outs, scratch=(), **extra):
    return pl.pallas_call(
        kernel,
        out_shape=outs,
        scratch_shapes=scratch,
        compiler_params=pltpu.CompilerParams(vmem_limit_bytes=56 << 20),
        **extra,
    )


TILE = 256


def tile_masks(seg_ref, block, tile):
    width = (tile + 1) * TILE
    segs = seg_ref[...]
    index = lax.broadcasted_iota(jnp.int32, (TILE, 1), 0) + (block * BLK + tile * TILE)
    own_id = jnp.zeros((TILE, 1), jnp.int32)
    for value in (1, 2, 3):
        below = jnp.sum(jnp.where(segs < value, 1, 0), axis=1, keepdims=True)
        own_id = own_id + jnp.where(index >= below, 1, 0)
    keys = segs[:, block * BLK : block * BLK + width]
    column = lax.broadcasted_iota(jnp.int32, (TILE, width), 1) + block * BLK
    own = (own_id == keys) & (column <= index)
    if block == 0:
        return own, None
    return own, own_id == segs[:, block * BLK - CTX : block * BLK]


def tile_scores(q, k, kc, own, ctx, scale):
    s = jnp.where(own, dot(q, k, NT) * scale, NEG)
    if ctx is None:
        return s, None
    return s, jnp.where(ctx, dot(q, kc, NT) * scale, NEG)


def attn_fwd_kernel(blocks, q_ref, k_ref, v_ref, ck_ref, cv_ref, seg_ref, o_ref, lse_ref):
    scale = HEAD**-0.5
    for block in range(blocks):
        for tile in range(BLK // TILE):
            own, ctx = tile_masks(seg_ref, block, tile)
            start, base = block * BLK + tile * TILE, block * BLK
            rows, keys = pl.ds(start, TILE), pl.ds(base, (tile + 1) * TILE)
            for head in range(q_ref.shape[1] // HEAD):
                cols = pl.ds(head * HEAD, HEAD)
                s, sc = tile_scores(
                    q_ref[rows, cols], k_ref[keys, cols], ck_ref[:, cols], own, ctx, scale
                )
                top = jnp.max(s, axis=1, keepdims=True)
                if sc is not None:
                    top = jnp.maximum(top, jnp.max(sc, axis=1, keepdims=True))
                total = jnp.sum(jnp.exp(s - top), axis=1, keepdims=True)
                if sc is not None:
                    total = total + jnp.sum(jnp.exp(sc - top), axis=1, keepdims=True)
                lse = top + jnp.log(total)
                lse_ref[head, rows, :] = lse
                out = dot(jnp.exp(s - lse).astype(BF16), v_ref[keys, cols])
                if sc is not None:
                    out = out + dot(jnp.exp(sc - lse).astype(BF16), cv_ref[:, cols])
                o_ref[rows, cols] = out.astype(BF16)


def attn_bwd_kernel(
    blocks, q_ref, k_ref, v_ref, ck_ref, cv_ref, seg_ref, lse_ref, do_ref,
    gq_ref, gk_ref, gv_ref, gck_ref, gcv_ref, ak_ref, av_ref,
):
    scale = HEAD**-0.5
    for block in range(blocks):
        base = block * BLK
        for tile in range(BLK // TILE):
            own, ctx = tile_masks(seg_ref, block, tile)
            width = (tile + 1) * TILE
            rows, keys = pl.ds(base + tile * TILE, TILE), pl.ds(base, width)
            for head in range(q_ref.shape[1] // HEAD):
                cols = pl.ds(head * HEAD, HEAD)
                q, k, v, do = q_ref[rows, cols], k_ref[keys, cols], v_ref[keys, cols], do_ref[rows, cols]
                kc, vc = ck_ref[:, cols], cv_ref[:, cols]
                s, sc = tile_scores(q, k, kc, own, ctx, scale)
                lse = lse_ref[head, rows, :]
                p = jnp.exp(s - lse)
                dp = dot(do, v, NT)
                weighted = jnp.sum(p * dp, axis=1, keepdims=True)
                if sc is not None:
                    pc = jnp.exp(sc - lse)
                    dpc = dot(do, vc, NT)
                    weighted = weighted + jnp.sum(pc * dpc, axis=1, keepdims=True)
                ds = (p * (dp - weighted)).astype(BF16)
                gq = dot(ds, k)
                gk = dot(ds, q, TN)
                gv = dot(p.astype(BF16), do, TN)
                if tile > 0:
                    half = tile * TILE
                    ak_ref[0:half, cols] = ak_ref[0:half, cols] + gk[0:half, :]
                    av_ref[0:half, cols] = av_ref[0:half, cols] + gv[0:half, :]
                    ak_ref[half:width, cols] = gk[half:width, :]
                    av_ref[half:width, cols] = gv[half:width, :]
                else:
                    ak_ref[0:width, cols] = gk
                    av_ref[0:width, cols] = gv
                if sc is not None:
                    dsc = (pc * (dpc - weighted)).astype(BF16)
                    gq = gq + dot(dsc, kc)
                    gkc = dot(dsc, q, TN) * scale
                    gvc = dot(pc.astype(BF16), do, TN)
                    if tile > 0:
                        gkc = gkc + gck_ref[:, cols]
                        gvc = gvc + gcv_ref[:, cols]
                    gck_ref[:, cols] = gkc
                    gcv_ref[:, cols] = gvc
                gq_ref[rows, cols] = (gq * scale).astype(BF16)
        gk_ref[base : base + BLK, :] = (ak_ref[...] * scale).astype(BF16)
        gv_ref[base : base + BLK, :] = av_ref[...].astype(BF16)


def normalize(values):
    centered = values - jnp.mean(values, axis=-1, keepdims=True)
    inverse = lax.rsqrt(jnp.mean(centered * centered, axis=-1, keepdims=True) + EPS)
    return centered * inverse, inverse


def norm_back(grad, hat, inverse, gain):
    u = grad * gain
    return inverse * (
        u - jnp.mean(u, axis=-1, keepdims=True) - hat * jnp.mean(u * hat, axis=-1, keepdims=True)
    )


def shards(
    tokens, cotangent, segments, w_query, w_key, w_value, w_out, w_up, up_bias, w_down, down_bias,
    norm1_gain, norm1_bias, norm2_gain, norm2_bias, decay_rates, input_mix, key_mix, value_mix,
    key_skip, value_skip,
):
    here = lax.axis_index("chan")
    own_tokens, width = tokens.shape
    length = segments.shape[1]
    own_cols = w_query.shape[1]
    shape = jax.ShapeDtypeStruct
    gather = functools.partial(lax.all_gather, axis_name="chan", axis=0, tiled=True)

    def scatter(partial):
        return lax.psum_scatter(partial.astype(BF16), "chan", scatter_dimension=0, tiled=True).astype(F32)

    def scatter_rows(partial):
        return lax.psum_scatter(partial.astype(BF16), "rows", scatter_dimension=0, tiled=True).astype(F32)

    row_tokens = gather(tokens)
    row_cot = gather(cotangent)
    full_out = lax.all_gather(w_out, "chan", axis=1, tiled=True)
    hat1, inv1 = normalize(row_tokens.astype(F32))
    hidden1 = (hat1 * norm1_gain + norm1_bias).astype(BF16)
    q, k, v = (dot(hidden1, w).astype(BF16) for w in (w_query, w_key, w_value))
    x = lax.dynamic_slice_in_dim(hidden1, here * own_cols, own_cols, 1)
    a = jnp.exp(-decay_rates)
    s = jnp.sqrt(-jnp.expm1(-2.0 * decay_rates))
    b = s * input_mix
    par = jnp.stack(
        [a, b, key_mix, value_mix, key_mix * b, value_mix * b, jnp.exp(-128.0 * decay_rates),
         128.0 * jnp.exp(-127.0 * decay_rates)]
    ).transpose(0, 2, 1)
    skip = jnp.stack([key_skip, value_skip])
    states = par.shape[1]
    ctx_k, ctx_v = call(
        ssm_fwd_kernel,
        [shape((CTX, own_cols), F32)] * 2,
        [pltpu.VMEM((CTX, own_cols), F32)],
    )(x, segments, par, skip)
    ctx_k, ctx_v = ctx_k.astype(BF16), ctx_v.astype(BF16)
    heads = own_cols // HEAD
    blocks = length // BLK
    attn, lse = call(
        functools.partial(attn_fwd_kernel, blocks),
        [shape((length, own_cols), BF16), shape((heads, length, 1), F32)],
    )(q, k, v, ctx_k, ctx_v, segments)
    row_attn = lax.all_gather(attn, "chan", axis=1, tiled=True)
    resid2 = row_tokens.astype(F32) + dot(row_attn, full_out)
    hat2, inv2 = normalize(resid2)
    hidden2 = (hat2 * norm2_gain + norm2_bias).astype(BF16)
    preact = dot(hidden2, w_up) + up_bias
    activated, gelu_back = jax.vjp(jax.nn.gelu, preact)
    act = activated.astype(BF16)
    grad_pre = gelu_back(dot(row_cot, w_down))[0].astype(BF16)
    grad_hidden2 = scatter(dot(grad_pre, w_up, NT))

    def own(values):
        return lax.dynamic_slice_in_dim(values, here * own_tokens, own_tokens, 0)

    own_hat2, own_inv2 = own(hat2), own(inv2)
    grad_resid2 = cotangent.astype(F32) + norm_back(grad_hidden2, own_hat2, own_inv2, norm2_gain)
    row_branch = gather(grad_resid2.astype(BF16))
    ffn = scatter(dot(act, w_down, NT))
    output = (own(resid2) + ffn + down_bias).astype(BF16)
    grad_up = scatter_rows(dot(hidden2, grad_pre, TN))
    grad_down = scatter_rows(dot(row_cot, act, TN))
    out_rows = lax.dynamic_slice_in_dim(full_out, here * own_cols, own_cols, 0)
    grad_attn = dot(row_branch, out_rows, NT).astype(BF16)
    grad_q, grad_k, grad_v, grad_ck, grad_cv = call(
        functools.partial(attn_bwd_kernel, blocks),
        [shape((length, own_cols), BF16)] * 3 + [shape((CTX, own_cols), F32)] * 2,
        [pltpu.VMEM((BLK, own_cols), F32)] * 2,
    )(q, k, v, ctx_k, ctx_v, segments, lse, grad_attn)
    grad_x, grad_par, grad_skip = call(
        ssm_bwd_kernel,
        [shape((length, own_cols), F32), shape((4, states, own_cols), F32), shape((2, own_cols), F32)],
        [pltpu.VMEM((CTX + 1, states, own_cols), F32)],
    )(x, segments, par, skip, grad_ck, grad_cv)
    partial1 = dot(grad_q, w_query, NT) + dot(grad_k, w_key, NT) + dot(grad_v, w_value, NT)
    place = lax.dynamic_update_slice_in_dim(
        jnp.zeros((length, width), F32), grad_x.astype(BF16).astype(F32), here * own_cols, 1
    )
    grad_hidden1 = scatter(partial1 + place)
    own_hat1, own_inv1 = own(hat1), own(inv1)
    grad_tokens = (grad_resid2 + norm_back(grad_hidden1, own_hat1, own_inv1, norm1_gain)).astype(BF16)
    branch_cols = lax.dynamic_slice_in_dim(row_branch, here * own_cols, own_cols, 1)
    grad_out = scatter_rows(dot(row_attn, branch_cols, TN))
    grad_qkv = scatter_rows(
        jnp.concatenate([dot(hidden1, g, TN) for g in (grad_q, grad_k, grad_v)], axis=1)
    )
    sk, sv, sx, sg = (grad_par[i].T for i in range(4))
    grad_in = s * sx
    grad_dec = (a * a / s) * input_mix * sx - a * b * sg
    grad_up_bias = jnp.sum(grad_pre.astype(F32), axis=0)
    mine = jnp.concatenate(
        [t.reshape(-1) for t in (grad_dec, grad_in, sk, sv, grad_skip[0], grad_skip[1], grad_up_bias)]
    )
    mine = lax.all_gather(lax.psum(mine, "rows"), "chan", axis=0)
    size = own_cols * states
    pieces = [mine[:, i * size : (i + 1) * size].reshape(width, states) for i in range(4)]
    rest = mine[:, 4 * size :]
    skips = [rest[:, i * own_cols : (i + 1) * own_cols].reshape(width) for i in range(2)]
    up_bias_grad = rest[:, 2 * own_cols :].reshape(-1)
    shared = lax.psum(
        jnp.stack(
            [
                jnp.sum(grad_hidden1 * own_hat1, axis=0),
                jnp.sum(grad_hidden1, axis=0),
                jnp.sum(grad_hidden2 * own_hat2, axis=0),
                jnp.sum(grad_hidden2, axis=0),
                jnp.sum(cotangent.astype(F32), axis=0),
            ]
        ),
        ("rows", "chan"),
    )
    return (
        output, grad_tokens,
        grad_qkv[:, :own_cols], grad_qkv[:, own_cols : 2 * own_cols], grad_qkv[:, 2 * own_cols :],
        grad_out, grad_up, up_bias_grad, grad_down,
        shared[4], shared[0], shared[1], shared[2], shared[3],
        pieces[0], pieces[1], pieces[2], pieces[3], skips[0], skips[1],
    )


def solution(mesh):
    both, row, col = P(("rows", "chan"), None), P("rows", None), P(None, "chan")
    state = P("chan", None)
    in_specs = (
        both, both, row, col, col, col, col, col, P("chan"), col,
        P(), P(), P(), P(), P(), state, state, state, state, P("chan"), P("chan"),
    )
    grid = P("rows", "chan")
    out_specs = (both, both, grid, grid, grid, grid, grid, P(), grid) + (P(),) * 11
    return jax.shard_map(shards, mesh=mesh, in_specs=in_specs, out_specs=out_specs, check_vma=False)
```

time: 1830 us -> 653 us (0.36)
  other arithmetic: 739 us -> 36.1 us
  waiting for transfers between devices: 738 us -> 424 us
  local copies, waits for them, and re-layouts: 154 us -> 39.3 us
  blocking collectives: 75.4 us -> 45.5 us
  starting transfers between devices: 28 us -> 1.69 us
  Pallas kernels: 0 us -> 24.5 us
    another operation x61 -> x2, other arithmetic: 461 us -> 2.01 us  [the longest x1 1.28 us: shards(): skip = jnp.stack([key_skip, value_skip])]
    reduce_scatter x7 -> x5, waiting for transfers between devices: 611 us -> 205 us  [the longest x2 115 us: scatter_rows(): lax.psum_scatter(partial.astype(BF16), 'rows', scatter_dimension=0, tiled...]
    scatter-add x4 -> x0, other arithmetic: 149 us -> none  [ssm_block(): before = jnp.take(running, jnp.maximum(last_start - 1, 0), axis=0)]
    unnamed x16 -> x15, waiting for transfers between devices: 3.3 us -> 98.1 us
    reduce_sum x21 -> x6, other arithmetic: 73.1 us -> 11.7 us  [the longest x1 3.17 us: shards(): jnp.sum(cotangent.astype(F32), axis=0)]
    psum x1, waiting for transfers between devices: 11.3 us -> 70 us  [shards(): mine = lax.all_gather(lax.psum(mine, 'rows'), 'chan', axis=0)]
    all_gather x6 -> x5, waiting for transfers between devices: 99.2 us -> 51.3 us  [the longest x1 21.9 us: shards(): row_attn = lax.all_gather(attn, 'chan', axis=1, tiled=True)]
    gather x8 -> x0, local copies, waits for them, and re-layouts: 40.2 us -> none  [ssm_block(): before = jnp.take(running, jnp.maximum(last_start - 1, 0), axis=0)]
  transfers between devices with their start and end apart: 22 -> 13, of which waited for: 15 -> 11; matrix products, arithmetic and copies ran while one was open for 50% -> 17% of each run, Pallas kernels for 0% -> 4%
where the time goes in v1:
time: 653 us; the launch traced here: 645 us
  waiting for transfers between devices  424 us (65%)
  matrix products  59.5 us (9%)
  blocking collectives  45.5 us (7%)
  local copies, waits for them, and re-layouts  39.3 us (6%)
  other arithmetic  36.1 us (6%)
  Pallas kernels  24.5 us (4%)
  between operations  14.8 us (2%)
    reduce_scatter x2, waiting for transfers between devices, scatter_rows(): lax.psum_scatter(partial.astype(BF16), 'rows', scatter_dimension=0, tiled...  115 us
    unnamed x15, waiting for transfers between devices  98.1 us
    reduce_scatter x3, waiting for transfers between devices, scatter(): lax.psum_scatter(partial.astype(BF16), 'chan', scatter_dimension=0, tiled...  89.9 us
    psum x1, waiting for transfers between devices, shards(): mine = lax.all_gather(lax.psum(mine, 'rows'), 'chan', axis=0)  70 us
    dot_general x18, matrix products, dot(): return lax.dot_general(left, right, dims, preferred_element_type=F32)  59.5 us
    psum x1, blocking collectives, shards(): lax.psum(jnp.stack([jnp.sum(grad_hidden1 * own_hat1, axis=0), jnp.sum(gra...  39.5 us
    unnamed x90, local copies, waits for them, and re-layouts  29.6 us
    all_gather x1, waiting for transfers between devices, shards(): row_attn = lax.all_gather(attn, 'chan', axis=1, tiled=True)  21.9 us
  transfers between devices with their start and end apart: 13, of which 11 were waited for; matrix products, arithmetic and copies ran while one was open for 17% of the time, Pallas kernels for 4%

profile of v1, /device:TPU:0, one launch (start us, length us, event | category | flops | bytes accessed | tf_op | source)
XLA Modules:
  0.0 645.5 jit_solution(15312406948602481746)
XLA Ops:
  16.0 18.9 %all-gather.7.cloned.1.call-done = bf16[1024,1024]{1,0:T(8,128)(2,1)} async-done(((bf16[256,1024]{1,0:T(8,128)(2,1)}), bf16[1024,1024]{1,0:T(8,128)(2,1)}) %all-gather.7.cloned.1.call-update) | async-done | bytes 2097168 | tf_op jit(solution)/shard_map/all_gather | solution.py:321
  34.9 2.1 convert_reduce_fusion
  37.0 2.3 fusion.2
  39.4 2.8 fusion
  43.0 4.0 shard_map.356
  47.0 1.5 convert_element_type.104.ck_ref
  54.6 6.1 shard_map.357
  61.9 21.9 %all-gather.9.cloned.1.call-done = bf16[1024,1024]{1,0:T(8,128)(2,1)} async-done(((bf16[1024,256]{1,0:T(8,128)(2,1)}), bf16[1024,1024]{1,0:T(8,128)(2,1)}) %all-gather.9.cloned.1.call-update) | async-done | bytes 2097168 | tf_op jit(solution)/shard_map/all_gather | solution.py:349
  83.8 5.3 fusion.39
  91.1 2.0 copy-done.3
  93.1 4.3 fusion.26
  97.4 10.4 %all-gather.13.cloned.1.call-done = bf16[1024,1024]{1,0:T(8,128)(2,1)} async-done(((bf16[256,1024]{1,0:T(8,128)(2,1)}), bf16[1024,1024]{1,0:T(8,128)(2,1)}) %all-gather.13.cloned.1.call-update) | async-done | bytes 2097168 | tf_op jit(solution)/shard_map/all_gather | solution.py:322
  107.8 7.4 %convert_reduce_fusion.1 = (f32[1024]{0:T(1024)S(1)}, bf16[1024,1024]{1,0:T(8,128)(2,1)S(1)}) fusion(f32[1024,1024]{1,0:T(8,128)} %fusion.26, f32[1024]{0:T(1024)S(1)} %copy-done.30, bf16[1024,1024]{1,0:T(8,128)(2,1)} %all-gather.13.cloned.1.call-done, bf16[1024,1024]{1,0:T(8,128)(2,1)S(1)} %copy-done), kind=kOutput, calls=%fused_computation.15 | convolution fusion | flops 2171599872 | bytes 10493952 | tf_op jit(solution)/shard_map/dot_general | solution.py:23
  116.6 3.7 convolution_convert_fusion.1
  120.4 31.4 %reduce-scatter.14.cloned.1.call-done = bf16[256,1024]{1,0:T(8,128)(2,1)} async-done(((bf16[1024,1024]{1,0:T(8,128)(2,1)}), bf16[256,1024]{1,0:T(8,128)(2,1)}) %reduce-scatter.14.cloned.1.call-update) | async-done | bytes 524304 | tf_op jit(solution)/shard_map/reduce_scatter | solution.py:316
  151.9 1.8 fusion.24
  153.7 2.5 fusion.33
  156.5 7.2 %convert_bitcast_fusion = bf16[1024,1024]{0,1:T(8,128)(2,1)} fusion(bf16[1024,1024]{1,0:T(8,128)(2,1)} %all-gather.13.cloned.1.call-done, f32[1024,1024]{1,0:T(8,128)} %fusion.26, f32[1024]{0:T(1024)S(1)} %copy-done.30), kind=kOutput, calls=%fused_computation.22 | convolution fusion | flops 2159017984 | bytes 8392704 | tf_op jit(solution)/shard_map/dot_general | solution.py:23
  163.7 4.2 copy.75
  168.0 6.7 %convolution_convert_fusion = bf16[1024,1024]{1,0:T(8,128)(2,1)} fusion(bf16[1024,1024]{1,0:T(8,128)(2,1)} %copy-done.31, f32[1024,1024]{1,0:T(8,128)} %copy-done.3, f32[1024]{0:T(1024)S(1)} %copy-done.29, f32[1024]{0:T(1024)S(1)} %copy-done.24), kind=kOutput, calls=%fused_computation.23 | convolution fusion | flops 2151677952 | bytes 8396800 | tf_op jit(solution)/shard_map/dot_general | solution.py:23
  174.7 6.4 convolution_convert_fusion.2
  181.4 3.2 convolution_convert_fusion.7.do_ref
  184.6 7.8 %shard_map.358 = (bf16[1024,256]{1,0:T(8,128)(2,1)}, bf16[1024,256]{1,0:T(8,128)(2,1)}, bf16[1024,256]{1,0:T(8,128)(2,1)}, f32[128,256]{1,0:T(8,128)}, f32[128,256]{1,0:T(8,128)}) custom-call(bf16[1024,256]{1,0:T(8,128)(2,1)} %convolution_convert_fusion.10.q_ref, bf16[1024,256]{1,0:T(8,128)(2,1)} %convolution_convert_fusion.9.k_ref, ...), custom_call_target="tpu_custom_call" | custom-call | tf_op jit(solution)/shard_map/pallas_call | solution.py:371
  192.5 6.6 %shard_map.359 = (f32[1024,256]{1,0:T(8,128)}, f32[4,16,256]{2,1,0:T(8,128)}, f32[2,256]{1,0:T(2,128)}) custom-call(bf16[1024,256]{1,0:T(8,128)(2,1)} %constant_dynamic-slice_fusion.x_ref, s32[1,1024]{1,0:T(1,128)} %seg_ref.7, f32[8,16,256]{2,1,0:T(8,128)} %bitcast.105, f32[2,256]{1,0:T(2,128)} %pad_maximum_fusion.1.skip_ref, ...), custom_call_target="tpu_custom_call" | custom-call | tf_op jit(solution)/shard_map/pallas_call | solution.py:376
  203.1 3.3 convolution_convert_fusion.3
  206.5 2.5 convolution_convert_fusion.6
  211.9 2.6 copy.73
  214.9 1.9 fusion.41
  219.1 1.7 convert_element_type.119
  220.9 29.9 %reduce-scatter.24.cloned.1.call-done = bf16[128,1024]{1,0:T(8,128)(2,1)} async-done(((bf16[1024,1024]{1,0:T(8,128)(2,1)}), bf16[128,1024]{1,0:T(8,128)(2,1)}) %reduce-scatter.24.cloned.1.call-update) | async-done | bytes 262160
  252.9 68.7 %reduce-scatter.20.cloned.1.call-done = bf16[128,1024]{1,0:T(8,128)(2,1)} async-done(((bf16[1024,1024]{1,0:T(8,128)(2,1)}), bf16[128,1024]{1,0:T(8,128)(2,1)}) %reduce-scatter.20.cloned.1.call-update) | async-done | bytes 262160 | tf_op jit(solution)/shard_map/reduce_scatter | solution.py:319
  321.6 1.8 convert_element_type.126
  323.4 31.4 %reduce-scatter.12.cloned.1.call-done = bf16[256,1024]{1,0:T(8,128)(2,1)} async-done(((bf16[1024,1024]{1,0:T(8,128)(2,1)}), bf16[256,1024]{1,0:T(8,128)(2,1)}) %reduce-scatter.12.cloned.1.call-update) | async-done | bytes 524304 | tf_op jit(solution)/shard_map/reduce_scatter | solution.py:316
  354.8 2.3 add_convert_fusion.2
  357.1 70.0 %all-reduce.2.cloned.1.call-done = f32[1,17920]{1,0:T(1,128)} async-done(((f32[1,17920]{1,0:T(1,128)}), f32[1,17920]{1,0:T(1,128)}) %all-reduce.2.cloned.1.call-update) | async-done | bytes 71696 | tf_op jit(solution)/shard_map/psum | solution.py:400
  427.1 6.1 all-gather
  436.2 1.8 copy.71
  439.1 1.8 copy.70
  442.0 1.8 copy.69
  444.9 1.8 copy.68
  446.8 46.2 %reduce-scatter.18.cloned.1.call-done = bf16[128,256]{1,0:T(8,128)(2,1)} async-done(((bf16[1024,256]{1,0:T(8,128)(2,1)}), bf16[128,256]{1,0:T(8,128)(2,1)}) %reduce-scatter.18.cloned.1.call-update) | async-done | bytes 65552 | tf_op jit(solution)/shard_map/reduce_scatter | solution.py:319
  494.5 66.1 %reduce-scatter.22.cloned.1.call-done = bf16[128,768]{1,0:T(8,128)(2,1)} async-done(((bf16[1024,768]{1,0:T(8,128)(2,1)}), bf16[128,768]{1,0:T(8,128)(2,1)}) %reduce-scatter.22.cloned.1.call-update) | async-done | bytes 196624
  562.4 1.7 copy.66
  564.1 1.7 copy.65
  566.5 27.0 %reduce-scatter.16.cloned.1.call-done = bf16[256,1024]{1,0:T(8,128)(2,1)} async-done(((bf16[1024,1024]{1,0:T(8,128)(2,1)}), bf16[256,1024]{1,0:T(8,128)(2,1)}) %reduce-scatter.16.cloned.1.call-update) | async-done | bytes 524304 | tf_op jit(solution)/shard_map/reduce_scatter | solution.py:316
  593.5 1.8 fusion.25
  595.4 3.2 convert_reduce_fusion.4
  598.6 39.5 %psum.15 = f32[5,1024]{1,0:T(8,128)S(1)} all-reduce(f32[5,1024]{1,0:T(8,128)S(1)} %stack.71), channel_id=1, replica_groups=mesh['rows'=8,'chan'=4] {'rows','chan'}, use_global_device_ids=true, to_apply=%region_22.0 | all-reduce | flops 5120 | bytes 40960 | tf_op jit(solution)/shard_map/psum | solution.py:406
  (160 shorter events, 43.2 us)
Async XLA Ops:
  7.2 100.7 %copy-start = (bf16[1024,1024]{1,0:T(8,128)(2,1)S(1)}, bf16[1024,1024]{1,0:T(8,128)(2,1)}, u32[]{:S(2)}) copy-start(bf16[1024,1024]{1,0:T(8,128)(2,1)} %param.30) | copy-start | bytes 6291460
  7.2 32.1 %copy-start.23 = (f32[1024]{0:T(1024)S(1)}, f32[1024]{0:T(1024)}, u32[]{:S(2)}) copy-start(f32[1024]{0:T(1024)} %param.32) | copy-start | bytes 12292
  7.2 32.1 %copy-start.25 = (f32[1024]{0:T(1024)S(1)}, f32[1024]{0:T(1024)}, u32[]{:S(2)}) copy-start(f32[1024]{0:T(1024)} %param.33) | copy-start | bytes 12292
  7.2 27.7 %all-gather.7.cloned.1.call-start = ((), (), s32[]{:S(2)}) async-start(), calls=%async_computation.7 | async-start | bytes 2621440 | tf_op jit(solution)/shard_map/all_gather | solution.py:321
  8.0 53.9 %all-gather.11.cloned.1.call-start = ((), (), s32[]{:S(2)}) async-start(), calls=%async_computation.9 | async-start | bytes 2621440 | tf_op jit(solution)/shard_map/all_gather | solution.py:323
  8.7 75.1 %all-gather.9.cloned.1.call-start = ((), (), s32[]{:S(2)}) async-start(), calls=%async_computation.8 | async-start | bytes 2621440 | tf_op jit(solution)/shard_map/all_gather | solution.py:349
  16.0 26.2 %copy-start.10 = (f32[8,256,16]{1,2,0:T(8,128)}, f32[8,256,16]{1,2,0:T(8,128)S(1)}, u32[]{:S(2)}) copy-start(f32[8,256,16]{1,2,0:T(8,128)S(1)} %constant_dynamic-update-slice_fusion) | copy-start | bytes 393220
  34.9 4.4 copy-start.2
  39.4 10.7 %copy-start.18 = (bf16[1024,256]{1,0:T(8,128)(2,1)S(1)}, bf16[1024,256]{1,0:T(8,128)(2,1)}, u32[]{:S(2)}) copy-start(bf16[1024,256]{1,0:T(8,128)(2,1)} %param.26) | copy-start | bytes 1572868
  42.2 10.9 %copy-start.6 = (bf16[1024,1024]{1,0:T(8,128)(2,1)}, bf16[1024,1024]{1,0:T(8,128)(2,1)S(1)}, u32[]{:S(2)}) copy-start(bf16[1024,1024]{1,0:T(8,128)(2,1)S(1)} %get-tuple-element.115) | copy-start | bytes 6291460
  42.2 9.4 %copy-start.11 = (bf16[1024,256]{1,0:T(8,128)(2,1)S(1)}, bf16[1024,256]{1,0:T(8,128)(2,1)}, u32[]{:S(2)}) copy-start(bf16[1024,256]{1,0:T(8,128)(2,1)} %param.25) | copy-start | bytes 1572868
  51.6 1.5 copy-start.13
  60.7 47.1 %all-gather.13.cloned.1.call-start = ((), (), s32[]{:S(2)}) async-start(), calls=%async_computation.11 | async-start | bytes 2621440 | tf_op jit(solution)/shard_map/all_gather | solution.py:322
  61.3 90.6 %reduce-scatter.14.cloned.1.call-start = ((), (), s32[]{:S(2)}) async-start(), calls=%async_computation.12 | async-start | bytes 2621440 | tf_op jit(solution)/shard_map/reduce_scatter | solution.py:316
  89.1 2.0 copy-start.1
  89.7 3.4 copy-start.24
  89.7 3.4 copy-start.27
  89.7 3.4 copy-start.29
  91.1 2.0 copy-start.3
  93.1 14.7 %copy-start.30 = (f32[1024]{0:T(1024)S(1)}, f32[1024]{0:T(1024)}, u32[]{:S(2)}) copy-start(f32[1024]{0:T(1024)} %param.29) | copy-start | bytes 12292
  107.8 8.7 %copy-start.28 = (bf16[1024,1024]{1,0:T(8,128)(2,1)S(1)}, bf16[1024,1024]{1,0:T(8,128)(2,1)}, u32[]{:S(2)}) copy-start(bf16[1024,1024]{1,0:T(8,128)(2,1)} %param.28) | copy-start | bytes 6291460
  115.3 1.3 copy-start.31
  116.6 37.1 %copy-start.5 = (bf16[256,1024]{1,0:T(8,128)(2,1)S(1)}, bf16[256,1024]{1,0:T(8,128)(2,1)}, u32[]{:S(2)}) copy-start(bf16[256,1024]{1,0:T(8,128)(2,1)} %param.22) | copy-start | bytes 1572868
  120.3 61.1 %all-gather.15.cloned.1.call-start = ((), (), s32[]{:S(2)}) async-start(), calls=%async_computation.13 | async-start | bytes 2621440 | tf_op jit(solution)/shard_map/all_gather | solution.py:364
  156.3 94.6 %reduce-scatter.24.cloned.1.call-start = ((), (), s32[]{:S(2)}) async-start(), calls=%async_computation.19 | async-start | bytes 2359296
  167.9 153.7 %reduce-scatter.20.cloned.1.call-start = ((), (), s32[]{:S(2)}) async-start(), calls=%async_computation.16 | async-start | bytes 2359296 | tf_op jit(solution)/shard_map/reduce_scatter | solution.py:319
  174.7 180.1 %reduce-scatter.12.cloned.1.call-start = ((), (), s32[]{:S(2)}) async-start(), calls=%async_computation.10 | async-start | bytes 2621440 | tf_op jit(solution)/shard_map/reduce_scatter | solution.py:316
  181.1 19.0 %copy-start.9 = (f32[256,16]{0,1:T(8,128)S(1)}, f32[256,16]{0,1:T(8,128)}, u32[]{:S(2)}) copy-start(f32[256,16]{0,1:T(8,128)} %param.36) | copy-start | bytes 49156
  181.1 19.0 %copy-start.22 = (f32[256,16]{0,1:T(8,128)S(1)}, f32[256,16]{0,1:T(8,128)}, u32[]{:S(2)}) copy-start(f32[256,16]{0,1:T(8,128)} %param.37) | copy-start | bytes 49156
  181.1 246.0 %all-reduce.2.cloned.1.call-start = ((), (), s32[]{:S(2)}) async-start(), calls=%async_computation.17 | async-start | bytes 143360 | tf_op jit(solution)/shard_map/psum | solution.py:400
  201.0 5.5 copy-start.15
  203.0 290.0 %reduce-scatter.18.cloned.1.call-start = ((), (), s32[]{:S(2)}) async-start(), calls=%async_computation.15 | async-start | bytes 589824 | tf_op jit(solution)/shard_map/reduce_scatter | solution.py:319
  206.4 354.2 %reduce-scatter.22.cloned.1.call-start = ((), (), s32[]{:S(2)}) async-start(), calls=%async_computation.18 | async-start | bytes 1769472
  206.5 2.5 copy-start.7
  206.5 2.5 copy-start.17
  206.5 3.3 copy-start.20
  210.6 4.3 copy-start.12
  214.5 379.0 %reduce-scatter.16.cloned.1.call-start = ((), (), s32[]{:S(2)}) async-start(), calls=%async_computation.14 | async-start | bytes 2621440 | tf_op jit(solution)/shard_map/reduce_scatter | solution.py:316
  214.9 2.0 copy-start.14
  214.9 2.0 copy-start.16
  214.9 2.7 copy-start.19
  214.9 2.7 copy-start.21
  217.6 1.2 copy-start.8
  219.1 135.7 %copy-start.26 = (f32[1024]{0:T(1024)S(1)}, f32[1024]{0:T(1024)}, u32[]{:S(2)}) copy-start(f32[1024]{0:T(1024)} %param.31) | copy-start | bytes 12292
  435.1 160.3 %copy-start.4 = (bf16[256,1024]{1,0:T(8,128)(2,1)S(1)}, bf16[256,1024]{1,0:T(8,128)(2,1)}, u32[]{:S(2)}) copy-start(bf16[256,1024]{1,0:T(8,128)(2,1)} %reduce-scatter.14.cloned.1.call-done) | copy-start | bytes 1572868
Sparse Core Ops, SparseCore 0:
  9.6 25.2 all-gather.6
  36.5 22.8 all-gather.10
  60.9 22.8 all-gather.8
  85.2 22.5 all-gather.12
  120.4 31.4 reduce-scatter.13
  156.4 22.5 all-gather.14
  182.9 67.8 reduce-scatter.23
  254.8 66.7 reduce-scatter.19
  324.3 30.4 reduce-scatter.11
  358.6 68.4 all-reduce.1
  431.1 61.8 reduce-scatter.17
  496.6 63.9 reduce-scatter.21
  563.1 30.3 reduce-scatter.15

commit v2 on v1

v2 whole, which is shorter than its diff:
```python
import functools
import math

import jax
import jax.numpy as jnp
from jax import lax
from jax.experimental import pallas as pl
from jax.experimental.pallas import tpu as pltpu
from jax.sharding import PartitionSpec as P

HEAD = 128
CTX = 128
BLK = 512
TILE = 256
EPS = 1e-05
NEG = -1e30
F32 = jnp.float32
BF16 = jnp.bfloat16
NN = (((1,), (0,)), ((), ()))
NT = (((1,), (1,)), ((), ()))
TN = (((0,), (0,)), ((), ()))
ROOT = math.sqrt(2.0 / math.pi)
MESH = pl.DeviceIdType.MESH


def dot(left, right, dims=NN):
    return lax.dot_general(left, right, dims, preferred_element_type=F32)


def at(start, size):
    if isinstance(start, int):
        return pl.ds(start, size)
    return pl.ds(pl.multiple_of(start, math.gcd(size, 1024)), size)


def ssm_params(rate_ref, in_ref, key_ref, value_ref):
    rate = rate_ref[...].T
    a = jnp.exp(-rate)
    s = jnp.sqrt(1.0 - a * a)
    return dict(rate=rate, a=a, s=s, mix=in_ref[...].T, km=key_ref[...].T, vm=value_ref[...].T)


def ssm_forward(x_ref, seg_ref, par, skip_k, skip_v, ck_ref, cv_ref, wide_k, wide_v, keep_ref):
    a, rate = par["a"], par["rate"]
    b = par["s"] * par["mix"]
    kb, vb = par["km"] * b, par["vm"] * b
    a128, d128 = jnp.exp(-128.0 * rate), 128.0 * jnp.exp(-127.0 * rate)
    first = BLK - CTX
    parts = first // 128
    mask = segment_mask(seg_ref)
    row = lax.broadcasted_iota(jnp.int32, (8, 1), 0)
    zero = jnp.zeros(a.shape, F32)

    def step(i, carry):
        out = []
        for j in range(parts):
            g, e = carry[j]
            base = pl.multiple_of(j * 128 + i * 8, 8)
            x8 = jnp.where(mask(row + base), x_ref[pl.ds(base, 8), :], 0.0)
            for t in range(8):
                e = a * e + g
                g = a * g + x8[t : t + 1, :]
            out.append((g, e))
        return tuple(out)

    ends = lax.fori_loop(0, 16, step, tuple((zero, zero) for _ in range(parts)))
    g, e = ends[0]
    for j in range(1, parts):
        e = ends[j][1] + a128 * e + d128 * g
        g = ends[j][0] + a128 * g
    keep_ref[0] = g

    def ahead(i, g):
        base = pl.multiple_of(first + i * 8, 8)
        raw = x_ref[pl.ds(base, 8), :]
        x8 = jnp.where(mask(row + base), raw, 0.0)
        ks, vs = [], []
        for t in range(8):
            g = a * g + x8[t : t + 1, :]
            keep_ref[i * 8 + t + 1] = g
            ks.append(jnp.sum(g * kb, axis=0, keepdims=True))
            vs.append(jnp.sum(g * vb, axis=0, keepdims=True))
        rows = pl.ds(pl.multiple_of(i * 8, 8), 8)
        wide_k[rows, :] = jnp.concatenate(ks, axis=0) + skip_k * raw
        wide_v[rows, :] = jnp.concatenate(vs, axis=0) + skip_v * raw
        return g

    lax.fori_loop(0, CTX // 8, ahead, g)
    ck_ref[...] = wide_k[...].astype(BF16)
    cv_ref[...] = wide_v[...].astype(BF16)
    return e


def segment_mask(seg_ref):
    segs = seg_ref[...]
    first = jnp.sum(jnp.where(segs < segs[:, BLK : BLK + 1], 1, 0), axis=1, keepdims=True)
    return lambda index: index >= first


def ssm_backward(x_ref, seg_ref, par, skip_k, skip_v, gk_ref, gv_ref, keep_ref, e0, gx_ref, small_ref):
    a, s, km, vm = par["a"], par["s"], par["km"], par["vm"]
    b = s * par["mix"]
    first = BLK - CTX
    mask = segment_mask(seg_ref)
    row = lax.broadcasted_iota(jnp.int32, (8, 1), 0)
    zero = jnp.zeros(a.shape, F32)

    def back(j, carry):
        lam, sk, sv, sx, sg = carry
        i = CTX // 8 - 1 - j
        base = pl.multiple_of(first + i * 8, 8)
        rows = pl.ds(pl.multiple_of(i * 8, 8), 8)
        inside = mask(row + base)
        x8 = jnp.where(inside, x_ref[pl.ds(base, 8), :], 0.0)
        k8, v8 = gk_ref[rows, :], gv_ref[rows, :]
        outs = [None] * 8
        for t in reversed(range(8)):
            kt, vt = k8[t : t + 1, :], v8[t : t + 1, :]
            lam = a * lam + km * kt + vm * vt
            now = keep_ref[i * 8 + t + 1]
            sk = sk + now * kt
            sv = sv + now * vt
            sx = sx + lam * x8[t : t + 1, :]
            sg = sg + lam * keep_ref[i * 8 + t]
            outs[t] = jnp.sum(lam * b, axis=0, keepdims=True)
        gx = jnp.where(inside, jnp.concatenate(outs, axis=0), 0.0)
        gx_ref[pl.ds(base, 8), :] = gx + skip_k * k8 + skip_v * v8
        return (lam, sk, sv, sx, sg)

    lam, sk, sv, sx, sg = lax.fori_loop(0, CTX // 8, back, (zero,) * 5)
    sx = sx + lam * (a * keep_ref[0])
    sg = sg + lam * (a * e0)
    ns = a.shape[0]
    small_ref[0:ns, :] = (a * a / s) * par["mix"] * sx - a * b * sg
    small_ref[ns : 2 * ns, :] = s * sx
    small_ref[2 * ns : 3 * ns, :] = sk * b
    small_ref[3 * ns : 4 * ns, :] = sv * b

    def tail(j, w):
        base = pl.multiple_of(first - 8 - j * 8, 8)
        outs = [None] * 8
        for t in reversed(range(8)):
            w = a * w
            outs[t] = jnp.sum(w, axis=0, keepdims=True)
        gx_ref[pl.ds(base, 8), :] = jnp.where(mask(row + base), jnp.concatenate(outs, axis=0), 0.0)
        return w

    lax.fori_loop(0, first // 8, tail, lam * b)
    raw = x_ref[first:BLK, :]
    small_ref[4 * ns : 4 * ns + 1, :] = jnp.sum(gk_ref[...] * raw, axis=0, keepdims=True)
    small_ref[4 * ns + 1 : 4 * ns + 2, :] = jnp.sum(gv_ref[...] * raw, axis=0, keepdims=True)


def tile_masks(seg_ref, block, tile):
    width = (tile + 1) * TILE
    segs = seg_ref[...]
    index = lax.broadcasted_iota(jnp.int32, (TILE, 1), 0) + (block * BLK + tile * TILE)
    own_id = jnp.zeros((TILE, 1), jnp.int32)
    for value in (1, 2, 3):
        below = jnp.sum(jnp.where(segs < value, 1, 0), axis=1, keepdims=True)
        own_id = own_id + jnp.where(index >= below, 1, 0)
    keys = segs[:, block * BLK : block * BLK + width]
    column = lax.broadcasted_iota(jnp.int32, (TILE, width), 1) + block * BLK
    own = (own_id == keys) & (column <= index)
    if block == 0:
        return own, None
    return own, own_id == segs[:, block * BLK - CTX : block * BLK]


def attn_forward(block, q_ref, k_ref, v_ref, ck_ref, cv_ref, seg_ref, store, lse_ref):
    scale = HEAD**-0.5
    for tile in range(BLK // TILE):
        own, ctx = tile_masks(seg_ref, block, tile)
        rows = pl.ds(block * BLK + tile * TILE, TILE)
        keys = pl.ds(block * BLK, (tile + 1) * TILE)
        for head in range(q_ref.shape[1] // HEAD):
            cols = pl.ds(head * HEAD, HEAD)
            q = q_ref[rows, cols]
            s = jnp.where(own, dot(q, k_ref[keys, cols], NT) * scale, NEG)
            top = jnp.max(s, axis=1, keepdims=True)
            if ctx is not None:
                sc = jnp.where(ctx, dot(q, ck_ref[:, cols], NT) * scale, NEG)
                top = jnp.maximum(top, jnp.max(sc, axis=1, keepdims=True))
            p = jnp.exp(s - top)
            total = jnp.sum(p, axis=1, keepdims=True)
            if ctx is not None:
                pc = jnp.exp(sc - top)
                total = total + jnp.sum(pc, axis=1, keepdims=True)
            lse_ref[head, rows, :] = top + jnp.log(total)
            inverse = 1.0 / total
            out = dot((p * inverse).astype(BF16), v_ref[keys, cols])
            if ctx is not None:
                out = out + dot((pc * inverse).astype(BF16), cv_ref[:, cols])
            store(rows, head, out.astype(BF16))


def attn_backward(
    block, q_ref, k_ref, v_ref, ck_ref, cv_ref, seg_ref, lse_ref, do_ref,
    gq_ref, gk_ref, gv_ref, gck_ref, gcv_ref, ak_ref, av_ref,
):
    scale = HEAD**-0.5
    base = block * BLK
    for tile in range(BLK // TILE):
        own, ctx = tile_masks(seg_ref, block, tile)
        width = (tile + 1) * TILE
        rows, keys = pl.ds(base + tile * TILE, TILE), pl.ds(base, width)
        for head in range(q_ref.shape[1] // HEAD):
            cols = pl.ds(head * HEAD, HEAD)
            q, k, v = q_ref[rows, cols], k_ref[keys, cols], v_ref[keys, cols]
            do = do_ref[tile * TILE : (tile + 1) * TILE, cols]
            lse = lse_ref[head, rows, :]
            p = jnp.exp(jnp.where(own, dot(q, k, NT) * scale, NEG) - lse)
            dp = dot(do, v, NT)
            weighted = jnp.sum(p * dp, axis=1, keepdims=True)
            if ctx is not None:
                kc, vc = ck_ref[:, cols], cv_ref[:, cols]
                pc = jnp.exp(jnp.where(ctx, dot(q, kc, NT) * scale, NEG) - lse)
                dpc = dot(do, vc, NT)
                weighted = weighted + jnp.sum(pc * dpc, axis=1, keepdims=True)
            ds = (p * (dp - weighted)).astype(BF16)
            gq = dot(ds, k)
            gk = dot(ds, q, TN)
            gv = dot(p.astype(BF16), do, TN)
            half = tile * TILE
            if tile > 0:
                ak_ref[0:half, cols] = ak_ref[0:half, cols] + gk[0:half, :]
                av_ref[0:half, cols] = av_ref[0:half, cols] + gv[0:half, :]
            ak_ref[half:width, cols] = gk[half:width, :]
            av_ref[half:width, cols] = gv[half:width, :]
            if ctx is not None:
                dsc = (pc * (dpc - weighted)).astype(BF16)
                gq = gq + dot(dsc, kc)
                gkc = dot(dsc, q, TN) * scale
                gvc = dot(pc.astype(BF16), do, TN)
                if tile > 0:
                    gkc = gkc + gck_ref[:, cols]
                    gvc = gvc + gcv_ref[:, cols]
                gck_ref[:, cols] = gkc
                gcv_ref[:, cols] = gvc
            gq_ref[rows, cols] = (gq * scale).astype(BF16)
    gk_ref[base : base + BLK, :] = (ak_ref[...] * scale).astype(BF16)
    gv_ref[base : base + BLK, :] = av_ref[...].astype(BF16)


def normalize(values):
    centered = values - jnp.mean(values, axis=-1, keepdims=True)
    inverse = lax.rsqrt(jnp.mean(centered * centered, axis=-1, keepdims=True) + EPS)
    return centered * inverse, inverse


def norm_back(grad, hat, inverse, gain):
    u = grad * gain
    return inverse * (
        u - jnp.mean(u, axis=-1, keepdims=True) - hat * jnp.mean(u * hat, axis=-1, keepdims=True)
    )


class Links:
    def __init__(self, plan, send, recv):
        self.plan, self.send, self.recv, self.used = plan, send, recv, 0
        self.chan, self.rows = lax.axis_index("chan"), lax.axis_index("rows")
        self.mate = self.chan + 1 - 2 * lax.rem(self.chan, 2)
        self.core = lax.rem(self.chan, 2)
        self.y = self.chan // 2
        self.x = lax.rem(self.rows, plan["X"])
        self.z = self.rows // plan["X"]

    def far(self, j):
        count = self.plan["Y"]
        return 2 * lax.rem(self.y + count + j, count) + self.core

    def other(self, chan):
        return chan + 1 - 2 * lax.rem(chan, 2)

    def put(self, source, target, **device):
        i = self.used
        self.used += 1
        copy = pltpu.make_async_remote_copy(
            src_ref=source, dst_ref=target, send_sem=self.send.at[i], recv_sem=self.recv.at[i],
            device_id=device, device_id_type=MESH,
        )
        copy.start()
        return copy

    def load(self, source, target):
        i = self.used
        self.used += 1
        copy = pltpu.make_async_copy(source, target, self.send.at[i])
        copy.start()
        return copy

    def enter(self):
        barrier = pltpu.get_barrier_semaphore()
        plan = self.plan
        partners = [{"chan": self.mate}]
        partners += [{"chan": self.far(j)} for j in range(1, plan["Y"])]
        partners += [{"rows": self.row_of(self.z, self.x + i)} for i in range(1, plan["X"])]
        partners += [{"rows": self.row_of(self.z + i, self.x)} for i in range(1, plan["Z"])]
        for partner in partners:
            pl.semaphore_signal(barrier, inc=1, device_id=partner, device_id_type=MESH)
        return lambda: pl.semaphore_wait(barrier, len(partners))

    def row_of(self, z, x):
        return lax.rem(z, self.plan["Z"]) * self.plan["X"] + lax.rem(x, self.plan["X"])


class Gather:
    def __init__(self, links, view):
        self.links, self.view = links, view
        own = view(links.chan)
        count = range(1, links.plan["Y"])
        self.direct = [links.put(own, own, chan=links.far(j)) for j in count]
        self.near = links.put(own, own, chan=links.mate)
        self.passed = []

    def forward(self):
        links = self.links
        for j, copy in enumerate(self.direct, 1):
            copy.wait_recv()
            shard = self.view(links.far(-j))
            self.passed.append(links.put(shard, shard, chan=links.mate))

    def finish(self):
        self.near.wait()
        for copy in self.passed:
            copy.wait()
        for copy in self.direct:
            copy.wait_send()


class Scatter:
    def __init__(self, links, mixed_out, mixed_in, far_out, far_in, near_out, near_in):
        self.links = links
        self.mixed_out, self.mixed_in, self.far_out, self.far_in = mixed_out, mixed_in, far_out, far_in
        self.near_out, self.near_in = near_out, near_in
        self.mix, self.direct = [], []

    def for_mate(self, j, value):
        self.mixed_out[j - 1] = value.astype(BF16)
        self.mix.append(
            self.links.put(self.mixed_out.at[j - 1], self.mixed_in.at[j - 1], chan=self.links.mate)
        )

    def for_far(self, j, value_ref):
        self.mix[j - 1].wait_recv()
        self.far_out[j - 1] = (value_ref[...] + self.mixed_in[j - 1].astype(F32)).astype(BF16)

    def send_far(self):
        links = self.links
        self.direct = [
            links.put(self.far_out.at[j - 1], self.far_in.at[j - 1], chan=links.far(j))
            for j in range(1, links.plan["Y"])
        ]

    def for_near(self, value):
        self.near_out[...] = value.astype(BF16)
        self.near = self.links.put(self.near_out, self.near_in, chan=self.links.mate)

    def total(self, own):
        self.near.wait()
        own = own + self.near_in[...].astype(F32)
        for j, copy in enumerate(self.direct):
            copy.wait()
            own = own + self.far_in[j].astype(F32)
        for copy in self.mix:
            copy.wait_send()
        return own


class RowScatter:
    def __init__(self, links, stage, x_in, z_in):
        self.links, self.stage, self.x_in, self.z_in = links, stage, x_in, z_in

    def slab(self, z, x):
        size = self.x_in.shape[2]
        return pl.ds(pl.multiple_of(self.links.row_of(z, x) * size, size), size)

    def over_x(self):
        links, plan = self.links, self.links.plan
        self.first = []
        for step in range(1, plan["Z"] + 1):
            for i in range(1, plan["X"]):
                self.first.append(
                    links.put(
                        self.stage.at[self.slab(links.z + step, links.x + i)],
                        self.x_in.at[i - 1, step - 1],
                        rows=links.row_of(links.z, links.x + i),
                    )
                )

    def mixed(self, step):
        links, plan = self.links, self.links.plan
        value = self.stage[self.slab(links.z + step, links.x), :].astype(F32)
        for i in range(1, plan["X"]):
            self.first[(step - 1) * (plan["X"] - 1) + i - 1].wait()
            value = value + self.x_in[i - 1, step - 1].astype(F32)
        return value

    def over_z(self):
        links, plan = self.links, self.links.plan
        self.second = []
        for step in range(1, plan["Z"]):
            slab = self.slab(links.z + step, links.x)
            self.stage[slab, :] = self.mixed(step).astype(BF16)
            self.second.append(
                links.put(
                    self.stage.at[slab], self.z_in.at[step - 1],
                    rows=links.row_of(links.z + step, links.x),
                )
            )
        self.own = self.mixed(plan["Z"])

    def total(self):
        value = self.own
        for i, copy in enumerate(self.second):
            copy.wait()
            value = value + self.z_in[i].astype(F32)
        return value


def names(plan):
    n, length, d, t, c, f = (plan[k] for k in ("n", "L", "D", "T", "C", "F"))
    far = plan["Y"] - 1
    x1, z, rw = plan["X"] - 1, plan["Z"], plan["RW"]
    grid = (length, d)
    out = [("tok", grid, BF16), ("h1", grid, BF16), ("cot", grid, BF16), ("wout", (d, d), BF16)]
    out += [("attn", grid, BF16), ("h2", grid, BF16), ("act", (length, f), BF16), ("gpre", (length, f), BF16)]
    out += [(w, (d, c), BF16) for w in ("wq", "wk", "wv")] + [("wup", (d, f), BF16), ("wdn", (d, f), BF16)]
    out += [(w, (length, c), BF16) for w in ("q", "k", "v")]
    out += [("ck", (CTX, c), BF16), ("cv", (CTX, c), BF16), ("gck", (CTX, c), F32), ("gcv", (CTX, c), F32)]
    out += [("lse", (c // HEAD, length, 1), F32), ("xs", (BLK, c), F32), ("gx", (BLK, c), F32)]
    out += [("keep", (CTX + 1, plan["NS"], c), F32), ("ak", (BLK, c), F32), ("av", (BLK, c), F32)]
    out += [("do", (BLK, c), BF16), ("r2own", (t, d), F32), ("p", (t, d), F32)]
    out += [("acc", (t, d), F32), ("ffn", (t, d), F32)]
    for s in ("a", "b"):
        out += [(s + part, (far, t, d), BF16) for part in ("_mo", "_mi", "_fo", "_fi")]
        out += [(s + part, (t, d), BF16) for part in ("_no", "_ni")]
    out += [("stage", (d, f), BF16)]
    for s in ("up", "dn", "at"):
        out += [(s + "_xi", (x1, z, rw, f), BF16), (s + "_zi", (z - 1, rw, f), BF16)]
    steps = plan["R"].bit_length() - 1
    out += [("small", (plan["SM"], c), F32), ("smallin", (steps, plan["SM"], c), F32), ("smallout", (steps, plan["SM"], c), F32)]
    out += [("smallall", (n, plan["SM"], c), F32)]
    return out


INPUTS = (
    "tokens", "cotangent", "segments", "w_query", "w_key", "w_value", "w_out", "w_up", "up_bias", "w_down",
    "down_bias", "norm1_gain", "norm1_bias", "norm2_gain", "norm2_bias", "decay_rates", "input_mix",
    "key_mix", "value_mix", "key_skip", "value_skip",
)
LARGE = (
    "tokens", "cotangent", "w_query", "w_key", "w_value", "w_out", "w_up", "w_down",
)


class Box:
    def __init__(self, **items):
        self.__dict__.update(items)


def layer_kernel(plan, *refs):
    i = Box(**dict(zip(INPUTS, refs[:21])))
    outs = refs[21 : 21 + plan["outs"]]
    o_out, o_tok, o_q, o_k, o_v, o_o, o_up, o_dn, o_ub, o_vec, o_dec, o_in, o_km, o_vm, o_skip = outs
    scratch = refs[21 + plan["outs"] :]
    s = Box(**dict(zip([x[0] for x in names(plan)], scratch)))
    links = Links(plan, scratch[-2], scratch[-1])
    n, length, d, t, c, f = (plan[k] for k in ("n", "L", "D", "T", "C", "F"))
    far = range(1, plan["Y"])
    here, mate = links.chan, links.mate
    own_rows, own_cols = at(here * t, t), at(here * c, c)
    rows_of = lambda owner: at(owner * t, t)

    ready = links.enter()
    got_tok = links.load(i.tokens, s.tok.at[own_rows])
    got_w = [links.load(a, b) for a, b in ((i.w_query, s.wq), (i.w_key, s.wk), (i.w_value, s.wv))]
    got_cot = links.load(i.cotangent, s.cot.at[own_rows])
    got_out = links.load(i.w_out, s.wout.at[:, own_cols])
    got_up, got_dn = links.load(i.w_up, s.wup), links.load(i.w_down, s.wdn)
    par = ssm_params(i.decay_rates, i.input_mix, i.key_mix, i.value_mix)
    got_tok.wait()
    ready()
    tok_gather = Gather(links, lambda o: s.tok.at[rows_of(o)])

    def project(owner):
        rows = rows_of(owner)
        hat, _ = normalize(s.tok[rows, :].astype(F32))
        s.h1[rows, :] = (hat * i.norm1_gain[...] + i.norm1_bias[...]).astype(BF16)
        for w, target in ((s.wq, s.q), (s.wk, s.k), (s.wv, s.v)):
            target[rows, :] = dot(s.h1[rows, :], w[...]).astype(BF16)

    for got in got_w:
        got.wait()
    project(here)
    tok_gather.near.wait_recv()
    project(mate)
    got_cot.wait()
    got_out.wait()
    tok_gather.forward()
    out_gather = Gather(links, lambda o: s.wout.at[:, at(o * c, c)])
    cot_gather = Gather(links, lambda o: s.cot.at[rows_of(o)])
    for j in far:
        project(links.far(-j))
    for j, copy in zip(far, tok_gather.passed):
        copy.wait_recv()
        project(links.other(links.far(-j)))
    tok_gather.near.wait_send()
    for copy in tok_gather.passed + tok_gather.direct:
        copy.wait_send()

    s.xs[...] = s.h1[0:BLK, own_cols].astype(F32)
    skip_k, skip_v = i.key_skip[...], i.value_skip[...]
    e0 = ssm_forward(s.xs, i.segments, par, skip_k, skip_v, s.ck, s.cv, s.gck, s.gcv, s.keep)

    def store(rows, head, value):
        s.attn[rows, at(here * c + head * HEAD, HEAD)] = value

    attn_gathers = []
    for block in range(length // BLK):
        attn_forward(block, s.q, s.k, s.v, s.ck, s.cv, i.segments, store, s.lse)
        attn_gathers.append(
            Gather(links, lambda o, block=block: s.attn.at[pl.ds(block * BLK, BLK), at(o * c, c)])
        )
    out_gather.forward()
    cot_gather.forward()
    for gather in attn_gathers:
        gather.forward()
    out_gather.finish()
    cot_gather.finish()
    for gather in attn_gathers:
        gather.finish()
    got_up.wait()
    got_dn.wait()

    wide = 256

    def feed(owner, keep):
        rows = rows_of(owner)

        def residual(e, carry):
            cols = at(e * wide, wide)
            s.p[:, cols] = s.tok[rows, cols].astype(F32) + dot(s.attn[rows, :], s.wout[:, cols])
            return carry

        lax.fori_loop(0, d // wide, residual, 0)
        hat, _ = normalize(s.p[...])
        s.h2[rows, :] = (hat * i.norm2_gain[...] + i.norm2_bias[...]).astype(BF16)
        if keep:
            s.r2own[...] = s.p[...]

        def hidden(e, carry):
            cols = at(e * wide, wide)
            v = dot(s.h2[rows, :], s.wup[:, cols]) + i.up_bias[:, cols]
            grad = dot(s.cot[rows, :], s.wdn[:, cols])
            square = v * v
            th = jnp.tanh(ROOT * (v + 0.044715 * (square * v)))
            half = 0.5 * (1.0 + th)
            s.act[rows, cols] = (v * half).astype(BF16)
            slope = half + 0.5 * v * (1.0 - th * th) * (ROOT * (1.0 + 0.134145 * square))
            s.gpre[rows, cols] = (grad * slope).astype(BF16)
            return carry

        lax.fori_loop(0, f // wide, hidden, 0)

    def back_tile(owner, source, weight):
        rows = rows_of(owner)

        def part(e, carry):
            cols = at(e * wide, wide)
            s.p[:, cols] = dot(source[rows, :], weight[cols, :], NT)
            return carry

        lax.fori_loop(0, d // wide, part, 0)

    def weight_grad(left, right, stage, column):
        def part(e, carry):
            cols = at(e * wide, wide)
            stage[cols, column : column + right.shape[1]] = dot(left[:, cols], right[...], TN).astype(BF16)
            return carry

        lax.fori_loop(0, d // wide, part, 0)

    scatter = lambda k: Scatter(links, *(getattr(s, k + x) for x in ("_mo", "_mi", "_fo", "_fi", "_no", "_ni")))
    grad2 = scatter("a")
    for j in far:
        feed(links.other(links.far(j)), False)
        back_tile(links.other(links.far(j)), s.gpre, s.wup)
        grad2.for_mate(j, s.p[...])
    for j in far:
        feed(links.far(j), False)
        back_tile(links.far(j), s.gpre, s.wup)
        grad2.for_far(j, s.p)
    grad2.send_far()
    feed(mate, False)
    back_tile(mate, s.gpre, s.wup)
    grad2.for_near(s.p[...])
    feed(here, True)
    back_tile(here, s.gpre, s.wup)
    s.acc[...] = s.p[...]

    def rows_sum(k, stage):
        return RowScatter(links, stage, *(getattr(s, k + x) for x in ("_xi", "_zi")))

    weight_grad(s.cot, s.act, s.stage, 0)
    down_sum = rows_sum("dn", s.stage)
    down_sum.over_x()
    ffn = scatter("b")
    for j in far:
        back_tile(links.other(links.far(j)), s.act, s.wdn)
        ffn.for_mate(j, s.p[...])
    for j in far:
        back_tile(links.far(j), s.act, s.wdn)
        ffn.for_far(j, s.p)
    back_tile(mate, s.act, s.wdn)
    ffn.for_near(s.p[...])
    back_tile(here, s.act, s.wdn)
    s.ffn[...] = s.p[...]
    weight_grad(s.h2, s.gpre, s.act, 0)
    up_sum = rows_sum("up", s.act)
    up_sum.over_x()

    base = 4 * plan["NS"] + 2
    bias_rows = f // c
    for e in range(bias_rows):
        s.small[base + e : base + e + 1, :] = jnp.sum(
            s.gpre[:, e * c : (e + 1) * c].astype(F32), axis=0, keepdims=True
        )
    base += bias_rows

    def keep_vector(k, value):
        for e in range(n):
            s.small[base + k * n + e : base + k * n + e + 1, :] = value[:, e * c : (e + 1) * c]

    def colsum(value):
        return jnp.sum(value, axis=0, keepdims=True)

    grad_hidden2 = grad2.total(s.acc[...])
    hat2, inv2 = normalize(s.r2own[...])
    own_cot = s.cot[own_rows, :].astype(F32)
    s.acc[...] = own_cot + norm_back(grad_hidden2, hat2, inv2, i.norm2_gain[...])
    s.tok[own_rows, :] = s.acc[...].astype(BF16)
    branch_gather = Gather(links, lambda o: s.tok.at[rows_of(o)])
    keep_vector(0, colsum(own_cot))
    keep_vector(3, colsum(grad_hidden2 * hat2))
    keep_vector(4, colsum(grad_hidden2))
    down_sum.over_z()
    branch_gather.forward()
    branch_gather.finish()
    ffn.send_far()

    for block in reversed(range(length // BLK)):
        s.do[...] = dot(s.tok[block * BLK : (block + 1) * BLK, :], s.wout[own_cols, :], NT).astype(BF16)
        attn_backward(
            block, s.q, s.k, s.v, s.ck, s.cv, i.segments, s.lse, s.do,
            s.q, s.k, s.v, s.gck, s.gcv, s.ak, s.av,
        )
        if block == 1:
            up_sum.over_z()
            ssm_backward(
                s.xs, i.segments, par, skip_k, skip_v, s.gck, s.gcv, s.keep, e0, s.gx, s.small
            )

    def input_tile(owner):
        rows = rows_of(owner)

        def part(e, carry):
            cols = at(e * wide, wide)
            s.p[:, cols] = (
                dot(s.q[rows, :], s.wq[cols, :], NT)
                + dot(s.k[rows, :], s.wk[cols, :], NT)
                + dot(s.v[rows, :], s.wv[cols, :], NT)
            )
            return carry

        lax.fori_loop(0, d // wide, part, 0)

        @pl.when(owner < BLK // t)
        def _():
            s.p[:, own_cols] = s.p[:, own_cols] + s.gx[rows, :].astype(BF16).astype(F32)

    grad1 = scatter("a")
    for j in far:
        input_tile(links.other(links.far(j)))
        grad1.for_mate(j, s.p[...])
    for j in far:
        input_tile(links.far(j))
        grad1.for_far(j, s.p)
    grad1.send_far()
    input_tile(mate)
    grad1.for_near(s.p[...])
    input_tile(here)
    weight_grad(s.h1, s.q, s.h2, 0)
    weight_grad(s.h1, s.k, s.h2, c)
    weight_grad(s.h1, s.v, s.h2, 2 * c)
    s.q[...] = s.tok[:, own_cols]
    weight_grad(s.attn, s.q, s.h2, 3 * c)
    attn_sum = rows_sum("at", s.h2 if f == d else s.h2.at[:, 0:f])
    attn_sum.over_x()
    o_dn[...] = down_sum.total()
    o_up[...] = up_sum.total()
    o_out[...] = (s.r2own[...] + ffn.total(s.ffn[...]) + i.down_bias[...]).astype(BF16)

    got_tok = links.load(i.tokens, s.gpre.at[0:t] if f == d else s.cot.at[0:t])
    got_tok.wait()
    own_tok = (s.gpre if f == d else s.cot)[0:t, :].astype(F32)
    hat1, inv1 = normalize(own_tok)
    grad_hidden1 = grad1.total(s.p[...])
    o_tok[...] = (s.acc[...] + norm_back(grad_hidden1, hat1, inv1, i.norm1_gain[...])).astype(BF16)
    keep_vector(1, colsum(grad_hidden1 * hat1))
    keep_vector(2, colsum(grad_hidden1))

    steps = plan["R"].bit_length() - 1
    for step in range(steps):
        s.smallout[step] = s.small[...]
        bit = 1 << step
        up = lax.rem(links.rows // bit, 2)
        copy = links.put(s.smallout.at[step], s.smallin.at[step], rows=links.rows + bit - 2 * bit * up)
        if step == 0:
            attn_sum.over_z()
        copy.wait()
        s.small[...] = s.small[...] + s.smallin[step]
    s.smallall[here] = s.small[...]
    small_gather = Gather(links, lambda o: s.smallall.at[o])
    total = attn_sum.total()
    for e, target in enumerate((o_q, o_k, o_v, o_o)):
        target[...] = total[:, e * c : (e + 1) * c]
    small_gather.forward()
    small_gather.finish()
    ns = plan["NS"]
    for e in range(n):
        piece = s.smallall[e]
        for k, target in enumerate((o_dec, o_in, o_km, o_vm)):
            target[e * c : (e + 1) * c, :] = piece[k * ns : (k + 1) * ns, :].T
        o_skip[:, e * c : (e + 1) * c] = piece[4 * ns : 4 * ns + 2, :]
        for b in range(bias_rows):
            o_ub[:, e * f + b * c : e * f + (b + 1) * c] = piece[4 * ns + 2 + b : 4 * ns + 3 + b, :]
    vectors = s.smallall[0]
    for e in range(1, n):
        vectors = vectors + s.smallall[e]
    for k in range(5):
        for e in range(n):
            o_vec[k : k + 1, e * c : (e + 1) * c] = vectors[base + k * n + e : base + k * n + e + 1, :]


def shards(*args):
    a = dict(zip(INPUTS, args))
    n, r = lax.axis_size("chan"), lax.axis_size("rows")
    t, d = a["tokens"].shape
    c, f = a["w_query"].shape[1], a["w_up"].shape[1]
    ns = a["decay_rates"].shape[1]
    x = math.isqrt(r // 2)
    small = 4 * ns + 2 + f // c + 5 * n
    plan = dict(
        n=n, R=r, L=a["segments"].shape[1], D=d, T=t, C=c, F=f, NS=ns, Y=n // 2, X=x, Z=r // x,
        RW=d // r, SM=-(-small // 8) * 8, outs=15,
    )
    shape = jax.ShapeDtypeStruct
    rw = d // r
    outs = [shape((t, d), BF16)] * 2 + [shape((rw, c), F32)] * 4 + [shape((rw, f), F32)] * 2
    outs += [shape((1, n * f), F32), shape((5, d), F32)] + [shape((d, ns), F32)] * 4 + [shape((2, d), F32)]
    values = [v if v.ndim == 2 else v.reshape(1, -1) for v in args]
    vmem, any_space = pl.BlockSpec(memory_space=pltpu.VMEM), pl.BlockSpec(memory_space=pl.ANY)
    sems = pltpu.SemaphoreType.DMA((plan_semaphores(plan),))
    got = pl.pallas_call(
        functools.partial(layer_kernel, plan),
        out_shape=outs,
        in_specs=[any_space if k in LARGE else vmem for k in INPUTS],
        out_specs=[vmem] * len(outs),
        scratch_shapes=[pltpu.VMEM(s, k) for _, s, k in names(plan)] + [sems, sems],
        compiler_params=pltpu.CompilerParams(
            collective_id=0, has_side_effects=True, vmem_limit_bytes=60 << 20
        ),
    )(*values)
    out, tok, q, k, v, o, up, dn, ub, vec, dec, mix, km, vm, skip = got
    return (
        out, tok, q, k, v, o, up, ub[0], dn, vec[0], vec[1], vec[2], vec[3], vec[4],
        dec, mix, km, vm, skip[0], skip[1],
    )


def plan_semaphores(plan):
    y, x, z = plan["Y"] - 1, plan["X"] - 1, plan["Z"]
    gathers = 6 + plan["L"] // BLK
    return 12 + gathers * (2 * y + 1) + 3 * (2 * y + 1) + 3 * (x * z + z - 1) + plan["R"].bit_length()


def solution(mesh):
    both, row, col = P(("rows", "chan"), None), P("rows", None), P(None, "chan")
    state = P("chan", None)
    in_specs = (
        both, both, row, col, col, col, col, col, P("chan"), col,
        P(), P(), P(), P(), P(), state, state, state, state, P("chan"), P("chan"),
    )
    grid = P("rows", "chan")
    out_specs = (both, both, grid, grid, grid, grid, grid, P(), grid) + (P(),) * 11
    return jax.shard_map(shards, mesh=mesh, in_specs=in_specs, out_specs=out_specs, check_vma=False)
```

time: 653 us -> 213 us (0.33); the launches traced: 645 us -> 212 us
  waiting for transfers between devices: 424 us -> 0 us
  Pallas kernels: 24.5 us -> 191 us
  matrix products: 59.5 us -> 0 us
  blocking collectives: 45.5 us -> 0 us
  other arithmetic: 36.1 us -> 0 us
  local copies, waits for them, and re-layouts: 39.3 us -> 20.4 us
  between operations: 14.8 us -> 0.71 us
    reduce_scatter x5 -> x0, waiting for transfers between devices: 205 us -> none  [the longest x2 115 us: scatter_rows(): lax.psum_scatter(partial.astype(BF16), 'rows', scatter_dimension=0, tiled...]
    pallas_call x4 -> x1, Pallas kernels: 24.5 us -> 191 us  [shards(): pl.pallas_call(functools.partial(layer_kernel, plan), out_shape=outs, in_...]
    unnamed x15 -> x0, waiting for transfers between devices: 98.1 us -> none
    psum x1 -> x0, waiting for transfers between devices: 70 us -> none  [shards(): mine = lax.all_gather(lax.psum(mine, 'rows'), 'chan', axis=0)]
    dot_general x18 -> x0, matrix products: 59.5 us -> none  [dot(): return lax.dot_general(left, right, dims, preferred_element_type=F32)]
    all_gather x5 -> x0, waiting for transfers between devices: 51.3 us -> none  [the longest x1 21.9 us: shards(): row_attn = lax.all_gather(attn, 'chan', axis=1, tiled=True)]
    psum x1 -> x0, blocking collectives: 39.5 us -> none  [shards(): lax.psum(jnp.stack([jnp.sum(grad_hidden1 * own_hat1, axis=0), jnp.sum(gra...]
    convert_element_type x7 -> x0, other arithmetic: 12.9 us -> none  [the longest x2 3.29 us: scatter_rows(): lax.psum_scatter(partial.astype(BF16), 'rows', scatter_dimension=0, tiled...]
  transfers between devices with their start and end apart: 13 -> 0, of which waited for: 11 -> 0; matrix products, arithmetic and copies ran while one was open for 17% -> 0% of each run, Pallas kernels for 4% -> 0%
where the time goes in v2:
time: 213 us; the launch traced here: 212 us
  Pallas kernels  191 us (90%)
  local copies, waits for them, and re-layouts  20.4 us (10%)
    pallas_call x1, Pallas kernels, shards(): pl.pallas_call(functools.partial(layer_kernel, plan), out_shape=outs, in_...  191 us
    unnamed x37, local copies, waits for them, and re-layouts  18.8 us

profile of v2, /device:TPU:0, one launch (start us, length us, event | category | flops | bytes accessed | tf_op | source)
XLA Modules:
  0.0 212.2 jit_solution(5331471529227210694)
XLA Ops:
  0.7 1.5 copy.41.refs_15_
  2.1 1.5 copy.42.refs_16_
  3.6 1.5 copy.43.refs_17_
  5.1 1.5 copy.44.refs_18_
  6.5 191.1 %shard_map.356 = (bf16[256,1024]{1,0:T(8,128)(2,1)}, bf16[256,1024]{1,0:T(8,128)(2,1)}, f32[128,256]{1,0:T(8,128)}, f32[128,256]{1,0:T(8,128)}, f32[128,256]{1,0...) custom-call(bf16[256,1024]{1,0:T(8,128)(2,1)} %refs_0_.1, ...), custom_call_target="tpu_custom_call" | custom-call | tf_op jit(solution)/shard_map/pallas_call | solution.py:765
  197.6 0.0 copy-start
  197.6 0.0 copy-start.4
  197.6 0.0 copy-start.3
  197.7 1.6 fusion
  199.2 0.0 copy-start.8
  199.2 1.9 copy.45
  201.1 0.0 copy-start.7
  201.1 0.0 copy-start.6
  201.1 1.9 copy.46
  203.0 0.0 copy-start.5
  203.0 0.0 copy-start.2
  203.0 1.9 copy.47
  204.9 0.0 copy-done
  204.9 0.8 copy.48
  205.7 0.0 copy-done.4
  205.7 0.0 copy-start.9
  205.7 0.0 copy-start.1
  205.7 0.8 copy.58
  206.5 0.0 copy-done.3
  206.5 0.8 copy.59
  207.3 0.0 copy-done.8
  207.3 0.7 copy.60
  208.0 0.0 copy-done.7
  208.0 0.7 copy.61
  208.6 0.0 copy-done.6
  208.6 0.7 copy.62
  209.3 0.0 copy-done.5
  209.3 0.7 copy.63
  210.0 0.0 copy-done.2
  210.0 0.8 copy.64
  210.7 0.0 copy-done.9
  210.8 0.6 copy.65
  211.4 0.0 copy-done.1
  211.4 0.8 copy.66
Async XLA Ops:
  197.6 7.3 %copy-start = (f32[1024,16]{1,0:T(8,128)S(1)}, f32[1024,16]{1,0:T(8,128)}, u32[]{:S(2)}) copy-start(f32[1024,16]{1,0:T(8,128)} %get-tuple-element.67) | copy-start | bytes 196612
  197.6 8.1 %copy-start.4 = (bf16[256,1024]{1,0:T(8,128)(2,1)S(1)}, bf16[256,1024]{1,0:T(8,128)(2,1)}, u32[]{:S(2)}) copy-start(bf16[256,1024]{1,0:T(8,128)(2,1)} %get-tuple-element.99) | copy-start | bytes 1572868
  197.6 8.9 %copy-start.3 = (bf16[256,1024]{1,0:T(8,128)(2,1)S(1)}, bf16[256,1024]{1,0:T(8,128)(2,1)}, u32[]{:S(2)}) copy-start(bf16[256,1024]{1,0:T(8,128)(2,1)} %get-tuple-element.100) | copy-start | bytes 1572868
  199.2 8.1 %copy-start.8 = (f32[128,256]{1,0:T(8,128)S(1)}, f32[128,256]{1,0:T(8,128)}, u32[]{:S(2)}) copy-start(f32[128,256]{1,0:T(8,128)} %get-tuple-element.101) | copy-start | bytes 393220
  201.1 6.9 %copy-start.7 = (f32[128,256]{1,0:T(8,128)S(1)}, f32[128,256]{1,0:T(8,128)}, u32[]{:S(2)}) copy-start(f32[128,256]{1,0:T(8,128)} %get-tuple-element.102) | copy-start | bytes 393220
  201.1 7.5 %copy-start.6 = (f32[128,256]{1,0:T(8,128)S(1)}, f32[128,256]{1,0:T(8,128)}, u32[]{:S(2)}) copy-start(f32[128,256]{1,0:T(8,128)} %get-tuple-element.103) | copy-start | bytes 393220
  203.0 6.3 %copy-start.5 = (f32[128,256]{1,0:T(8,128)S(1)}, f32[128,256]{1,0:T(8,128)}, u32[]{:S(2)}) copy-start(f32[128,256]{1,0:T(8,128)} %get-tuple-element.104) | copy-start | bytes 393220
  203.0 6.9 %copy-start.2 = (f32[128,1024]{1,0:T(8,128)S(1)}, f32[128,1024]{1,0:T(8,128)}, u32[]{:S(2)}) copy-start(f32[128,1024]{1,0:T(8,128)} %get-tuple-element.105) | copy-start | bytes 1572868
  205.7 5.0 %copy-start.9 = (f32[1,4096]{1,0:T(1,128)S(1)}, f32[1,4096]{1,0:T(1,128)}, u32[]{:S(2)}) copy-start(f32[1,4096]{1,0:T(1,128)} %get-tuple-element.42) | copy-start | bytes 49156
  205.7 5.6 %copy-start.1 = (f32[128,1024]{1,0:T(8,128)S(1)}, f32[128,1024]{1,0:T(8,128)}, u32[]{:S(2)}) copy-start(f32[128,1024]{1,0:T(8,128)} %get-tuple-element.107) | copy-start | bytes 1572868

commit v3 on v2

--- a/solution.py
+++ b/solution.py
@@ -34,10 +34,10 @@
 
 
 def ssm_params(rate_ref, in_ref, key_ref, value_ref):
-    rate = rate_ref[...].T
+    rate = rate_ref[...]
     a = jnp.exp(-rate)
     s = jnp.sqrt(1.0 - a * a)
-    return dict(rate=rate, a=a, s=s, mix=in_ref[...].T, km=key_ref[...].T, vm=value_ref[...].T)
+    return dict(rate=rate, a=a, s=s, mix=in_ref[...], km=key_ref[...], vm=value_ref[...])
 
 
 def ssm_forward(x_ref, seg_ref, par, skip_k, skip_v, ck_ref, cv_ref, wide_k, wide_v, keep_ref):
@@ -259,9 +259,9 @@
     def __init__(self, plan, send, recv):
         self.plan, self.send, self.recv, self.used = plan, send, recv, 0
         self.chan, self.rows = lax.axis_index("chan"), lax.axis_index("rows")
-        self.mate = self.chan + 1 - 2 * lax.rem(self.chan, 2)
         self.core = lax.rem(self.chan, 2)
         self.y = self.chan // 2
+        self.mate = self.other(self.chan)
         self.x = lax.rem(self.rows, plan["X"])
         self.z = self.rows // plan["X"]
 
@@ -293,7 +293,8 @@
         barrier = pltpu.get_barrier_semaphore()
         plan = self.plan
         partners = [{"chan": self.mate}]
-        partners += [{"chan": self.far(j)} for j in range(1, plan["Y"])]
+        for j in range(1, plan["Y"]):
+            partners += [{"chan": self.far(j)}, {"chan": self.other(self.far(j))}]
         partners += [{"rows": self.row_of(self.z, self.x + i)} for i in range(1, plan["X"])]
         partners += [{"rows": self.row_of(self.z + i, self.x)} for i in range(1, plan["Z"])]
         for partner in partners:
@@ -328,6 +329,56 @@
             copy.wait_send()
 
 
+class SlabGather:
+    def __init__(self, links, whole, width):
+        self.links, self.whole, self.width = links, whole, width
+        plan = links.plan
+        self.size = whole.shape[0] // plan["R"]
+        own = self.view(links.rows * self.size, self.size, links.chan)
+        self.over_y = [links.put(own, own, chan=links.far(j)) for j in range(1, plan["Y"])]
+        column = whole.at[:, at(links.chan * width, width)]
+        self.near = links.put(column, column, chan=links.mate)
+
+    def view(self, start, size, chan):
+        return self.whole.at[at(start, size), at(chan * self.width, self.width)]
+
+    def spread_x(self):
+        links, plan = self.links, self.links.plan
+        self.over_x = []
+        for j, copy in enumerate(self.over_y, 1):
+            copy.wait_recv()
+            slab = self.view(links.rows * self.size, self.size, links.far(-j))
+            for i in range(1, plan["X"]):
+                self.over_x.append(links.put(slab, slab, rows=links.row_of(links.z, links.x + i)))
+
+    def spread_z(self):
+        links, plan = self.links, self.links.plan
+        self.over_z = []
+        for copy in self.over_x:
+            copy.wait_recv()
+        group = plan["X"] * self.size
+        for j in range(1, plan["Y"]):
+            slab = self.view(links.z * group, group, links.far(-j))
+            for i in range(1, plan["Z"]):
+                self.over_z.append(links.put(slab, slab, rows=links.row_of(links.z + i, links.x)))
+
+    def forward(self):
+        links, plan = self.links, self.links.plan
+        for copy in self.over_z:
+            copy.wait_recv()
+        self.passed = []
+        for j in range(1, plan["Y"]):
+            column = self.whole.at[:, at(links.far(-j) * self.width, self.width)]
+            self.passed.append(links.put(column, column, chan=links.mate))
+
+    def finish(self):
+        self.near.wait()
+        for copy in self.passed:
+            copy.wait()
+        for copy in self.over_y + self.over_x + self.over_z:
+            copy.wait_send()
+
+
 class Scatter:
     def __init__(self, links, mixed_out, mixed_in, far_out, far_in, near_out, near_in):
         self.links = links
@@ -341,16 +392,15 @@
             self.links.put(self.mixed_out.at[j - 1], self.mixed_in.at[j - 1], chan=self.links.mate)
         )
 
-    def for_far(self, j, value_ref):
+    def for_far(self, j, value):
         self.mix[j - 1].wait_recv()
-        self.far_out[j - 1] = (value_ref[...] + self.mixed_in[j - 1].astype(F32)).astype(BF16)
-
-    def send_far(self):
+        self.far_out[j - 1] = (value + self.mixed_in[j - 1].astype(F32)).astype(BF16)
+
+    def send_far(self, j):
         links = self.links
-        self.direct = [
+        self.direct.append(
             links.put(self.far_out.at[j - 1], self.far_in.at[j - 1], chan=links.far(j))
-            for j in range(1, links.plan["Y"])
-        ]
+        )
 
     def for_near(self, value):
         self.near_out[...] = value.astype(BF16)
@@ -370,36 +420,36 @@
 class RowScatter:
     def __init__(self, links, stage, x_in, z_in):
         self.links, self.stage, self.x_in, self.z_in = links, stage, x_in, z_in
+        self.first, self.second = {}, []
 
     def slab(self, z, x):
         size = self.x_in.shape[2]
         return pl.ds(pl.multiple_of(self.links.row_of(z, x) * size, size), size)
 
-    def over_x(self):
+    def compute(self, left, right):
         links, plan = self.links, self.links.plan
-        self.first = []
+        size = plan["X"] * self.x_in.shape[2]
         for step in range(1, plan["Z"] + 1):
+            rows = at(lax.rem(links.z + step, plan["Z"]) * size, size)
+            self.stage[rows, :] = dot(left[:, rows], right[...], TN).astype(BF16)
             for i in range(1, plan["X"]):
-                self.first.append(
-                    links.put(
-                        self.stage.at[self.slab(links.z + step, links.x + i)],
-                        self.x_in.at[i - 1, step - 1],
-                        rows=links.row_of(links.z, links.x + i),
-                    )
+                self.first[step, i] = links.put(
+                    self.stage.at[self.slab(links.z + step, links.x + i)],
+                    self.x_in.at[i - 1, step - 1],
+                    rows=links.row_of(links.z, links.x + i),
                 )
 
     def mixed(self, step):
         links, plan = self.links, self.links.plan
         value = self.stage[self.slab(links.z + step, links.x), :].astype(F32)
         for i in range(1, plan["X"]):
-            self.first[(step - 1) * (plan["X"] - 1) + i - 1].wait()
+            self.first[step, i].wait()
             value = value + self.x_in[i - 1, step - 1].astype(F32)
         return value
 
-    def over_z(self):
+    def over_z(self, *steps):
         links, plan = self.links, self.links.plan
-        self.second = []
-        for step in range(1, plan["Z"]):
+        for step in steps or range(1, plan["Z"]):
             slab = self.slab(links.z + step, links.x)
             self.stage[slab, :] = self.mixed(step).astype(BF16)
             self.second.append(
@@ -408,14 +458,30 @@
                     rows=links.row_of(links.z + step, links.x),
                 )
             )
-        self.own = self.mixed(plan["Z"])
 
     def total(self):
-        value = self.own
+        value = self.mixed(self.links.plan["Z"])
         for i, copy in enumerate(self.second):
             copy.wait()
             value = value + self.z_in[i].astype(F32)
         return value
+
+
+class Doubling:
+    def __init__(self, links, block, out, got):
+        self.links, self.block, self.out, self.got, self.step = links, block, out, got, 0
+
+    def begin(self):
+        step, rows = self.step, self.links.rows
+        self.out[step] = self.block[...]
+        bit = 1 << step
+        partner = rows + bit - 2 * bit * lax.rem(rows // bit, 2)
+        self.copy = self.links.put(self.out.at[step], self.got.at[step], rows=partner)
+
+    def end(self):
+        self.copy.wait()
+        self.block[...] = self.block[...] + self.got[self.step]
+        self.step += 1
 
 
 def names(plan):
@@ -425,22 +491,23 @@
     grid = (length, d)
     out = [("tok", grid, BF16), ("h1", grid, BF16), ("cot", grid, BF16), ("wout", (d, d), BF16)]
     out += [("attn", grid, BF16), ("h2", grid, BF16), ("act", (length, f), BF16), ("gpre", (length, f), BF16)]
-    out += [(w, (d, c), BF16) for w in ("wq", "wk", "wv")] + [("wup", (d, f), BF16), ("wdn", (d, f), BF16)]
-    out += [(w, (length, c), BF16) for w in ("q", "k", "v")]
+    out += [("wqkv", (d, 3 * c), BF16), ("wup", (d, f), BF16), ("wdn", (d, f), BF16)]
+    out += [("qkv", (length, 3 * c), BF16), ("tk", (t, d), BF16), ("gb", (length, c), BF16)]
     out += [("ck", (CTX, c), BF16), ("cv", (CTX, c), BF16), ("gck", (CTX, c), F32), ("gcv", (CTX, c), F32)]
     out += [("lse", (c // HEAD, length, 1), F32), ("xs", (BLK, c), F32), ("gx", (BLK, c), F32)]
     out += [("keep", (CTX + 1, plan["NS"], c), F32), ("ak", (BLK, c), F32), ("av", (BLK, c), F32)]
-    out += [("do", (BLK, c), BF16), ("r2own", (t, d), F32), ("p", (t, d), F32)]
+    out += [("do", (BLK, c), BF16), ("r2own", (t, d), F32), ("p", (BLK, d), F32)]
     out += [("acc", (t, d), F32), ("ffn", (t, d), F32)]
     for s in ("a", "b"):
         out += [(s + part, (far, t, d), BF16) for part in ("_mo", "_mi", "_fo", "_fi")]
         out += [(s + part, (t, d), BF16) for part in ("_no", "_ni")]
-    out += [("stage", (d, f), BF16)]
-    for s in ("up", "dn", "at"):
-        out += [(s + "_xi", (x1, z, rw, f), BF16), (s + "_zi", (z - 1, rw, f), BF16)]
+    out += [("stage", (d, f), BF16), ("ostage", (d, c), BF16)]
+    for s, w in (("up", f), ("dn", f), ("qk", 3 * c), ("ou", c)):
+        out += [(s + "_xi", (x1, z, rw, w), BF16), (s + "_zi", (z - 1, rw, w), BF16)]
     steps = plan["R"].bit_length() - 1
-    out += [("small", (plan["SM"], c), F32), ("smallin", (steps, plan["SM"], c), F32), ("smallout", (steps, plan["SM"], c), F32)]
-    out += [("smallall", (n, plan["SM"], c), F32)]
+    block = (plan["SM"], c)
+    out += [("small", block, F32), ("smallin", (steps,) + block, F32), ("smallout", (steps,) + block, F32)]
+    out += [("fx", (plan["X"], 8, d), F32), ("fz", (z, 8, d), F32), ("fc", (n, 8, d), F32)]
     return out
 
 
@@ -452,6 +519,7 @@
 LARGE = (
     "tokens", "cotangent", "w_query", "w_key", "w_value", "w_out", "w_up", "w_down",
 )
+STATES = ("decay_rates", "input_mix", "key_mix", "value_mix")
 
 
 class Box:
@@ -459,181 +527,192 @@
         self.__dict__.update(items)
 
 
+def colsum(value):
+    return jnp.sum(value, axis=0, keepdims=True)
+
+
 def layer_kernel(plan, *refs):
     i = Box(**dict(zip(INPUTS, refs[:21])))
-    outs = refs[21 : 21 + plan["outs"]]
-    o_out, o_tok, o_q, o_k, o_v, o_o, o_up, o_dn, o_ub, o_vec, o_dec, o_in, o_km, o_vm, o_skip = outs
-    scratch = refs[21 + plan["outs"] :]
+    o_out, o_tok, o_w4, o_up, o_dn, o_small, o_last = refs[21:28]
+    scratch = refs[28:]
     s = Box(**dict(zip([x[0] for x in names(plan)], scratch)))
     links = Links(plan, scratch[-2], scratch[-1])
     n, length, d, t, c, f = (plan[k] for k in ("n", "L", "D", "T", "C", "F"))
     far = range(1, plan["Y"])
-    here, mate = links.chan, links.mate
+    here, mate, core = links.chan, links.mate, links.core
+    pair = 2 * t
     own_rows, own_cols = at(here * t, t), at(here * c, c)
+    own_part, mate_part = at(core * t, t), at((1 - core) * t, t)
     rows_of = lambda owner: at(owner * t, t)
+    chip_rows = lambda owner: at(owner // 2 * pair, pair)
+    q_ref, k_ref, v_ref = (s.qkv.at[:, e * c : (e + 1) * c] for e in range(3))
 
     ready = links.enter()
     got_tok = links.load(i.tokens, s.tok.at[own_rows])
-    got_w = [links.load(a, b) for a, b in ((i.w_query, s.wq), (i.w_key, s.wk), (i.w_value, s.wv))]
+    got_out = links.load(i.w_out, s.wout.at[:, own_cols])
+    got_w = [
+        links.load(w, s.wqkv.at[:, e * c : (e + 1) * c])
+        for e, w in enumerate((i.w_query, i.w_key, i.w_value))
+    ]
     got_cot = links.load(i.cotangent, s.cot.at[own_rows])
-    got_out = links.load(i.w_out, s.wout.at[:, own_cols])
     got_up, got_dn = links.load(i.w_up, s.wup), links.load(i.w_down, s.wdn)
+    got_own = links.load(i.tokens, s.tk)
     par = ssm_params(i.decay_rates, i.input_mix, i.key_mix, i.value_mix)
     got_tok.wait()
+    got_out.wait()
     ready()
+    out_gather = SlabGather(links, s.wout, c)
     tok_gather = Gather(links, lambda o: s.tok.at[rows_of(o)])
-
-    def project(owner):
-        rows = rows_of(owner)
+    out_gather.spread_x()
+
+    def project(rows):
         hat, _ = normalize(s.tok[rows, :].astype(F32))
         s.h1[rows, :] = (hat * i.norm1_gain[...] + i.norm1_bias[...]).astype(BF16)
-        for w, target in ((s.wq, s.q), (s.wk, s.k), (s.wv, s.v)):
-            target[rows, :] = dot(s.h1[rows, :], w[...]).astype(BF16)
+        s.qkv[rows, :] = dot(s.h1[rows, :], s.wqkv[...]).astype(BF16)
 
     for got in got_w:
         got.wait()
-    project(here)
+    project(own_rows)
+    out_gather.spread_z()
     tok_gather.near.wait_recv()
-    project(mate)
+    project(rows_of(mate))
     got_cot.wait()
-    got_out.wait()
+    half = t // 2
+    cot_views = [lambda o, e=e: s.cot.at[at(o * t + e * half, half)] for e in range(2)]
     tok_gather.forward()
-    out_gather = Gather(links, lambda o: s.wout.at[:, at(o * c, c)])
-    cot_gather = Gather(links, lambda o: s.cot.at[rows_of(o)])
+    cot_gathers = [Gather(links, cot_views[0])]
     for j in far:
-        project(links.far(-j))
+        project(rows_of(links.far(-j)))
     for j, copy in zip(far, tok_gather.passed):
         copy.wait_recv()
-        project(links.other(links.far(-j)))
+        project(rows_of(links.other(links.far(-j))))
     tok_gather.near.wait_send()
     for copy in tok_gather.passed + tok_gather.direct:
         copy.wait_send()
 
+    def store(rows, head, value):
+        s.attn[rows, at(here * c + head * HEAD, HEAD)] = value
+
+    attn_gathers = []
+
+    def attend(block):
+        attn_forward(block, q_ref, k_ref, v_ref, s.ck, s.cv, i.segments, store, s.lse)
+        attn_gathers.append(
+            Gather(links, lambda o: s.attn.at[pl.ds(block * BLK, BLK), at(o * c, c)])
+        )
+
+    attend(0)
     s.xs[...] = s.h1[0:BLK, own_cols].astype(F32)
     skip_k, skip_v = i.key_skip[...], i.value_skip[...]
     e0 = ssm_forward(s.xs, i.segments, par, skip_k, skip_v, s.ck, s.cv, s.gck, s.gcv, s.keep)
-
-    def store(rows, head, value):
-        s.attn[rows, at(here * c + head * HEAD, HEAD)] = value
-
-    attn_gathers = []
-    for block in range(length // BLK):
-        attn_forward(block, s.q, s.k, s.v, s.ck, s.cv, i.segments, store, s.lse)
-        attn_gathers.append(
-            Gather(links, lambda o, block=block: s.attn.at[pl.ds(block * BLK, BLK), at(o * c, c)])
-        )
+    cot_gathers[0].forward()
+    attend(1)
+    cot_gathers.append(Gather(links, cot_views[1]))
     out_gather.forward()
-    cot_gather.forward()
-    for gather in attn_gathers:
-        gather.forward()
-    out_gather.finish()
-    cot_gather.finish()
-    for gather in attn_gathers:
-        gather.finish()
+    attn_gathers[0].forward()
     got_up.wait()
     got_dn.wait()
-
-    wide = 256
-
-    def feed(owner, keep):
-        rows = rows_of(owner)
-
-        def residual(e, carry):
-            cols = at(e * wide, wide)
+    out_gather.finish()
+
+    wide = 512
+
+    def loop(count, body):
+        def step(e, carry):
+            body(at(e * wide, wide))
+            return carry
+
+        lax.fori_loop(0, count // wide, step, 0)
+
+    def feed(block):
+        rows = pl.ds(block * BLK, BLK)
+
+        def residual(cols):
             s.p[:, cols] = s.tok[rows, cols].astype(F32) + dot(s.attn[rows, :], s.wout[:, cols])
-            return carry
-
-        lax.fori_loop(0, d // wide, residual, 0)
+
+        loop(d, residual)
         hat, _ = normalize(s.p[...])
         s.h2[rows, :] = (hat * i.norm2_gain[...] + i.norm2_bias[...]).astype(BF16)
-        if keep:
-            s.r2own[...] = s.p[...]
-
-        def hidden(e, carry):
-            cols = at(e * wide, wide)
+
+        @pl.when(here * t // BLK == block)
+        def _():
+            s.r2own[...] = s.p[at(lax.rem(here * t, BLK), t), :]
+
+        def hidden(cols):
             v = dot(s.h2[rows, :], s.wup[:, cols]) + i.up_bias[:, cols]
-            grad = dot(s.cot[rows, :], s.wdn[:, cols])
             square = v * v
             th = jnp.tanh(ROOT * (v + 0.044715 * (square * v)))
-            half = 0.5 * (1.0 + th)
-            s.act[rows, cols] = (v * half).astype(BF16)
-            slope = half + 0.5 * v * (1.0 - th * th) * (ROOT * (1.0 + 0.134145 * square))
-            s.gpre[rows, cols] = (grad * slope).astype(BF16)
-            return carry
-
-        lax.fori_loop(0, f // wide, hidden, 0)
-
-    def back_tile(owner, source, weight):
-        rows = rows_of(owner)
-
-        def part(e, carry):
-            cols = at(e * wide, wide)
-            s.p[:, cols] = dot(source[rows, :], weight[cols, :], NT)
-            return carry
-
-        lax.fori_loop(0, d // wide, part, 0)
-
-    def weight_grad(left, right, stage, column):
-        def part(e, carry):
-            cols = at(e * wide, wide)
-            stage[cols, column : column + right.shape[1]] = dot(left[:, cols], right[...], TN).astype(BF16)
-            return carry
-
-        lax.fori_loop(0, d // wide, part, 0)
+            part = 0.5 * (1.0 + th)
+            s.act[rows, cols] = (v * part).astype(BF16)
+            slope = part + 0.5 * v * (1.0 - th * th) * (ROOT * (1.0 + 0.134145 * square))
+            s.gpre[rows, cols] = slope.astype(BF16)
+
+        loop(f, hidden)
+
+    attn_gathers[0].finish()
+    feed(0)
+    attn_gathers[1].forward()
+    cot_gathers[1].forward()
+    attn_gathers[1].finish()
+    feed(1)
+    for gather in cot_gathers:
+        gather.finish()
+
+    def rows_sum(k, stage):
+        return RowScatter(links, stage, getattr(s, k + "_xi"), getattr(s, k + "_zi"))
+
+    down_sum = rows_sum("dn", s.stage)
+    down_sum.compute(s.cot, s.act)
+
+    def slope_grad(owner):
+        rows = chip_rows(owner)
+
+        def part(cols):
+            grad = dot(s.cot[rows, :], s.wdn[:, cols])
+            s.gpre[rows, cols] = (grad * s.gpre[rows, cols].astype(F32)).astype(BF16)
+
+        loop(f, part)
+
+    def back(owner, source, weight):
+        rows = chip_rows(owner)
+
+        def part(cols):
+            s.p[0:pair, cols] = dot(source[rows, :], weight[cols, :], NT)
+
+        loop(d, part)
 
     scatter = lambda k: Scatter(links, *(getattr(s, k + x) for x in ("_mo", "_mi", "_fo", "_fi", "_no", "_ni")))
     grad2 = scatter("a")
     for j in far:
-        feed(links.other(links.far(j)), False)
-        back_tile(links.other(links.far(j)), s.gpre, s.wup)
-        grad2.for_mate(j, s.p[...])
-    for j in far:
-        feed(links.far(j), False)
-        back_tile(links.far(j), s.gpre, s.wup)
-        grad2.for_far(j, s.p)
-    grad2.send_far()
-    feed(mate, False)
-    back_tile(mate, s.gpre, s.wup)
-    grad2.for_near(s.p[...])
-    feed(here, True)
-    back_tile(here, s.gpre, s.wup)
-    s.acc[...] = s.p[...]
-
-    def rows_sum(k, stage):
-        return RowScatter(links, stage, *(getattr(s, k + x) for x in ("_xi", "_zi")))
-
-    weight_grad(s.cot, s.act, s.stage, 0)
-    down_sum = rows_sum("dn", s.stage)
-    down_sum.over_x()
+        slope_grad(links.far(j))
+        back(links.far(j), s.gpre, s.wup)
+        grad2.for_mate(j, s.p[mate_part, :])
+        if j == plan["Y"] - 1:
+            slope_grad(here)
+        grad2.for_far(j, s.p[own_part, :])
+        grad2.send_far(j)
+    back(here, s.gpre, s.wup)
+    grad2.for_near(s.p[mate_part, :])
+    s.acc[...] = s.p[own_part, :]
     ffn = scatter("b")
     for j in far:
-        back_tile(links.other(links.far(j)), s.act, s.wdn)
-        ffn.for_mate(j, s.p[...])
-    for j in far:
-        back_tile(links.far(j), s.act, s.wdn)
-        ffn.for_far(j, s.p)
-    back_tile(mate, s.act, s.wdn)
-    ffn.for_near(s.p[...])
-    back_tile(here, s.act, s.wdn)
-    s.ffn[...] = s.p[...]
-    weight_grad(s.h2, s.gpre, s.act, 0)
+        back(links.far(j), s.act, s.wdn)
+        ffn.for_mate(j, s.p[mate_part, :])
+        ffn.for_far(j, s.p[own_part, :])
+    back(here, s.act, s.wdn)
+    ffn.for_near(s.p[mate_part, :])
+    s.ffn[...] = s.p[own_part, :]
     up_sum = rows_sum("up", s.act)
-    up_sum.over_x()
+    up_sum.compute(s.h2, s.gpre)
 
     base = 4 * plan["NS"] + 2
     bias_rows = f // c
     for e in range(bias_rows):
-        s.small[base + e : base + e + 1, :] = jnp.sum(
-            s.gpre[:, e * c : (e + 1) * c].astype(F32), axis=0, keepdims=True
-        )
+        s.small[base + e : base + e + 1, :] = colsum(s.gpre[:, e * c : (e + 1) * c].astype(F32))
     base += bias_rows
 
     def keep_vector(k, value):
         for e in range(n):
             s.small[base + k * n + e : base + k * n + e + 1, :] = value[:, e * c : (e + 1) * c]
-
-    def colsum(value):
-        return jnp.sum(value, axis=0, keepdims=True)
 
     grad_hidden2 = grad2.total(s.acc[...])
     hat2, inv2 = normalize(s.r2own[...])
@@ -642,105 +721,126 @@
     s.tok[own_rows, :] = s.acc[...].astype(BF16)
     branch_gather = Gather(links, lambda o: s.tok.at[rows_of(o)])
     keep_vector(0, colsum(own_cot))
-    keep_vector(3, colsum(grad_hidden2 * hat2))
-    keep_vector(4, colsum(grad_hidden2))
+    keep_vector(1, colsum(grad_hidden2 * hat2))
+    keep_vector(2, colsum(grad_hidden2))
     down_sum.over_z()
     branch_gather.forward()
     branch_gather.finish()
-    ffn.send_far()
-
-    for block in reversed(range(length // BLK)):
+    for j in far:
+        ffn.send_far(j)
+
+    def attend_back(block):
         s.do[...] = dot(s.tok[block * BLK : (block + 1) * BLK, :], s.wout[own_cols, :], NT).astype(BF16)
         attn_backward(
-            block, s.q, s.k, s.v, s.ck, s.cv, i.segments, s.lse, s.do,
-            s.q, s.k, s.v, s.gck, s.gcv, s.ak, s.av,
+            block, q_ref, k_ref, v_ref, s.ck, s.cv, i.segments, s.lse, s.do,
+            q_ref, k_ref, v_ref, s.gck, s.gcv, s.ak, s.av,
         )
-        if block == 1:
-            up_sum.over_z()
-            ssm_backward(
-                s.xs, i.segments, par, skip_k, skip_v, s.gck, s.gcv, s.keep, e0, s.gx, s.small
-            )
-
-    def input_tile(owner):
-        rows = rows_of(owner)
-
-        def part(e, carry):
-            cols = at(e * wide, wide)
-            s.p[:, cols] = (
-                dot(s.q[rows, :], s.wq[cols, :], NT)
-                + dot(s.k[rows, :], s.wk[cols, :], NT)
-                + dot(s.v[rows, :], s.wv[cols, :], NT)
-            )
-            return carry
-
-        lax.fori_loop(0, d // wide, part, 0)
-
-        @pl.when(owner < BLK // t)
+
+    attend_back(1)
+    ssm_backward(s.xs, i.segments, par, skip_k, skip_v, s.gck, s.gcv, s.keep, e0, s.gx, s.small)
+    steps = plan["R"].bit_length() - 1
+    doubling = Doubling(links, s.small, s.smallout, s.smallin)
+    doubling.begin()
+    attend_back(0)
+
+    def input_back(owner):
+        rows = chip_rows(owner)
+
+        def part(cols):
+            s.p[0:pair, cols] = dot(s.qkv[rows, :], s.wqkv[cols, :], NT)
+
+        loop(d, part)
+
+        @pl.when(owner // 2 * pair < BLK)
         def _():
-            s.p[:, own_cols] = s.p[:, own_cols] + s.gx[rows, :].astype(BF16).astype(F32)
+            s.p[0:pair, own_cols] = s.p[0:pair, own_cols] + s.gx[rows, :].astype(BF16).astype(F32)
 
     grad1 = scatter("a")
+    qkv_sum = rows_sum("qk", s.h2.at[:, 0 : 3 * c])
     for j in far:
-        input_tile(links.other(links.far(j)))
-        grad1.for_mate(j, s.p[...])
-    for j in far:
-        input_tile(links.far(j))
-        grad1.for_far(j, s.p)
-    grad1.send_far()
-    input_tile(mate)
-    grad1.for_near(s.p[...])
-    input_tile(here)
-    weight_grad(s.h1, s.q, s.h2, 0)
-    weight_grad(s.h1, s.k, s.h2, c)
-    weight_grad(s.h1, s.v, s.h2, 2 * c)
-    s.q[...] = s.tok[:, own_cols]
-    weight_grad(s.attn, s.q, s.h2, 3 * c)
-    attn_sum = rows_sum("at", s.h2 if f == d else s.h2.at[:, 0:f])
-    attn_sum.over_x()
+        input_back(links.far(j))
+        grad1.for_mate(j, s.p[mate_part, :])
+        if j == 1:
+            qkv_sum.compute(s.h1, s.qkv)
+        grad1.for_far(j, s.p[own_part, :])
+        grad1.send_far(j)
+    doubling.end()
+    doubling.begin()
+    input_back(here)
+    grad1.for_near(s.p[mate_part, :])
+    s.gb[...] = s.tok[:, own_cols]
+    out_sum = rows_sum("ou", s.ostage)
+    out_sum.compute(s.attn, s.gb)
+    up_sum.over_z()
+    for step in range(1, steps):
+        doubling.end()
+        if step < steps - 1:
+            doubling.begin()
+    o_small[here] = s.small[...]
+    small_gather = Gather(links, lambda o: o_small.at[o])
     o_dn[...] = down_sum.total()
+    qkv_sum.over_z()
+    out_sum.over_z()
     o_up[...] = up_sum.total()
     o_out[...] = (s.r2own[...] + ffn.total(s.ffn[...]) + i.down_bias[...]).astype(BF16)
 
-    got_tok = links.load(i.tokens, s.gpre.at[0:t] if f == d else s.cot.at[0:t])
-    got_tok.wait()
-    own_tok = (s.gpre if f == d else s.cot)[0:t, :].astype(F32)
-    hat1, inv1 = normalize(own_tok)
-    grad_hidden1 = grad1.total(s.p[...])
+    got_own.wait()
+    hat1, inv1 = normalize(s.tk[...].astype(F32))
+    grad_hidden1 = grad1.total(s.p[own_part, :])
     o_tok[...] = (s.acc[...] + norm_back(grad_hidden1, hat1, inv1, i.norm1_gain[...])).astype(BF16)
-    keep_vector(1, colsum(grad_hidden1 * hat1))
-    keep_vector(2, colsum(grad_hidden1))
-
-    steps = plan["R"].bit_length() - 1
-    for step in range(steps):
-        s.smallout[step] = s.small[...]
-        bit = 1 << step
-        up = lax.rem(links.rows // bit, 2)
-        copy = links.put(s.smallout.at[step], s.smallin.at[step], rows=links.rows + bit - 2 * bit * up)
-        if step == 0:
-            attn_sum.over_z()
+    s.fx[links.x, 0:1, :] = colsum(grad_hidden1 * hat1)
+    s.fx[links.x, 1:2, :] = colsum(grad_hidden1)
+    s.fx[links.x, 2:8, :] = jnp.zeros((6, d), F32)
+
+    def spread(slots, own, targets):
+        return [links.put(slots.at[own], slots.at[own], **target) for target in targets]
+
+    hops = spread(s.fx, links.x, [{"rows": links.row_of(links.z, links.x + e)} for e in range(1, plan["X"])])
+    small_gather.forward()
+    for hop in hops:
+        hop.wait()
+    s.fz[links.z] = sum([s.fx[e] for e in range(1, plan["X"])], s.fx[0])
+    hops = spread(s.fz, links.z, [{"rows": links.row_of(links.z + e, links.x)} for e in range(1, plan["Z"])])
+    small_gather.finish()
+    for hop in hops:
+        hop.wait()
+    s.fc[here] = sum([s.fz[e] for e in range(1, plan["Z"])], s.fz[0])
+    group = [mate] + [links.far(j) for j in far] + [links.other(links.far(j)) for j in far]
+    hops = spread(s.fc, here, [{"chan": e} for e in group])
+    o_w4[:, 3 * c : 4 * c] = out_sum.total()
+    o_w4[:, 0 : 3 * c] = qkv_sum.total()
+    for hop in hops:
+        hop.wait()
+    o_last[...] = sum([s.fc[e] for e in range(1, n)], s.fc[0])
+
+
+def finish_kernel(plan, *refs):
+    out, tok, w4, up, dn, small, last = refs[:7]
+    o_out, o_tok, o_q, o_k, o_v, o_o, o_up, o_ub, o_dn, o_db, o_g1, o_b1, o_g2, o_b2 = refs[7:21]
+    o_dec, o_in, o_km, o_vm, o_ks, o_vs, sem = refs[21:]
+    n, c, f, ns = (plan[k] for k in ("n", "C", "F", "NS"))
+    moves = [(out, o_out), (tok, o_tok), (up, o_up), (dn, o_dn)]
+    moves += [(w4.at[:, e * c : (e + 1) * c], o) for e, o in enumerate((o_q, o_k, o_v, o_o))]
+    copies = [pltpu.make_async_copy(a, b, sem.at[e]) for e, (a, b) in enumerate(moves)]
+    for copy in copies:
+        copy.start()
+    bias_rows = f // c
+    base = 4 * ns + 2 + bias_rows
+    for e in range(n):
+        cols = slice(e * c, (e + 1) * c)
+        for k, target in enumerate((o_dec, o_in, o_km, o_vm)):
+            target[:, cols] = small[e, k * ns : (k + 1) * ns, :]
+        o_ks[:, cols] = small[e, 4 * ns : 4 * ns + 1, :]
+        o_vs[:, cols] = small[e, 4 * ns + 1 : 4 * ns + 2, :]
+        for b in range(bias_rows):
+            o_ub[:, e * f + b * c : e * f + (b + 1) * c] = small[e, 4 * ns + 2 + b : 4 * ns + 3 + b, :]
+        for k, target in enumerate((o_db, o_g2, o_b2)):
+            row = base + k * n + e
+            target[:, cols] = sum([small[g, row : row + 1, :] for g in range(1, n)], small[0, row : row + 1, :])
+    o_g1[...] = last[0:1, :]
+    o_b1[...] = last[1:2, :]
+    for copy in copies:
         copy.wait()
-        s.small[...] = s.small[...] + s.smallin[step]
-    s.smallall[here] = s.small[...]
-    small_gather = Gather(links, lambda o: s.smallall.at[o])
-    total = attn_sum.total()
-    for e, target in enumerate((o_q, o_k, o_v, o_o)):
-        target[...] = total[:, e * c : (e + 1) * c]
-    small_gather.forward()
-    small_gather.finish()
-    ns = plan["NS"]
-    for e in range(n):
-        piece = s.smallall[e]
-        for k, target in enumerate((o_dec, o_in, o_km, o_vm)):
-            target[e * c : (e + 1) * c, :] = piece[k * ns : (k + 1) * ns, :].T
-        o_skip[:, e * c : (e + 1) * c] = piece[4 * ns : 4 * ns + 2, :]
-        for b in range(bias_rows):
-            o_ub[:, e * f + b * c : e * f + (b + 1) * c] = piece[4 * ns + 2 + b : 4 * ns + 3 + b, :]
-    vectors = s.smallall[0]
-    for e in range(1, n):
-        vectors = vectors + s.smallall[e]
-    for k in range(5):
-        for e in range(n):
-            o_vec[k : k + 1, e * c : (e + 1) * c] = vectors[base + k * n + e : base + k * n + e + 1, :]
 
 
 def shards(*args):
@@ -750,16 +850,18 @@
     c, f = a["w_query"].shape[1], a["w_up"].shape[1]
     ns = a["decay_rates"].shape[1]
     x = math.isqrt(r // 2)
-    small = 4 * ns + 2 + f // c + 5 * n
+    small = 4 * ns + 2 + f // c + 3 * n
     plan = dict(
         n=n, R=r, L=a["segments"].shape[1], D=d, T=t, C=c, F=f, NS=ns, Y=n // 2, X=x, Z=r // x,
-        RW=d // r, SM=-(-small // 8) * 8, outs=15,
+        RW=d // r, SM=-(-small // 8) * 8,
     )
     shape = jax.ShapeDtypeStruct
     rw = d // r
-    outs = [shape((t, d), BF16)] * 2 + [shape((rw, c), F32)] * 4 + [shape((rw, f), F32)] * 2
-    outs += [shape((1, n * f), F32), shape((5, d), F32)] + [shape((d, ns), F32)] * 4 + [shape((2, d), F32)]
-    values = [v if v.ndim == 2 else v.reshape(1, -1) for v in args]
+    outs = [shape((t, d), BF16)] * 2 + [shape((rw, 4 * c), F32)] + [shape((rw, f), F32)] * 2
+    outs += [shape((n, plan["SM"], c), F32), shape((8, d), F32)]
+    for k in STATES:
+        a[k] = a[k].T
+    values = [v if v.ndim == 2 else v.reshape(1, -1) for v in (a[k] for k in INPUTS)]
     vmem, any_space = pl.BlockSpec(memory_space=pltpu.VMEM), pl.BlockSpec(memory_space=pl.ANY)
     sems = pltpu.SemaphoreType.DMA((plan_semaphores(plan),))
     got = pl.pallas_call(
@@ -772,17 +874,35 @@
             collective_id=0, has_side_effects=True, vmem_limit_bytes=60 << 20
         ),
     )(*values)
-    out, tok, q, k, v, o, up, dn, ub, vec, dec, mix, km, vm, skip = got
-    return (
-        out, tok, q, k, v, o, up, ub[0], dn, vec[0], vec[1], vec[2], vec[3], vec[4],
-        dec, mix, km, vm, skip[0], skip[1],
-    )
+    row, state, line = shape((1, d), F32), shape((ns, d), F32), shape((rw, c), F32)
+    token = shape((t, d), BF16)
+    wide = shape((rw, f), F32)
+    outs = [token, token, line, line, line, line, wide, shape((1, n * f), F32), wide]
+    outs += [row] * 5 + [state] * 4 + [row] * 2
+    large = (0, 1, 2, 3, 4, 5, 6, 8)
+    done = pl.pallas_call(
+        functools.partial(finish_kernel, plan),
+        out_shape=outs,
+        in_specs=[vmem] * 7,
+        out_specs=[any_space if e in large else vmem for e in range(len(outs))],
+        scratch_shapes=[pltpu.SemaphoreType.DMA((len(large),))],
+    )(*got)
+    done = list(done)
+    for e in range(len(done)):
+        if 14 <= e < 18:
+            done[e] = done[e].T
+        elif e not in large:
+            done[e] = done[e].reshape(-1)
+    return tuple(done)
 
 
 def plan_semaphores(plan):
     y, x, z = plan["Y"] - 1, plan["X"] - 1, plan["Z"]
-    gathers = 6 + plan["L"] // BLK
-    return 12 + gathers * (2 * y + 1) + 3 * (2 * y + 1) + 3 * (x * z + z - 1) + plan["R"].bit_length()
+    gathers = 5 + plan["L"] // BLK
+    slabs = 1 + y * (2 + x + z)
+    hops = x + z + plan["n"]
+    rows = 4 * (x * z + z - 1)
+    return 12 + gathers * (2 * y + 1) + slabs + 3 * (2 * y + 1) + rows + plan["R"].bit_length() + hops
 
 
 def solution(mesh):

time: 213 us -> 168 us (0.79)
  Pallas kernels: 191 us -> 166 us
  local copies, waits for them, and re-layouts: 20.4 us -> 0 us
    pallas_call x1, Pallas kernels: 191 us -> 162 us  [shards(): pl.pallas_call(functools.partial(layer_kernel, plan), out_shape=outs, in_...]
    unnamed x37 -> x0, local copies, waits for them, and re-layouts: 18.8 us -> none
    pallas_call x0 -> x1, Pallas kernels: none -> 4.07 us  [shards(): pl.pallas_call(functools.partial(finish_kernel, plan), out_shape=outs, in...]
where the time goes in v3:
time: 168 us; the launch traced here: 167 us
  Pallas kernels  166 us (99%)
    pallas_call x1, Pallas kernels, shards(): pl.pallas_call(functools.partial(layer_kernel, plan), out_shape=outs, in_...  162 us
    pallas_call x1, Pallas kernels, shards(): pl.pallas_call(functools.partial(finish_kernel, plan), out_shape=outs, in...  4.07 us

profile of v3, /device:TPU:0, one launch (start us, length us, event | category | flops | bytes accessed | tf_op | source)
XLA Modules:
  0.0 167.3 jit_solution(9278570027321050188)
XLA Ops:
  0.7 162.3 %shard_map.356 = (bf16[256,1024]{1,0:T(8,128)(2,1)}, bf16[256,1024]{1,0:T(8,128)(2,1)}, f32[128,1024]{1,0:T(8,128)}, f32[128,1024]{1,0:T(8,128)}, f32[128,1024]{...) custom-call(bf16[256,1024]{1,0:T(8,128)(2,1)} %refs_0_.1, bf16[256,1024]{1,0:T(8,128)(2,1)} %refs_1_.1, ...), custom_call_target="tpu_custom_call" | custom-call | tf_op jit(solution)/shard_map/pallas_call | solution.py:867
  163.0 4.1 %shard_map.357 = (bf16[256,1024]{1,0:T(8,128)(2,1)}, bf16[256,1024]{1,0:T(8,128)(2,1)}, f32[128,256]{1,0:T(8,128)}, f32[128,256]{1,0:T(8,128)}, f32[128,256]{1,0...) custom-call(bf16[256,1024]{1,0:T(8,128)(2,1)} %get-tuple-element.47., ...), custom_call_target="tpu_custom_call" | custom-call | tf_op jit(solution)/shard_map/pallas_call | solution.py:883

commit v4 on v3

--- a/solution.py
+++ b/solution.py
@@ -1,4 +1,5 @@
 import functools
+import itertools
 import math
 
 import jax
@@ -404,6 +405,9 @@
 
     def for_near(self, value):
         self.near_out[...] = value.astype(BF16)
+        self.send_near()
+
+    def send_near(self):
         self.near = self.links.put(self.near_out, self.near_in, chan=self.links.mate)
 
     def total(self, own):
@@ -418,53 +422,85 @@
 
 
 class RowScatter:
-    def __init__(self, links, stage, x_in, z_in):
-        self.links, self.stage, self.x_in, self.z_in = links, stage, x_in, z_in
-        self.first, self.second = {}, []
-
-    def slab(self, z, x):
-        size = self.x_in.shape[2]
-        return pl.ds(pl.multiple_of(self.links.row_of(z, x) * size, size), size)
-
-    def compute(self, left, right):
-        links, plan = self.links, self.links.plan
-        size = plan["X"] * self.x_in.shape[2]
-        for step in range(1, plan["Z"] + 1):
-            rows = at(lax.rem(links.z + step, plan["Z"]) * size, size)
-            self.stage[rows, :] = dot(left[:, rows], right[...], TN).astype(BF16)
-            for i in range(1, plan["X"]):
-                self.first[step, i] = links.put(
-                    self.stage.at[self.slab(links.z + step, links.x + i)],
-                    self.x_in.at[i - 1, step - 1],
-                    rows=links.row_of(links.z, links.x + i),
-                )
-
-    def mixed(self, step):
-        links, plan = self.links, self.links.plan
-        value = self.stage[self.slab(links.z + step, links.x), :].astype(F32)
-        for i in range(1, plan["X"]):
-            self.first[step, i].wait()
-            value = value + self.x_in[i - 1, step - 1].astype(F32)
+    def __init__(self, links, stage, slots, order):
+        self.links, self.stage, self.slots, self.order = links, stage, slots, order
+        plan = links.plan
+        self.size = dict(x=plan["X"], l=2, h=plan["Z"] // 2)
+        self.copies, self.slot = {}, {}
+        self.todo = []
+        for k in range(3):
+            for key in self.keys(k):
+                self.slot[key] = len(self.slot)
+                if k:
+                    self.todo.append(key)
+
+    def keys(self, k):
+        rest = [range(self.size[axis] - 1, -1, -1) for axis in self.order[k + 1 :]]
+        for i in range(self.size[self.order[k]] - 1, 0, -1):
+            for offsets in itertools.product(*rest):
+                yield (k, i) + offsets
+
+    def place(self, offsets):
+        links = self.links
+        own = dict(x=links.x, l=lax.rem(links.z, 2), h=links.z // 2)
+        to = {axis: lax.rem(own[axis] + offsets.get(axis, 0), self.size[axis]) for axis in own}
+        return (to["h"] * 2 + to["l"]) * self.size["x"] + to["x"]
+
+    def slab(self, offsets):
+        size = self.slots.shape[1]
+        return pl.ds(pl.multiple_of(self.place(offsets) * size, size), size)
+
+    def send(self, key):
+        k, i = key[:2]
+        offsets = dict(zip(self.order[k:], key[1:]))
+        slab = self.slab(offsets)
+        if k:
+            self.stage[slab, :] = self.value(k, offsets).astype(BF16)
+        self.copies[key] = self.links.put(
+            self.stage.at[slab], self.slots.at[self.slot[key]], rows=self.place({self.order[k]: i})
+        )
+
+    def value(self, k, offsets):
+        total = self.stage[self.slab(offsets), :].astype(F32)
+        for j in range(k):
+            later = tuple(offsets.get(axis, 0) for axis in self.order[j + 1 :])
+            for i in range(1, self.size[self.order[j]]):
+                key = (j, i) + later
+                self.copies[key].wait_recv()
+                total = total + self.slots[self.slot[key]].astype(F32)
+        return total
+
+    def ready(self, low, high):
+        offsets = dict(l=low, h=high)
+        for x in range(self.size["x"] - 1, -1, -1):
+            offsets["x"] = x
+            key = (0,) + tuple(offsets[axis] for axis in self.order)
+            if key[1]:
+                self.send(key)
+
+    def advance(self, count=1):
+        for _ in range(min(count, len(self.todo))):
+            self.send(self.todo.pop(0))
+
+    def total(self):
+        self.advance(len(self.todo))
+        value = self.value(3, {})
+        for copy in self.copies.values():
+            copy.wait_send()
         return value
 
-    def over_z(self, *steps):
-        links, plan = self.links, self.links.plan
-        for step in steps or range(1, plan["Z"]):
-            slab = self.slab(links.z + step, links.x)
-            self.stage[slab, :] = self.mixed(step).astype(BF16)
-            self.second.append(
-                links.put(
-                    self.stage.at[slab], self.z_in.at[step - 1],
-                    rows=links.row_of(links.z + step, links.x),
-                )
-            )
-
-    def total(self):
-        value = self.mixed(self.links.plan["Z"])
-        for i, copy in enumerate(self.second):
-            copy.wait()
-            value = value + self.z_in[i].astype(F32)
-        return value
+
+def weight_sums(left, right, sums):
+    first = sums[0][0]
+    rows = first.links.plan["X"] * first.slots.shape[1]
+    for low in (1, 0):
+        for high in range(first.size["h"] - 1, -1, -1):
+            group = at(first.place(dict(l=low, h=high)) // first.size["x"] * rows, rows)
+            product = dot(left[:, group], right[...], TN).astype(BF16)
+            for one, cols in sums:
+                one.stage[group, :] = product[:, cols]
+            for one, _ in sums:
+                one.ready(low, high)
 
 
 class Doubling:
@@ -487,12 +523,12 @@
 def names(plan):
     n, length, d, t, c, f = (plan[k] for k in ("n", "L", "D", "T", "C", "F"))
     far = plan["Y"] - 1
-    x1, z, rw = plan["X"] - 1, plan["Z"], plan["RW"]
+    z, rw = plan["Z"], plan["RW"]
     grid = (length, d)
     out = [("tok", grid, BF16), ("h1", grid, BF16), ("cot", grid, BF16), ("wout", (d, d), BF16)]
     out += [("attn", grid, BF16), ("h2", grid, BF16), ("act", (length, f), BF16), ("gpre", (length, f), BF16)]
     out += [("wqkv", (d, 3 * c), BF16), ("wup", (d, f), BF16), ("wdn", (d, f), BF16)]
-    out += [("qkv", (length, 3 * c), BF16), ("tk", (t, d), BF16), ("gb", (length, c), BF16)]
+    out += [("qkv", (length, 3 * c), BF16), ("gbr", grid, BF16)]
     out += [("ck", (CTX, c), BF16), ("cv", (CTX, c), BF16), ("gck", (CTX, c), F32), ("gcv", (CTX, c), F32)]
     out += [("lse", (c // HEAD, length, 1), F32), ("xs", (BLK, c), F32), ("gx", (BLK, c), F32)]
     out += [("keep", (CTX + 1, plan["NS"], c), F32), ("ak", (BLK, c), F32), ("av", (BLK, c), F32)]
@@ -502,8 +538,8 @@
         out += [(s + part, (far, t, d), BF16) for part in ("_mo", "_mi", "_fo", "_fi")]
         out += [(s + part, (t, d), BF16) for part in ("_no", "_ni")]
     out += [("stage", (d, f), BF16), ("ostage", (d, c), BF16)]
-    for s, w in (("up", f), ("dn", f), ("qk", 3 * c), ("ou", c)):
-        out += [(s + "_xi", (x1, z, rw, w), BF16), (s + "_zi", (z - 1, rw, w), BF16)]
+    for s, w in (("up", f), ("dn", f), ("qk", 2 * c), ("va", c), ("ou", c)):
+        out += [(s + "_slots", (plan["R"] - 1, rw, w), BF16)]
     steps = plan["R"].bit_length() - 1
     block = (plan["SM"], c)
     out += [("small", block, F32), ("smallin", (steps,) + block, F32), ("smallout", (steps,) + block, F32)]
@@ -556,7 +592,6 @@
     ]
     got_cot = links.load(i.cotangent, s.cot.at[own_rows])
     got_up, got_dn = links.load(i.w_up, s.wup), links.load(i.w_down, s.wdn)
-    got_own = links.load(i.tokens, s.tk)
     par = ssm_params(i.decay_rates, i.input_mix, i.key_mix, i.value_mix)
     got_tok.wait()
     got_out.wait()
@@ -657,11 +692,12 @@
     for gather in cot_gathers:
         gather.finish()
 
-    def rows_sum(k, stage):
-        return RowScatter(links, stage, getattr(s, k + "_xi"), getattr(s, k + "_zi"))
-
-    down_sum = rows_sum("dn", s.stage)
-    down_sum.compute(s.cot, s.act)
+    def rows_sum(k, stage, order):
+        return RowScatter(links, stage, getattr(s, k + "_slots"), order)
+
+    every = slice(None)
+    down_sum = rows_sum("dn", s.stage, "xlh")
+    weight_sums(s.cot, s.act, [(down_sum, every)])
 
     def slope_grad(owner):
         rows = chip_rows(owner)
@@ -679,6 +715,14 @@
             s.p[0:pair, cols] = dot(source[rows, :], weight[cols, :], NT)
 
         loop(d, part)
+
+    def back_near(sums, source, weight, own):
+        def part(cols):
+            sums.near_out[:, cols] = dot(source[rows_of(mate), :], weight[cols, :], NT).astype(BF16)
+            own[:, cols] = dot(source[own_rows, :], weight[cols, :], NT)
+
+        loop(d, part)
+        sums.send_near()
 
     scatter = lambda k: Scatter(links, *(getattr(s, k + x) for x in ("_mo", "_mi", "_fo", "_fi", "_no", "_ni")))
     grad2 = scatter("a")
@@ -688,21 +732,19 @@
         grad2.for_mate(j, s.p[mate_part, :])
         if j == plan["Y"] - 1:
             slope_grad(here)
+            back_near(grad2, s.gpre, s.wup, s.acc)
         grad2.for_far(j, s.p[own_part, :])
         grad2.send_far(j)
-    back(here, s.gpre, s.wup)
-    grad2.for_near(s.p[mate_part, :])
-    s.acc[...] = s.p[own_part, :]
     ffn = scatter("b")
     for j in far:
         back(links.far(j), s.act, s.wdn)
         ffn.for_mate(j, s.p[mate_part, :])
+        if j == plan["Y"] - 1:
+            back_near(ffn, s.act, s.wdn, s.ffn)
         ffn.for_far(j, s.p[own_part, :])
-    back(here, s.act, s.wdn)
-    ffn.for_near(s.p[mate_part, :])
-    s.ffn[...] = s.p[own_part, :]
-    up_sum = rows_sum("up", s.act)
-    up_sum.compute(s.h2, s.gpre)
+    down_sum.advance()
+    up_sum = rows_sum("up", s.act, "xlh")
+    weight_sums(s.h2, s.gpre, [(up_sum, every)])
 
     base = 4 * plan["NS"] + 2
     bias_rows = f // c
@@ -714,34 +756,40 @@
         for e in range(n):
             s.small[base + k * n + e : base + k * n + e + 1, :] = value[:, e * c : (e + 1) * c]
 
+    down_sum.advance()
     grad_hidden2 = grad2.total(s.acc[...])
     hat2, inv2 = normalize(s.r2own[...])
     own_cot = s.cot[own_rows, :].astype(F32)
     s.acc[...] = own_cot + norm_back(grad_hidden2, hat2, inv2, i.norm2_gain[...])
-    s.tok[own_rows, :] = s.acc[...].astype(BF16)
-    branch_gather = Gather(links, lambda o: s.tok.at[rows_of(o)])
+    s.gbr[own_rows, :] = s.acc[...].astype(BF16)
+    branch_gather = Gather(links, lambda o: s.gbr.at[rows_of(o)])
     keep_vector(0, colsum(own_cot))
     keep_vector(1, colsum(grad_hidden2 * hat2))
     keep_vector(2, colsum(grad_hidden2))
-    down_sum.over_z()
+    down_sum.advance(plan["R"])
     branch_gather.forward()
     branch_gather.finish()
     for j in far:
         ffn.send_far(j)
+    out_sum = rows_sum("ou", s.ostage, "lhx")
+    weight_sums(s.attn, s.gbr.at[:, own_cols], [(out_sum, every)])
+    up_sum.advance()
 
     def attend_back(block):
-        s.do[...] = dot(s.tok[block * BLK : (block + 1) * BLK, :], s.wout[own_cols, :], NT).astype(BF16)
+        s.do[...] = dot(s.gbr[block * BLK : (block + 1) * BLK, :], s.wout[own_cols, :], NT).astype(BF16)
         attn_backward(
             block, q_ref, k_ref, v_ref, s.ck, s.cv, i.segments, s.lse, s.do,
             q_ref, k_ref, v_ref, s.gck, s.gcv, s.ak, s.av,
         )
 
     attend_back(1)
+    up_sum.advance()
     ssm_backward(s.xs, i.segments, par, skip_k, skip_v, s.gck, s.gcv, s.keep, e0, s.gx, s.small)
     steps = plan["R"].bit_length() - 1
     doubling = Doubling(links, s.small, s.smallout, s.smallin)
     doubling.begin()
     attend_back(0)
+    out_sum.advance(2)
 
     def input_back(owner):
         rows = chip_rows(owner)
@@ -755,63 +803,72 @@
         def _():
             s.p[0:pair, own_cols] = s.p[0:pair, own_cols] + s.gx[rows, :].astype(BF16).astype(F32)
 
+    def norm1_sums(owner, total):
+        hat, _ = normalize(s.tok[chip_rows(owner), :].astype(F32))
+        partial = s.p[0:pair, :]
+        return [total[0] + colsum(partial * hat), total[1] + colsum(partial)]
+
+    def spread(slots, own, targets):
+        return [links.put(slots.at[own], slots.at[own], **target) for target in targets]
+
+    def settle(hops, slots, count):
+        for hop in hops:
+            hop.wait()
+        return sum([slots[e] for e in range(1, count)], slots[0])
+
     grad1 = scatter("a")
-    qkv_sum = rows_sum("qk", s.h2.at[:, 0 : 3 * c])
+    qk_sum = rows_sum("qk", s.h2.at[:, 0 : 2 * c], "xlh")
+    value_sum = rows_sum("va", s.h2.at[:, 2 * c : 3 * c], "lxh")
+    norm1 = [jnp.zeros((1, d), F32)] * 2
     for j in far:
         input_back(links.far(j))
         grad1.for_mate(j, s.p[mate_part, :])
         if j == 1:
-            qkv_sum.compute(s.h1, s.qkv)
+            weight_sums(s.h1, s.qkv, [(value_sum, slice(2 * c, 3 * c)), (qk_sum, slice(0, 2 * c))])
         grad1.for_far(j, s.p[own_part, :])
         grad1.send_far(j)
+        norm1 = norm1_sums(links.far(j), norm1)
+    input_back(here)
+    grad1.for_near(s.p[mate_part, :])
+    norm1 = norm1_sums(here, norm1)
+    s.fx[links.x, 0:1, :] = norm1[0]
+    s.fx[links.x, 1:2, :] = norm1[1]
+    s.fx[links.x, 2:8, :] = jnp.zeros((6, d), F32)
+    hops = spread(s.fx, links.x, [{"rows": links.row_of(links.z, links.x + e)} for e in range(1, plan["X"])])
     doubling.end()
     doubling.begin()
-    input_back(here)
-    grad1.for_near(s.p[mate_part, :])
-    s.gb[...] = s.tok[:, own_cols]
-    out_sum = rows_sum("ou", s.ostage)
-    out_sum.compute(s.attn, s.gb)
-    up_sum.over_z()
+    up_sum.advance(plan["R"])
+    out_sum.advance(plan["R"])
+    s.fz[links.z] = settle(hops, s.fx, plan["X"])
+    hops = spread(s.fz, links.z, [{"rows": links.row_of(links.z + e, links.x)} for e in range(1, plan["Z"])])
+    o_dn[...] = down_sum.total()
     for step in range(1, steps):
         doubling.end()
         if step < steps - 1:
             doubling.begin()
     o_small[here] = s.small[...]
     small_gather = Gather(links, lambda o: o_small.at[o])
-    o_dn[...] = down_sum.total()
-    qkv_sum.over_z()
-    out_sum.over_z()
+    s.fc[here] = settle(hops, s.fz, plan["Z"])
+    group = [mate] + [links.far(j) for j in far] + [links.other(links.far(j)) for j in far]
+    hops = spread(s.fc, here, [{"chan": e} for e in group])
+    qk_sum.advance()
+    value_sum.advance()
+    o_out[...] = (s.r2own[...] + ffn.total(s.ffn[...]) + i.down_bias[...]).astype(BF16)
+    small_gather.forward()
+    qk_sum.advance()
+    value_sum.advance()
     o_up[...] = up_sum.total()
-    o_out[...] = (s.r2own[...] + ffn.total(s.ffn[...]) + i.down_bias[...]).astype(BF16)
-
-    got_own.wait()
-    hat1, inv1 = normalize(s.tk[...].astype(F32))
+    o_last[...] = settle(hops, s.fc, n)
+    small_gather.finish()
+    qk_sum.advance(plan["R"])
+    value_sum.advance(plan["R"])
+
+    hat1, inv1 = normalize(s.tok[own_rows, :].astype(F32))
     grad_hidden1 = grad1.total(s.p[own_part, :])
     o_tok[...] = (s.acc[...] + norm_back(grad_hidden1, hat1, inv1, i.norm1_gain[...])).astype(BF16)
-    s.fx[links.x, 0:1, :] = colsum(grad_hidden1 * hat1)
-    s.fx[links.x, 1:2, :] = colsum(grad_hidden1)
-    s.fx[links.x, 2:8, :] = jnp.zeros((6, d), F32)
-
-    def spread(slots, own, targets):
-        return [links.put(slots.at[own], slots.at[own], **target) for target in targets]
-
-    hops = spread(s.fx, links.x, [{"rows": links.row_of(links.z, links.x + e)} for e in range(1, plan["X"])])
-    small_gather.forward()
-    for hop in hops:
-        hop.wait()
-    s.fz[links.z] = sum([s.fx[e] for e in range(1, plan["X"])], s.fx[0])
-    hops = spread(s.fz, links.z, [{"rows": links.row_of(links.z + e, links.x)} for e in range(1, plan["Z"])])
-    small_gather.finish()
-    for hop in hops:
-        hop.wait()
-    s.fc[here] = sum([s.fz[e] for e in range(1, plan["Z"])], s.fz[0])
-    group = [mate] + [links.far(j) for j in far] + [links.other(links.far(j)) for j in far]
-    hops = spread(s.fc, here, [{"chan": e} for e in group])
     o_w4[:, 3 * c : 4 * c] = out_sum.total()
-    o_w4[:, 0 : 3 * c] = qkv_sum.total()
-    for hop in hops:
-        hop.wait()
-    o_last[...] = sum([s.fc[e] for e in range(1, n)], s.fc[0])
+    o_w4[:, 0 : 2 * c] = qk_sum.total()
+    o_w4[:, 2 * c : 3 * c] = value_sum.total()
 
 
 def finish_kernel(plan, *refs):
@@ -901,7 +958,7 @@
     gathers = 5 + plan["L"] // BLK
     slabs = 1 + y * (2 + x + z)
     hops = x + z + plan["n"]
-    rows = 4 * (x * z + z - 1)
+    rows = 5 * (plan["R"] - 1)
     return 12 + gathers * (2 * y + 1) + slabs + 3 * (2 * y + 1) + rows + plan["R"].bit_length() + hops
 
 

time: 168 us -> 151 us (0.90)
  Pallas kernels: 166 us -> 150 us
    pallas_call x1, Pallas kernels: 162 us -> 146 us  [shards(): pl.pallas_call(functools.partial(layer_kernel, plan), out_shape=outs, in_...]
where the time goes in v4:
time: 151 us
  Pallas kernels  150 us (99%)
    pallas_call x1, Pallas kernels, shards(): pl.pallas_call(functools.partial(layer_kernel, plan), out_shape=outs, in_...  146 us
    pallas_call x1, Pallas kernels, shards(): pl.pallas_call(functools.partial(finish_kernel, plan), out_shape=outs, in...  4.07 us

profile of v4, /device:TPU:0, one launch (start us, length us, event | category | flops | bytes accessed | tf_op | source)
XLA Modules:
  0.0 150.6 jit_solution(7129906485703181362)
XLA Ops:
  0.7 145.6 %shard_map.356 = (bf16[256,1024]{1,0:T(8,128)(2,1)}, bf16[256,1024]{1,0:T(8,128)(2,1)}, f32[128,1024]{1,0:T(8,128)}, f32[128,1024]{1,0:T(8,128)}, f32[128,1024]{...) custom-call(bf16[256,1024]{1,0:T(8,128)(2,1)} %refs_0_.1, bf16[256,1024]{1,0:T(8,128)(2,1)} %refs_1_.1, ...), custom_call_target="tpu_custom_call" | custom-call | tf_op jit(solution)/shard_map/pallas_call | solution.py:924
  146.3 4.1 %shard_map.357 = (bf16[256,1024]{1,0:T(8,128)(2,1)}, bf16[256,1024]{1,0:T(8,128)(2,1)}, f32[128,256]{1,0:T(8,128)}, f32[128,256]{1,0:T(8,128)}, f32[128,256]{1,0...) custom-call(bf16[256,1024]{1,0:T(8,128)(2,1)} %get-tuple-element.47., ...), custom_call_target="tpu_custom_call" | custom-call | tf_op jit(solution)/shard_map/pallas_call | solution.py:940

commit v5 on v4

--- a/solution.py
+++ b/solution.py
@@ -397,10 +397,15 @@
         self.mix[j - 1].wait_recv()
         self.far_out[j - 1] = (value + self.mixed_in[j - 1].astype(F32)).astype(BF16)
 
-    def send_far(self, j):
+    def send_far(self, j, parts=1):
         links = self.links
+        size = self.near_out.shape[0] // parts
+        rows = [pl.ds(e * size, size) for e in range(parts)]
         self.direct.append(
-            links.put(self.far_out.at[j - 1], self.far_in.at[j - 1], chan=links.far(j))
+            [
+                links.put(self.far_out.at[j - 1, r], self.far_in.at[j - 1, r], chan=links.far(j))
+                for r in rows
+            ]
         )
 
     def for_near(self, value):
@@ -410,14 +415,17 @@
     def send_near(self):
         self.near = self.links.put(self.near_out, self.near_in, chan=self.links.mate)
 
-    def total(self, own):
-        self.near.wait()
-        own = own + self.near_in[...].astype(F32)
-        for j, copy in enumerate(self.direct):
-            copy.wait()
-            own = own + self.far_in[j].astype(F32)
-        for copy in self.mix:
-            copy.wait_send()
+    def total(self, own, part=0, parts=1):
+        size = self.near_out.shape[0] // parts
+        rows = pl.ds(part * size, size)
+        if part == 0:
+            self.near.wait()
+            for copy in self.mix:
+                copy.wait_send()
+        own = own + self.near_in[rows, :].astype(F32)
+        for j, copies in enumerate(self.direct):
+            copies[part].wait()
+            own = own + self.far_in[j, rows, :].astype(F32)
         return own
 
 
@@ -490,8 +498,8 @@
         return value
 
 
-def weight_sums(left, right, sums):
-    first = sums[0][0]
+def weight_sums(left, right, sums, hold):
+    first, later = sums[0][0], []
     rows = first.links.plan["X"] * first.slots.shape[1]
     for low in (1, 0):
         for high in range(first.size["h"] - 1, -1, -1):
@@ -500,7 +508,11 @@
             for one, cols in sums:
                 one.stage[group, :] = product[:, cols]
             for one, _ in sums:
-                one.ready(low, high)
+                if low < hold.get(one, 0):
+                    later.append(functools.partial(one.ready, low, high))
+                else:
+                    one.ready(low, high)
+    return later
 
 
 class Doubling:
@@ -675,10 +687,10 @@
         def hidden(cols):
             v = dot(s.h2[rows, :], s.wup[:, cols]) + i.up_bias[:, cols]
             square = v * v
-            th = jnp.tanh(ROOT * (v + 0.044715 * (square * v)))
-            part = 0.5 * (1.0 + th)
-            s.act[rows, cols] = (v * part).astype(BF16)
-            slope = part + 0.5 * v * (1.0 - th * th) * (ROOT * (1.0 + 0.134145 * square))
+            part = 0.5 + 0.5 * jnp.tanh(v * (ROOT + (0.044715 * ROOT) * square))
+            act = v * part
+            s.act[rows, cols] = act.astype(BF16)
+            slope = part + act * (1.0 - part) * (2.0 * ROOT + (0.26829 * ROOT) * square)
             s.gpre[rows, cols] = slope.astype(BF16)
 
         loop(f, hidden)
@@ -697,7 +709,7 @@
 
     every = slice(None)
     down_sum = rows_sum("dn", s.stage, "xlh")
-    weight_sums(s.cot, s.act, [(down_sum, every)])
+    weight_sums(s.cot, s.act, [(down_sum, every)], {})
 
     def slope_grad(owner):
         rows = chip_rows(owner)
@@ -734,7 +746,7 @@
             slope_grad(here)
             back_near(grad2, s.gpre, s.wup, s.acc)
         grad2.for_far(j, s.p[own_part, :])
-        grad2.send_far(j)
+        grad2.send_far(j, 2)
     ffn = scatter("b")
     for j in far:
         back(links.far(j), s.act, s.wdn)
@@ -744,7 +756,7 @@
         ffn.for_far(j, s.p[own_part, :])
     down_sum.advance()
     up_sum = rows_sum("up", s.act, "xlh")
-    weight_sums(s.h2, s.gpre, [(up_sum, every)])
+    weight_sums(s.h2, s.gpre, [(up_sum, every)], {})
 
     base = 4 * plan["NS"] + 2
     bias_rows = f // c
@@ -757,23 +769,32 @@
             s.small[base + k * n + e : base + k * n + e + 1, :] = value[:, e * c : (e + 1) * c]
 
     down_sum.advance()
-    grad_hidden2 = grad2.total(s.acc[...])
-    hat2, inv2 = normalize(s.r2own[...])
-    own_cot = s.cot[own_rows, :].astype(F32)
-    s.acc[...] = own_cot + norm_back(grad_hidden2, hat2, inv2, i.norm2_gain[...])
-    s.gbr[own_rows, :] = s.acc[...].astype(BF16)
-    branch_gather = Gather(links, lambda o: s.gbr.at[rows_of(o)])
-    keep_vector(0, colsum(own_cot))
-    keep_vector(1, colsum(grad_hidden2 * hat2))
-    keep_vector(2, colsum(grad_hidden2))
+    branch_gathers, norm2 = [], [jnp.zeros((1, d), F32)] * 3
+    for e in range(2):
+        rows = pl.ds(e * half, half)
+        tile_rows = at(here * t + e * half, half)
+        grad_hidden2 = grad2.total(s.acc[rows, :], e, 2)
+        hat2, inv2 = normalize(s.r2own[rows, :])
+        own_cot = s.cot[tile_rows, :].astype(F32)
+        grad_resid2 = own_cot + norm_back(grad_hidden2, hat2, inv2, i.norm2_gain[...])
+        s.acc[rows, :] = grad_resid2
+        s.gbr[tile_rows, :] = grad_resid2.astype(BF16)
+        branch_gathers.append(Gather(links, lambda o, e=e: s.gbr.at[at(o * t + e * half, half)]))
+        sums = colsum(own_cot), colsum(grad_hidden2 * hat2), colsum(grad_hidden2)
+        norm2 = [a + b for a, b in zip(norm2, sums)]
+    for k in range(3):
+        keep_vector(k, norm2[k])
     down_sum.advance(plan["R"])
-    branch_gather.forward()
-    branch_gather.finish()
+    up_sum.advance()
+    for gather in branch_gathers:
+        gather.forward()
+    for gather in branch_gathers:
+        gather.finish()
     for j in far:
         ffn.send_far(j)
-    out_sum = rows_sum("ou", s.ostage, "lhx")
-    weight_sums(s.attn, s.gbr.at[:, own_cols], [(out_sum, every)])
     up_sum.advance()
+    out_sum = rows_sum("ou", s.ostage, "xlh")
+    held = weight_sums(s.attn, s.gbr.at[:, own_cols], [(out_sum, every)], {out_sum: 2})
 
     def attend_back(block):
         s.do[...] = dot(s.gbr[block * BLK : (block + 1) * BLK, :], s.wout[own_cols, :], NT).astype(BF16)
@@ -783,13 +804,14 @@
         )
 
     attend_back(1)
-    up_sum.advance()
     ssm_backward(s.xs, i.segments, par, skip_k, skip_v, s.gck, s.gcv, s.keep, e0, s.gx, s.small)
+    doubling = Doubling(links, s.small, s.smallout, s.smallin)
     steps = plan["R"].bit_length() - 1
-    doubling = Doubling(links, s.small, s.smallout, s.smallin)
     doubling.begin()
+    for send in held:
+        send()
+    up_sum.advance(plan["R"])
     attend_back(0)
-    out_sum.advance(2)
 
     def input_back(owner):
         rows = chip_rows(owner)
@@ -824,7 +846,10 @@
         input_back(links.far(j))
         grad1.for_mate(j, s.p[mate_part, :])
         if j == 1:
-            weight_sums(s.h1, s.qkv, [(value_sum, slice(2 * c, 3 * c)), (qk_sum, slice(0, 2 * c))])
+            doubling.end()
+            doubling.begin()
+            both = [(value_sum, slice(2 * c, 3 * c)), (qk_sum, slice(0, 2 * c))]
+            held = weight_sums(s.h1, s.qkv, both, {qk_sum: 1})
         grad1.for_far(j, s.p[own_part, :])
         grad1.send_far(j)
         norm1 = norm1_sums(links.far(j), norm1)
@@ -834,39 +859,41 @@
     s.fx[links.x, 0:1, :] = norm1[0]
     s.fx[links.x, 1:2, :] = norm1[1]
     s.fx[links.x, 2:8, :] = jnp.zeros((6, d), F32)
+
+    group = [mate] + [links.far(j) for j in far] + [links.other(links.far(j)) for j in far]
+    group = [{"chan": e} for e in group]
     hops = spread(s.fx, links.x, [{"rows": links.row_of(links.z, links.x + e)} for e in range(1, plan["X"])])
+    for step in range(2, steps):
+        doubling.end()
+        doubling.begin()
+    for send in held:
+        send()
+    out_sum.advance(2)
+    o_dn[...] = down_sum.total()
+    qk_sum.advance()
+    value_sum.advance()
     doubling.end()
-    doubling.begin()
-    up_sum.advance(plan["R"])
-    out_sum.advance(plan["R"])
+    o_small[here] = s.small[...]
+    blocks = spread(o_small, here, group)
     s.fz[links.z] = settle(hops, s.fx, plan["X"])
     hops = spread(s.fz, links.z, [{"rows": links.row_of(links.z + e, links.x)} for e in range(1, plan["Z"])])
-    o_dn[...] = down_sum.total()
-    for step in range(1, steps):
-        doubling.end()
-        if step < steps - 1:
-            doubling.begin()
-    o_small[here] = s.small[...]
-    small_gather = Gather(links, lambda o: o_small.at[o])
-    s.fc[here] = settle(hops, s.fz, plan["Z"])
-    group = [mate] + [links.far(j) for j in far] + [links.other(links.far(j)) for j in far]
-    hops = spread(s.fc, here, [{"chan": e} for e in group])
     qk_sum.advance()
     value_sum.advance()
+    out_sum.advance(plan["R"])
+    o_up[...] = up_sum.total()
+    s.fc[here] = settle(hops, s.fz, plan["Z"])
+    hops = spread(s.fc, here, group)
+    qk_sum.advance(plan["R"])
+    o_w4[:, 3 * c : 4 * c] = out_sum.total()
     o_out[...] = (s.r2own[...] + ffn.total(s.ffn[...]) + i.down_bias[...]).astype(BF16)
-    small_gather.forward()
-    qk_sum.advance()
-    value_sum.advance()
-    o_up[...] = up_sum.total()
-    o_last[...] = settle(hops, s.fc, n)
-    small_gather.finish()
-    qk_sum.advance(plan["R"])
     value_sum.advance(plan["R"])
 
     hat1, inv1 = normalize(s.tok[own_rows, :].astype(F32))
     grad_hidden1 = grad1.total(s.p[own_part, :])
     o_tok[...] = (s.acc[...] + norm_back(grad_hidden1, hat1, inv1, i.norm1_gain[...])).astype(BF16)
-    o_w4[:, 3 * c : 4 * c] = out_sum.total()
+    o_last[...] = settle(hops, s.fc, n)
+    for copy in blocks:
+        copy.wait()
     o_w4[:, 0 : 2 * c] = qk_sum.total()
     o_w4[:, 2 * c : 3 * c] = value_sum.total()
 
@@ -955,11 +982,11 @@
 
 def plan_semaphores(plan):
     y, x, z = plan["Y"] - 1, plan["X"] - 1, plan["Z"]
-    gathers = 5 + plan["L"] // BLK
+    gathers = 6 + plan["L"] // BLK
     slabs = 1 + y * (2 + x + z)
     hops = x + z + plan["n"]
     rows = 5 * (plan["R"] - 1)
-    return 12 + gathers * (2 * y + 1) + slabs + 3 * (2 * y + 1) + rows + plan["R"].bit_length() + hops
+    return 12 + gathers * (2 * y + 1) + slabs + 3 * (2 * y + 1) + y + rows + plan["R"].bit_length() + hops
 
 
 def solution(mesh):

time: 151 us -> 139 us (0.921)
  Pallas kernels: 150 us -> 138 us
    pallas_call x1, Pallas kernels: 146 us -> 134 us  [shards(): pl.pallas_call(functools.partial(layer_kernel, plan), out_shape=outs, in_...]
where the time goes in v5:
time: 139 us
  Pallas kernels  138 us (99%)
    pallas_call x1, Pallas kernels, shards(): pl.pallas_call(functools.partial(layer_kernel, plan), out_shape=outs, in_...  134 us
    pallas_call x1, Pallas kernels, shards(): pl.pallas_call(functools.partial(finish_kernel, plan), out_shape=outs, in...  4.07 us

profile of v5, /device:TPU:0, one launch (start us, length us, event | category | flops | bytes accessed | tf_op | source)
XLA Modules:
  0.0 139.1 jit_solution(1294349246714868211)
XLA Ops:
  0.7 134.2 %shard_map.356 = (bf16[256,1024]{1,0:T(8,128)(2,1)}, bf16[256,1024]{1,0:T(8,128)(2,1)}, f32[128,1024]{1,0:T(8,128)}, f32[128,1024]{1,0:T(8,128)}, f32[128,1024]{...) custom-call(bf16[256,1024]{1,0:T(8,128)(2,1)} %refs_0_.1, bf16[256,1024]{1,0:T(8,128)(2,1)} %refs_1_.1, ...), custom_call_target="tpu_custom_call" | custom-call | tf_op jit(solution)/shard_map/pallas_call | solution.py:951
  134.8 4.1 %shard_map.357 = (bf16[256,1024]{1,0:T(8,128)(2,1)}, bf16[256,1024]{1,0:T(8,128)(2,1)}, f32[128,256]{1,0:T(8,128)}, f32[128,256]{1,0:T(8,128)}, f32[128,256]{1,0...) custom-call(bf16[256,1024]{1,0:T(8,128)(2,1)} %get-tuple-element.47., ...), custom_call_target="tpu_custom_call" | custom-call | tf_op jit(solution)/shard_map/pallas_call | solution.py:967

commit v6 on v5

--- a/solution.py
+++ b/solution.py
@@ -522,7 +522,7 @@
     def begin(self):
         step, rows = self.step, self.links.rows
         self.out[step] = self.block[...]
-        bit = 1 << step
+        bit = 1 << (self.out.shape[0] - 1 - step)
         partner = rows + bit - 2 * bit * lax.rem(rows // bit, 2)
         self.copy = self.links.put(self.out.at[step], self.got.at[step], rows=partner)
 
@@ -840,7 +840,7 @@
 
     grad1 = scatter("a")
     qk_sum = rows_sum("qk", s.h2.at[:, 0 : 2 * c], "xlh")
-    value_sum = rows_sum("va", s.h2.at[:, 2 * c : 3 * c], "lxh")
+    value_sum = rows_sum("va", s.h2.at[:, 2 * c : 3 * c], "lhx")
     norm1 = [jnp.zeros((1, d), F32)] * 2
     for j in far:
         input_back(links.far(j))
@@ -868,25 +868,25 @@
         doubling.begin()
     for send in held:
         send()
+    value_sum.advance()
     out_sum.advance(2)
-    o_dn[...] = down_sum.total()
-    qk_sum.advance()
-    value_sum.advance()
+    s.fz[links.z] = settle(hops, s.fx, plan["X"])
+    hops = spread(s.fz, links.z, [{"rows": links.row_of(links.z + e, links.x)} for e in range(1, plan["Z"])])
     doubling.end()
     o_small[here] = s.small[...]
     blocks = spread(o_small, here, group)
-    s.fz[links.z] = settle(hops, s.fx, plan["X"])
-    hops = spread(s.fz, links.z, [{"rows": links.row_of(links.z + e, links.x)} for e in range(1, plan["Z"])])
     qk_sum.advance()
     value_sum.advance()
-    out_sum.advance(plan["R"])
-    o_up[...] = up_sum.total()
     s.fc[here] = settle(hops, s.fz, plan["Z"])
     hops = spread(s.fc, here, group)
+    qk_sum.advance()
+    out_sum.advance(plan["R"])
+    o_dn[...] = down_sum.total()
+    o_out[...] = (s.r2own[...] + ffn.total(s.ffn[...]) + i.down_bias[...]).astype(BF16)
+    o_up[...] = up_sum.total()
     qk_sum.advance(plan["R"])
+    value_sum.advance(plan["R"])
     o_w4[:, 3 * c : 4 * c] = out_sum.total()
-    o_out[...] = (s.r2own[...] + ffn.total(s.ffn[...]) + i.down_bias[...]).astype(BF16)
-    value_sum.advance(plan["R"])
 
     hat1, inv1 = normalize(s.tok[own_rows, :].astype(F32))
     grad_hidden1 = grad1.total(s.p[own_part, :])

time: 139 us -> 138 us (level)
    pallas_call x1, Pallas kernels: 134 us -> 132 us  [shards(): pl.pallas_call(functools.partial(layer_kernel, plan), out_shape=outs, in_...]
where the time goes in v6:
time: 138 us; the launch traced here: 137 us
  Pallas kernels  137 us (99%)
    pallas_call x1, Pallas kernels, shards(): pl.pallas_call(functools.partial(layer_kernel, plan), out_shape=outs, in_...  132 us
    pallas_call x1, Pallas kernels, shards(): pl.pallas_call(functools.partial(finish_kernel, plan), out_shape=outs, in...  4.07 us

profile of v6, /device:TPU:0, one launch (start us, length us, event | category | flops | bytes accessed | tf_op | source)
XLA Modules:
  0.0 137.4 jit_solution(7028879863138536847)
XLA Ops:
  0.7 132.5 %shard_map.356 = (bf16[256,1024]{1,0:T(8,128)(2,1)}, bf16[256,1024]{1,0:T(8,128)(2,1)}, f32[128,1024]{1,0:T(8,128)}, f32[128,1024]{1,0:T(8,128)}, f32[128,1024]{...) custom-call(bf16[256,1024]{1,0:T(8,128)(2,1)} %refs_0_.1, bf16[256,1024]{1,0:T(8,128)(2,1)} %refs_1_.1, ...), custom_call_target="tpu_custom_call" | custom-call | tf_op jit(solution)/shard_map/pallas_call | solution.py:951
  133.1 4.1 %shard_map.357 = (bf16[256,1024]{1,0:T(8,128)(2,1)}, bf16[256,1024]{1,0:T(8,128)(2,1)}, f32[128,256]{1,0:T(8,128)}, f32[128,256]{1,0:T(8,128)}, f32[128,256]{1,0...) custom-call(bf16[256,1024]{1,0:T(8,128)(2,1)} %get-tuple-element.47., ...), custom_call_target="tpu_custom_call" | custom-call | tf_op jit(solution)/shard_map/pallas_call | solution.py:967
